TPU v7x, 256 devices: a whole 4x4x8 slice. The times are simulated.
256 devices in a mesh: grp: 4 (over x), tp: 32 (over y_lo, z, core), cores: 2 (over y_hi).
Axes of the slice: x: 4, y: 4 (y_hi: 2, y_lo: 2; y = y_hi * 2 + y_lo), z: 8, core: 2. Of those that a mesh axis runs over, the one named last changes fastest.
Arguments:
- tokens: bfloat16 [4096, 8192], P('grp', ('tp', 'cores')), may hold values from -6 to 6
- gate_up_weight: bfloat16 [8192, 2, 16384], P(None, None, ('tp', 'cores')), may hold values from -0.0625 to 0.0625
- down_factor_pool: bfloat16 [64, 8192, 256], P(('tp', 'cores'), 'grp'), may hold values from -0.0625 to 0.0625
- up_factor_pool: bfloat16 [64, 4, 64, 128, 128], P(('tp', 'cores'), 'grp'), may hold values from -0.5 to 0.5
- segment_adapters: int32 [4, 3], replicated, may hold values from 0 to 63
- segment_tile_counts: int32 [4, 3], P('grp'), may hold values from 1 to 4, 8 in all within a row
- adapter_pool_rows: int32 [64], replicated, may hold values from 0 to 63, each once
Outputs:
- hidden: bfloat16 [4096, 16384], P('grp', ('tp', 'cores'))
Inputs may be any that keep to these rules, and one draw needn't show every extreme that they name: `segment_tile_counts`: each row sums to 8. `adapter_pool_rows`: each pool row appears once.
All inputs are finite; a program needn't handle non-finite values.
Results may differ from a plain program's by a relative error of at most 0.0036.
Values may be sent and summed in bfloat16 or wider, within the bound.
No kernel may reach another device: no remote copies, remote signals or barrier semaphores. Data moves between devices by JAX's collectives and lax.ppermute only.
A program may use at most 192 MiB of HBM per device.

v0:
```python
import jax
import jax.numpy as jnp
from jax import lax
from jax.sharding import PartitionSpec as P

TILE = 128


adapter_scale = 0.5


def tile_segments(tile_lengths, tile_count):
    bounds = jnp.cumsum(tile_lengths)
    positions = jnp.arange(tile_count, dtype=jnp.int32)
    return jnp.sum((bounds[None, :] <= positions[:, None]).astype(jnp.int32), axis=1)


def per_device(
    tokens,
    gate_up_weight,
    down_factor_pool,
    up_factor_pool,
    segment_adapters,
    segment_tile_counts,
    adapter_pool_rows,
):
    groups = lax.axis_size("grp")
    device_shares = lax.axis_size(("tp", "cores"))
    group_index = lax.axis_index("grp")
    piece_index = lax.axis_index(("tp", "cores"))
    token_count = tokens.shape[0]
    full_width = tokens.shape[1] * device_shares
    local_hidden_width = gate_up_weight.shape[2]
    twice_rank = down_factor_pool.shape[2]
    rank_size = twice_rank // 2
    share_rows = down_factor_pool.shape[1] // device_shares
    local_count = down_factor_pool.shape[0]
    narrow = local_hidden_width // groups
    local_down_factor = down_factor_pool.reshape(
        local_count, device_shares, share_rows * twice_rank
    )
    local_up_factor = up_factor_pool.reshape(local_count, device_shares, -1)
    a_spread, b_spread = (
        lax.all_to_all(local_down_factor, ("tp", "cores"), split_axis=1, concat_axis=0, tiled=True),
        lax.all_to_all(local_up_factor, ("tp", "cores"), split_axis=1, concat_axis=0, tiled=True),
    )
    a_blocks, b_blocks = (
        lax.all_gather(a_spread, "grp", axis=1, tiled=True),
        lax.all_gather(b_spread, "grp", axis=1, tiled=True),
    )
    own_ids = lax.dynamic_index_in_dim(segment_adapters, group_index, 0, keepdims=False)
    own_slots = jnp.take(adapter_pool_rows, own_ids)
    a_chosen = jnp.take(a_blocks, own_slots, axis=0)
    b_chosen = jnp.take(b_blocks, own_slots, axis=0)
    gathered = lax.all_gather(tokens, ("tp", "cores"), axis=1, tiled=True)
    frozen_output = jnp.dot(
        gathered,
        gate_up_weight.reshape(full_width, 2 * local_hidden_width),
        preferred_element_type=jnp.float32,
    )
    frozen_output = frozen_output.reshape(token_count, 2, local_hidden_width)
    tile_count = token_count // TILE
    tile_seg = tile_segments(segment_tile_counts[0], tile_count)
    a_tiles = jnp.take(a_chosen, tile_seg, axis=0).reshape(
        tile_count, groups * share_rows, twice_rank
    )
    own_features = lax.dynamic_slice_in_dim(
        gathered.reshape(token_count, groups, device_shares, share_rows), piece_index, 1, axis=2
    )
    own_features = own_features.reshape(tile_count, TILE, groups * share_rows)
    partial_shrink = jnp.einsum(
        "tkd,tdr->tkr", own_features, a_tiles, preferred_element_type=jnp.float32
    )
    reduced_input = lax.psum(partial_shrink, ("tp", "cores")).astype(jnp.bfloat16)
    b_tiles = jnp.take(b_chosen, tile_seg, axis=0).reshape(tile_count, groups, rank_size, 2, narrow)
    gate_adapter_delta = jnp.einsum(
        "tkr,tmrw->tkmw",
        reduced_input[:, :, :rank_size],
        b_tiles[:, :, :, 0, :],
        preferred_element_type=jnp.float32,
    )
    up_adapter_delta = jnp.einsum(
        "tkr,tmrw->tkmw",
        reduced_input[:, :, rank_size:],
        b_tiles[:, :, :, 1, :],
        preferred_element_type=jnp.float32,
    )
    gate_combined = frozen_output[:, 0, :] + adapter_scale * gate_adapter_delta.reshape(
        token_count, local_hidden_width
    )
    up_combined = frozen_output[:, 1, :] + adapter_scale * up_adapter_delta.reshape(
        token_count, local_hidden_width
    )
    return (jax.nn.silu(gate_combined) * up_combined).astype(jnp.bfloat16)


def solution(mesh):
    return jax.shard_map(
        per_device,
        mesh=mesh,
        in_specs=(
            P("grp", ("tp", "cores")),
            P(None, None, ("tp", "cores")),
            P(("tp", "cores"), "grp", None),
            P(("tp", "cores"), "grp", None, None, None),
            P(),
            P("grp", None),
            P(),
        ),
        out_specs=P("grp", ("tp", "cores")),
        check_vma=False,
    )
```

profile of v0, /device:TPU:1, one launch (start us, length us, event | category | flops | bytes accessed | tf_op | source)
XLA Modules:
  0.0 825.1 jit_solution(2423148219487207486)
XLA Ops:
  6.5 4.0 reshape.205
  11.0 7.4 reduce.3
  19.2 40.9 %all_to_all.24 = bf16[64,2,4096]{2,1,0:T(2,128)(2,1)S(1)} all-to-all(bf16[64,2,4096]{2,1,0:T(2,128)(2,1)S(1)} %reshape.214), channel_id=1, replica_groups=mesh['grp'=4,'tp'=32,'cores'=2] {'tp','cores'}, dimensions={0} | all-to-all | bytes 2097152 | tf_op jit(solution)/shard_map/all_to_all | solution.py:44
  60.1 3.5 reshape.215
  63.6 10.1 %reshape.206 = bf16[1,64,16384]{2,0,1:T(2,128)(2,1)} reshape(bf16[1,1,64,128,128]{4,3,2,1,0:T(8,128)(2,1)} %param.10) | data formatting | bytes 4194304 | tf_op jit(solution)/shard_map/reshape | solution.py:42
  73.7 13.7 %reduce.2 = bf16[64,16384]{1,0:T(8,128)(2,1)S(1)} reduce(bf16[64,1,16384]{2,1,0:T(2,128)(2,1)} %bitcast.76, bf16[]{:T(256)} %broadcast.186), dimensions={1}, to_apply=%bitcast.67.reduce_sub_computation | reduce | bytes 4194306
  87.4 2.8 reshape.212
  90.2 56.8 %all_to_all.25 = bf16[64,2,8192]{2,1,0:T(2,128)(2,1)S(1)} all-to-all(bf16[64,2,8192]{2,1,0:T(2,128)(2,1)} %reshape.212), channel_id=1, replica_groups=mesh['grp'=4,'tp'=32,'cores'=2] {'tp','cores'}, dimensions={0} | all-to-all | bytes 4194304 | tf_op jit(solution)/shard_map/all_to_all | solution.py:45
  147.0 6.7 reshape.213
  154.7 8.0 copy.65
  162.7 12.3 %copy.48 = bf16[512,8192]{1,0:T(8,128)(2,1)} copy(bf16[512,8192]{0,1:T(8,128)(2,1)} %bitcast.74) | data formatting | bytes 16777216 | tf_op jit(solution)/shard_map/dot_general | solution.py:56
  175.8 27.4 %reduce = bf16[64,32768]{1,0:T(8,128)(2,1)} reduce(bf16[1,64,32768]{2,0,1:T(2,128)(2,1)} %all-gather.8.cloned.1.call-done, bf16[]{:T(256)} %constant.100), dimensions={0}, to_apply=%all-gather.reduce_sub_computation | reduce | bytes 8388610 | tf_op jit(solution)/shard_map/all_gather | solution.py:48
  203.2 7.9 reshape.198
  211.0 3.0 gather_fusion.1
  214.2 1.0 gather_fusion.2
  215.2 1.2 gather.30
  216.4 92.4 %all-gather.10.cloned.1.call-done = bf16[1,64,65536]{2,0,1:T(2,128)(2,1)} async-done(((bf16[1,64,16384]{2,0,1:T(2,128)(2,1)}), bf16[1,64,65536]{2,0,1:T(2,128)(2,1)}) %all-gather.10.cloned.1.call-update) | async-done | bytes 8388624 | tf_op jit(solution)/shard_map/all_gather | solution.py:49
  308.8 52.7 %reduce.1 = bf16[64,65536]{1,0:T(8,128)(2,1)} reduce(bf16[1,64,65536]{2,0,1:T(2,128)(2,1)} %all-gather.10.cloned.1.call-done, bf16[]{:T(256)} %constant.100), dimensions={0}, to_apply=%all-gather.1.reduce_sub_computation | reduce | bytes 16777218 | tf_op jit(solution)/shard_map/all_gather | solution.py:49
  361.4 11.7 %reshape.199 = bf16[64,4,16384]{2,1,0:T(4,128)(2,1)} reshape(bf16[64,65536]{1,0:T(8,128)(2,1)} %reduce.1) | data formatting | bytes 16777216 | tf_op jit(solution)/shard_map/all_gather | solution.py:49
  373.1 4.4 gather_fusion.3
  377.8 1.4 gather_fusion.4
  379.3 1.7 reshape.207
  380.9 1.5 copy.54
  383.5 129.4 %all-gather.6.cloned.1.call-done = bf16[1024,8192]{1,0:T(8,128)(2,1)} async-done(((bf16[1024,128]{1,0:T(8,128)(2,1)}), bf16[1024,8192]{1,0:T(8,128)(2,1)}) %all-gather.6.cloned.1.call-update) | async-done | bytes 16777232 | tf_op jit(solution)/shard_map/all_gather | solution.py:55
  512.9 22.4 %copy.49 = bf16[1024,8192]{0,1:T(8,128)(2,1)} copy(bf16[1024,8192]{1,0:T(8,128)(2,1)} %all-gather.6.cloned.1.call-done) | data formatting | bytes 33554432 | tf_op jit(solution)/shard_map/all_gather | solution.py:55
  535.3 1.0 constant_dynamic-slice_fusion.1
  536.7 258.6 %all-reduce.1 = bf16[8,128,256]{2,1,0:T(8,128)(2,1)S(1)} all-reduce(f32[8,128,256]{2,1,0:T(8,128)S(1)} %fusion.6), channel_id=1, replica_groups=mesh['grp'=4,'tp'=32,'cores'=2] {'tp','cores'}, use_global_device_ids=true, to_apply=%region_2.3 | all-reduce | flops 262144 | bytes 1572864 | tf_op jit(solution)/shard_map/psum | solution.py:74
  797.1 2.2 reshape.209
  799.3 1.4 fusion.11
  801.7 1.2 reshape.208
  802.9 14.5 %fusion = f32[1024,2,256]{2,0,1:T(8,128)S(1)} fusion(bf16[2,256,8192]{2,1,0:T(8,128)(2,1)} %bitcast.79, bf16[1024,8192]{1,0:T(8,128)(2,1)} %all-gather.6.cloned.1.call-done), kind=kOutput, calls=%fused_computation.5 | convolution fusion | flops 8589934592 | bytes 27262976 | tf_op jit(solution)/shard_map/dot_general | solution.py:56
  817.4 1.1 fusion.4
  (45 shorter events, 7.8 us)
Async XLA Ops:
  6.5 168.4 %copy-start = (s32[64]{0:T(128)S(1)}, s32[64]{0:T(128)}, u32[]{:S(2)}) copy-start(s32[64]{0:T(128)} %param.13) | copy-start | bytes 772
  6.5 169.3 %all-gather.8.cloned.1.call-start = ((), (), s32[]{:S(2)}) async-start(), calls=%async_computation.3 | async-start | bytes 10485760 | tf_op jit(solution)/shard_map/all_gather | solution.py:48
  63.6 245.2 %all-gather.10.cloned.1.call-start = ((), (), s32[]{:S(2)}) async-start(), calls=%async_computation.4 | async-start | bytes 20971520 | tf_op jit(solution)/shard_map/all_gather | solution.py:49
  90.2 64.3 %copy-start.6 = (s32[1,3]{1,0:T(1,128)S(1)}, s32[1,3]{1,0:T(1,128)}, u32[]{:S(2)}) copy-start(s32[1,3]{1,0:T(1,128)} %param.12) | copy-start | bytes 40
  153.7 359.1 %all-gather.6.cloned.1.call-start = ((), (), s32[]{:S(2)}) async-start(), calls=%async_computation.2 | async-start | bytes 17039360 | tf_op jit(solution)/shard_map/all_gather | solution.py:55
  162.7 12.3 %copy-start.5 = (s32[4,3]{1,0:T(4,128)S(1)}, s32[4,3]{1,0:T(4,128)}, u32[]{:S(2)}) copy-start(s32[4,3]{1,0:T(4,128)} %param.11) | copy-start | bytes 148
  383.5 152.8 %copy-start.4 = (bf16[8,128,256]{2,1,0:T(8,128)(2,1)S(1)}, bf16[8,128,256]{2,1,0:T(8,128)(2,1)}, u32[]{:S(2)}) copy-start(bf16[8,128,256]{2,1,0:T(8,128)(2,1)} %gather.30) | copy-start | bytes 1572868
  795.3 0.8 copy-start.3
  802.9 14.6 %copy-start.2 = (f32[1024,256]{1,0:T(8,128)S(1)}, f32[1024,256]{1,0:T(8,128)}, u32[]{:S(2)}) copy-start(f32[1024,256]{1,0:T(8,128)} %reshape.209) | copy-start | bytes 3145732
  802.9 15.7 %copy-start.1 = (s32[64]{0:T(128)S(1)}, s32[64]{0:T(128)}, u32[]{:S(2)}) copy-start(s32[64]{0:T(128)} %param.13) | copy-start | bytes 772
Sparse Core Ops, SparseCore 0:
  63.7 83.2 all-gather.7
  153.9 154.8 all-gather.9
  310.5 202.2 all-gather.5
where the time goes:
time: 834 us; the launch traced here: 825 us
  blocking collectives  356 us (43%)
  waiting for transfers between devices  223 us (27%)
  local copies, waits for them, and re-layouts  113 us (14%)
  other arithmetic  103 us (12%)
  matrix products  16.6 us (2%)
  between operations  13.4 us (2%)
    psum x1, blocking collectives, per_device(): lax.psum(partial_shrink, ('tp', 'cores')).astype(jnp.bfloat16)  259 us
    all_gather x1, waiting for transfers between devices, per_device(): gathered = lax.all_gather(tokens, ('tp', 'cores'), axis=1, tiled=True)  129 us
    all_gather x1, waiting for transfers between devices, per_device(): lax.all_gather(b_spread, 'grp', axis=1, tiled=True)  92.4 us
    all_to_all x1, blocking collectives, per_device(): lax.all_to_all(local_up_factor, ('tp', 'cores'), split_axis=1, concat_axi...  56.8 us
    all_gather x1, other arithmetic, per_device(): lax.all_gather(b_spread, 'grp', axis=1, tiled=True)  52.7 us
    all_to_all x1, blocking collectives, per_device(): lax.all_to_all(local_down_factor, ('tp', 'cores'), split_axis=1, concat_a...  40.9 us
    all_gather x1, other arithmetic, per_device(): lax.all_gather(a_spread, 'grp', axis=1, tiled=True)  27.4 us
    unnamed x21, local copies, waits for them, and re-layouts  22.9 us
  transfers between devices with their start and end apart: 3, of which 2 were waited for; matrix products, arithmetic and copies ran while one was open for 21% of the time, Pallas kernels for 0%

commit v1 on v0

v1 whole, which is shorter than its diff:
```python
import jax
import jax.numpy as jnp
from jax import lax
from jax.sharding import Mesh, PartitionSpec as P

TILE = 128
GRP = 4
YL, ZN, CORES, YH = 2, 8, 2, 2
AXES = ("grp", "ylo", "z", "core", "yhi")
PLANE = ("ylo", "z", "core", "yhi")
SHARES = YL * ZN * CORES * YH
f32 = jnp.float32
bf16 = jnp.bfloat16

adapter_scale = 0.5


def exchange(x, axes):
    return lax.all_to_all(x, axes, split_axis=0, concat_axis=0, tiled=True)


def per_device(
    tokens,
    gate_up_weight,
    down_factor_pool,
    up_factor_pool,
    segment_adapters,
    segment_tile_counts,
    adapter_pool_rows,
):
    group = lax.axis_index("grp")
    place = lax.axis_index(PLANE)
    token_count, share = tokens.shape
    tile_count = token_count // TILE
    width = gate_up_weight.shape[0]
    local_hidden = gate_up_weight.shape[2]
    twice_rank = down_factor_pool.shape[2]
    rank = twice_rank // 2
    segs = segment_adapters.shape[1]
    sub = share // GRP

    gathered = lax.all_gather(tokens, ("yhi", "ylo", "z", "core"), axis=1, tiled=True)
    w = gate_up_weight.reshape(YL * ZN * CORES, YH, share, 2 * local_hidden)
    w = jnp.transpose(w, (1, 0, 2, 3)).reshape(width, 2 * local_hidden)

    turned = tokens.T.reshape(GRP, sub, token_count)
    quarter, block = place // (SHARES // GRP), place % GRP
    own_features = []
    for k in range(GRP):
        pairs = []
        for p in range(SHARES):
            big, r = p // (SHARES // GRP), p % (SHARES // GRP)
            pairs.append((p, GRP * r + (big + k) % GRP))
        piece = lax.dynamic_index_in_dim(turned, (quarter + k) % GRP, 0, keepdims=False)
        own_features.append(lax.ppermute(piece, PLANE, pairs))
    own_features = jnp.stack(own_features).reshape(share, tile_count, TILE)

    halves = twice_rank // rank
    down_pieces = down_factor_pool.reshape(SHARES, sub, halves, rank)
    down_pieces = jnp.transpose(down_pieces, (0, 2, 1, 3)).reshape(SHARES, halves * sub, rank)
    up_pieces = up_factor_pool.reshape(SHARES, rank, rank)
    pieces = exchange(jnp.concatenate([up_pieces, down_pieces], axis=1), PLANE)
    chosen_rows = jnp.take(adapter_pool_rows, segment_adapters.reshape(-1))
    chosen = exchange(jnp.take(pieces, chosen_rows, axis=0), "grp")
    chosen = chosen.reshape(GRP, segs, rank + halves * sub, rank)
    up_chosen = chosen[:, :, :rank]
    down_chosen = chosen[:, :, rank:].reshape(GRP, segs, halves, sub, rank)
    down_chosen = jnp.take(down_chosen, (block - jnp.arange(GRP)) % GRP, axis=0)
    down_chosen = jnp.transpose(down_chosen, (1, 0, 3, 2, 4)).reshape(segs, share, twice_rank)

    bounds = jnp.cumsum(segment_tile_counts[0])
    positions = jnp.arange(tile_count, dtype=jnp.int32)
    tile_seg = jnp.sum((bounds[None, :] <= positions[:, None]).astype(jnp.int32), axis=1)

    partial = jnp.einsum(
        "dnr,ndc->nrc", own_features, jnp.take(down_chosen, tile_seg, axis=0),
        preferred_element_type=f32,
    ).astype(bf16)
    rows = token_count // SHARES
    partial = exchange(partial.reshape(SHARES, rows, twice_rank), PLANE)
    total = jnp.sum(partial.astype(f32), axis=0).astype(bf16)
    shrunk = exchange(jnp.broadcast_to(total[None], (SHARES, rows, twice_rank)), PLANE)
    shrunk = shrunk.reshape(tile_count, TILE, twice_rank)

    frozen = jnp.dot(gathered, w, preferred_element_type=f32)

    blocks = jnp.transpose(up_chosen, (1, 2, 0, 3)).reshape(segs, rank, GRP, 2, rank // 2)
    gate_blocks = jnp.take(blocks[:, :, :, 0].reshape(segs, rank, local_hidden), tile_seg, axis=0)
    up_blocks = jnp.take(blocks[:, :, :, 1].reshape(segs, rank, local_hidden), tile_seg, axis=0)
    gate_delta = jnp.einsum(
        "tkr,trw->tkw", shrunk[:, :, :rank], gate_blocks, preferred_element_type=f32
    ).reshape(token_count, local_hidden)
    up_delta = jnp.einsum(
        "tkr,trw->tkw", shrunk[:, :, rank:], up_blocks, preferred_element_type=f32
    ).reshape(token_count, local_hidden)
    gate = frozen[:, :local_hidden] + adapter_scale * gate_delta
    up = frozen[:, local_hidden:] + adapter_scale * up_delta
    return (jax.nn.silu(gate) * up).astype(bf16)


def solution(mesh):
    fine = Mesh(mesh.devices.reshape(GRP, YL, ZN, CORES, YH), AXES)
    return jax.shard_map(
        per_device,
        mesh=fine,
        in_specs=(
            P("grp", PLANE),
            P(None, None, PLANE),
            P(PLANE, "grp", None),
            P(PLANE, "grp", None, None, None),
            P(),
            P("grp", None),
            P(),
        ),
        out_specs=P("grp", PLANE),
        check_vma=False,
    )
```

time: 834 us -> 213 us (0.26)
  blocking collectives: 356 us -> 31.2 us
  waiting for transfers between devices: 223 us -> 72.2 us
  other arithmetic: 103 us -> 11.1 us
  local copies, waits for them, and re-layouts: 113 us -> 33 us
  starting transfers between devices: 0.09 us -> 35.4 us
    psum x1 -> x0, blocking collectives: 259 us -> none  [per_device(): lax.psum(partial_shrink, ('tp', 'cores')).astype(jnp.bfloat16)]
    all_gather x3 -> x1, waiting for transfers between devices: 222 us -> 0.02 us  [per_device(): lax.all_gather(tokens, ('yhi', 'ylo', 'z', 'core'), axis=1, tiled=True)]
    all_gather x2 -> x0, other arithmetic: 80 us -> none  [the longest x1 52.7 us: per_device(): lax.all_gather(b_spread, 'grp', axis=1, tiled=True)]
    all_to_all x0 -> x3, waiting for transfers between devices: none -> 68.7 us  [exchange(): return lax.all_to_all(x, axes, split_axis=0, concat_axis=0, tiled=True)]
    all_to_all x2 -> x1, blocking collectives: 97.7 us -> 31.2 us  [exchange(): return lax.all_to_all(x, axes, split_axis=0, concat_axis=0, tiled=True)]
    all_gather x3 -> x0, local copies, waits for them, and re-layouts: 42 us -> none  [the longest x1 22.4 us: per_device(): gathered = lax.all_gather(tokens, ('tp', 'cores'), axis=1, tiled=True)]
    all_to_all x0 -> x3, starting transfers between devices: none -> 22.2 us  [exchange(): return lax.all_to_all(x, axes, split_axis=0, concat_axis=0, tiled=True)]
    unnamed x21 -> x14, local copies, waits for them, and re-layouts: 22.9 us -> 1.44 us
  transfers between devices with their start and end apart: 3 -> 8, of which waited for: 2 -> 3; matrix products, arithmetic and copies ran while one was open for 21% -> 21% of each run, Pallas kernels for 0% -> 0%
where the time goes in v1:
time: 213 us; the launch traced here: 212 us
  waiting for transfers between devices  72.2 us (34%)
  starting transfers between devices  35.4 us (17%)
  local copies, waits for them, and re-layouts  33 us (15%)
  blocking collectives  31.2 us (15%)
  matrix products  15.5 us (7%)
  between operations  13.7 us (6%)
  other arithmetic  11.1 us (5%)
    all_to_all x3, waiting for transfers between devices, exchange(): return lax.all_to_all(x, axes, split_axis=0, concat_axis=0, tiled=True)  68.7 us
    all_to_all x1, blocking collectives, exchange(): return lax.all_to_all(x, axes, split_axis=0, concat_axis=0, tiled=True)  31.2 us
    all_to_all x3, starting transfers between devices, exchange(): return lax.all_to_all(x, axes, split_axis=0, concat_axis=0, tiled=True)  22.2 us
    dot_general x1, matrix products, per_device(): frozen = jnp.dot(gathered, w, preferred_element_type=f32)  14.3 us
    reshape x1, local copies, waits for them, and re-layouts, per_device(): w = gate_up_weight.reshape(YL * ZN * CORES, YH, share, 2 * local_hidden)  14.1 us
    ppermute x4, starting transfers between devices, per_device(): own_features.append(lax.ppermute(piece, PLANE, pairs))  13.2 us
    transpose x1, local copies, waits for them, and re-layouts, per_device(): w = jnp.transpose(w, (1, 0, 2, 3)).reshape(width, 2 * local_hidden)  7.59 us
  transfers between devices with their start and end apart: 8, of which 3 were waited for; matrix products, arithmetic and copies ran while one was open for 21% of the time, Pallas kernels for 0%

profile of v1, /device:TPU:1, one launch (start us, length us, event | category | flops | bytes accessed | tf_op | source)
XLA Modules:
  0.0 212.1 jit_solution(6479657130589343259)
XLA Ops:
  6.5 0.7 all-gather.2.cloned.1.call-update
  7.3 1.3 reshape.217
  8.9 3.5 %pad_maximum_fusion = bf16[64,192,128]{2,1,0:T(8,128)(2,1)} fusion(bf16[64,64,128]{2,1,0:T(8,128)(2,1)S(1)} %bitcast.57, bf16[64,128,128]{2,1,0:T(8,128)(2,1)} %bitcast.62), kind=kLoop, calls=%fused_computation.6 | loop fusion | flops 6291456 | bytes 6291456 | tf_op jit(solution)/shard_map/concatenate | solution.py:62
  12.4 13.2 %all-to-all-start = ((bf16[64,192,128]{2,1,0:T(8,128)(2,1)}), bf16[64,192,128]{2,1,0:T(8,128)(2,1)S(1)}, u32[]{:S(2)}, u32[]{:S(2)}) async-start(bf16[64,192,128]{2,1,0:T(8,128)(2,1)} %pad_maximum_fusion), calls=%async_computation | async-start | bytes 6291456 | tf_op jit(solution)/shard_map/all_to_all | solution.py:19
  25.7 0.9 copy.23
  26.5 1.0 dynamic-slice_bitcast_fusion.3
  27.5 2.4 %collective-permute-start.2 = (bf16[32,1024]{1,0:T(8,128)(2,1)S(1)}, bf16[32,1024]{1,0:T(8,128)(2,1)S(1)}, u32[]{:S(2)}, u32[]{:S(2)}) collective-permute-start(bf16[32,1024]{1,0:T(8,128)(2,1)S(1)} %get-tuple-element.10), channel_id=1, source_target_pairs={{0,2},{1,6},{2,10},{3,14},{4,18},{5,22},{6,26},{7,30},{8,34},{9,38... | collective-permute-start | bytes 196616 | tf_op jit(solution)/shard_map/ppermute | solution.py:55
  29.9 3.8 %collective-permute-start.3 = (bf16[32,1024]{1,0:T(8,128)(2,1)S(1)}, bf16[32,1024]{1,0:T(8,128)(2,1)S(1)}, u32[]{:S(2)}, u32[]{:S(2)}) collective-permute-start(bf16[32,1024]{1,0:T(8,128)(2,1)S(1)} %get-tuple-element.9), channel_id=1, source_target_pairs={{0,3},{1,7},{2,11},{3,15},{4,19},{5,23},{6,27},{7,31},{8,35},{9,39... | collective-permute-start | bytes 196616 | tf_op jit(solution)/shard_map/ppermute | solution.py:55
  33.6 4.0 %collective-permute-start = (bf16[32,1024]{1,0:T(8,128)(2,1)S(1)}, bf16[32,1024]{1,0:T(8,128)(2,1)}, u32[]{:S(2)}, u32[]{:S(2)}) collective-permute-start(bf16[32,1024]{1,0:T(8,128)(2,1)S(1)} %get-tuple-element.8), channel_id=1, source_target_pairs={{0,0},{1,4},{2,8},{3,12},{4,16},{5,20},{6,24},{7,28},{8,32},{9,36}... | collective-permute-start | bytes 196616 | tf_op jit(solution)/shard_map/ppermute | solution.py:55
  37.7 3.1 %collective-permute-start.1 = (bf16[32,1024]{1,0:T(8,128)(2,1)S(1)}, bf16[32,1024]{1,0:T(8,128)(2,1)}, u32[]{:S(2)}, u32[]{:S(2)}) collective-permute-start(bf16[32,1024]{1,0:T(8,128)(2,1)S(1)} %get-tuple-element.11), channel_id=1, source_target_pairs={{0,1},{1,5},{2,9},{3,13},{4,17},{5,21},{6,25},{7,29},{8,33},{9,37}... | collective-permute-start | bytes 196616 | tf_op jit(solution)/shard_map/ppermute | solution.py:55
  40.8 0.6 reshape.214
  41.5 0.7 reduce-window.8
  42.2 1.2 gather_fusion
  43.4 0.7 fusion.16
  44.0 0.7 convert_reduce_fusion
  45.3 0.7 compare_and_fusion.1
  45.9 63.2 %all-to-all-done = bf16[64,192,128]{2,1,0:T(8,128)(2,1)S(1)} async-done(((bf16[64,192,128]{2,1,0:T(8,128)(2,1)}), bf16[64,192,128]{2,1,0:T(8,128)(2,1)S(1)}, u32[]{:S(2)}, u32[]{:S(2)}) %all-to-all-start) | async-done | bytes 3145760 | tf_op jit(solution)/shard_map/all_to_all | solution.py:19
  109.1 1.5 gather_fusion.1
  110.6 2.0 broadcast_select_fusion
  112.6 3.9 %all-to-all-start.1 = ((bf16[12,192,128]{2,1,0:T(8,128)(2,1)}), bf16[12,192,128]{2,1,0:T(8,128)(2,1)S(1)}, u32[]{:S(2)}, u32[]{:S(2)}) async-start(bf16[12,192,128]{2,1,0:T(8,128)(2,1)} %broadcast_select_fusion), calls=%async_computation.1 | async-start | bytes 1179648 | tf_op jit(solution)/shard_map/all_to_all | solution.py:19
  117.2 2.7 %collective-permute-done.1 = bf16[32,1024]{1,0:T(8,128)(2,1)} collective-permute-done((bf16[32,1024]{1,0:T(8,128)(2,1)S(1)}, bf16[32,1024]{1,0:T(8,128)(2,1)}, u32[]{:S(2)}, u32[]{:S(2)}) %collective-permute-start.1) | collective-permute-done | bytes 65568 | tf_op jit(solution)/shard_map/ppermute | solution.py:55
  119.9 0.9 pad_maximum_fusion.1
  120.8 5.6 %all-to-all-done.1 = bf16[12,192,128]{2,1,0:T(8,128)(2,1)S(1)} async-done(((bf16[12,192,128]{2,1,0:T(8,128)(2,1)}), bf16[12,192,128]{2,1,0:T(8,128)(2,1)S(1)}, u32[]{:S(2)}, u32[]{:S(2)}) %all-to-all-start.1) | async-done | bytes 589856 | tf_op jit(solution)/shard_map/all_to_all | solution.py:19
  128.4 31.2 %all_to_all.20 = bf16[64,16,256]{2,1,0:T(8,128)(2,1)S(1)} all-to-all(bf16[64,16,256]{2,1,0:T(8,128)(2,1)S(1)} %bitcast.63), channel_id=1, replica_groups=mesh['grp'=4,'ylo'=2,'z'=8,'core'=2,'yhi'=2] {'ylo','z','core','yhi'}, dimensions={0} | all-to-all | bytes 1048576 | tf_op jit(solution)/shard_map/all_to_all | solution.py:19
  159.7 0.8 broadcast_in_dim.43
  160.5 5.1 %all-to-all-start.3 = ((bf16[64,16,256]{2,1,0:T(8,128)(2,1)}), bf16[64,16,256]{2,1,0:T(8,128)(2,1)S(1)}, u32[]{:S(2)}, u32[]{:S(2)}) async-start(bf16[64,16,256]{2,1,0:T(8,128)(2,1)} %broadcast_in_dim.43), calls=%async_computation.3 | async-start | bytes 1048576 | tf_op jit(solution)/shard_map/all_to_all | solution.py:19
  165.6 14.1 %reshape.210 = bf16[32,2,128,512]{3,2,1,0:T(8,128)(2,1)} reshape(bf16[8192,2,256]{2,1,0:T(2,128)(2,1)} %param.10) | data formatting | bytes 16777216 | tf_op jit(solution)/shard_map/reshape | solution.py:43
  179.8 7.6 %copy.22 = bf16[2,32,128,512]{3,2,1,0:T(8,128)(2,1)} copy(bf16[2,32,128,512]{3,2,0,1:T(8,128)(2,1)} %bitcast.55) | data formatting | bytes 16777216 | tf_op jit(solution)/shard_map/transpose | solution.py:44
  187.7 0.6 gather_fusion.4
  188.3 0.6 gather_fusion.5
  189.8 14.3 %fusion.23 = f32[1024,512]{1,0:T(8,128)S(1)} fusion(bf16[1024,8192]{1,0:T(8,128)(2,1)} %all-gather.2.cloned.1.call-done, bf16[8192,512]{1,0:T(8,128)(2,1)} %bitcast.56), kind=kOutput, calls=%fused_computation.67 | convolution fusion | flops 8589934592 | bytes 27262976 | tf_op jit(solution)/shard_map/dot_general | solution.py:85
  204.2 1.1 fusion.1
  (43 shorter events, 4.7 us)
Async XLA Ops:
  6.5 35.6 %copy-start = (s32[64]{0:T(128)S(1)}, s32[64]{0:T(128)}, u32[]{:S(2)}) copy-start(s32[64]{0:T(128)} %param.15) | copy-start | bytes 772
  6.5 183.2 %all-gather.2.cloned.1.call-start = ((), (), s32[]{:S(2)}) async-start(), calls=%async_computation.4 | async-start | bytes 17039360 | tf_op jit(solution)/shard_map/all_gather | solution.py:42
  8.9 16.8 %copy-start.2 = (bf16[1024,128]{1,0:T(8,128)(2,1)S(1)}, bf16[1024,128]{1,0:T(8,128)(2,1)}, u32[]{:S(2)}) copy-start(bf16[1024,128]{1,0:T(8,128)(2,1)} %param.9) | copy-start | bytes 786436
  8.9 31.9 %copy-start.3 = (s32[4,3]{1,0:T(4,128)S(1)}, s32[4,3]{1,0:T(4,128)}, u32[]{:S(2)}) copy-start(s32[4,3]{1,0:T(4,128)} %param.13) | copy-start | bytes 148
  8.9 32.6 %copy-start.4 = (s32[1,3]{1,0:T(1,128)S(1)}, s32[1,3]{1,0:T(1,128)}, u32[]{:S(2)}) copy-start(s32[1,3]{1,0:T(1,128)} %param.14) | copy-start | bytes 40
  12.4 96.7 %all-to-all-start = ((bf16[64,192,128]{2,1,0:T(8,128)(2,1)}), bf16[64,192,128]{2,1,0:T(8,128)(2,1)S(1)}, u32[]{:S(2)}, u32[]{:S(2)}) async-start(bf16[64,192,128]{2,1,0:T(8,128)(2,1)} %pad_maximum_fusion), calls=%async_computation | async-start | bytes 6291456 | tf_op jit(solution)/shard_map/all_to_all | solution.py:19
  27.5 89.6 %collective-permute-start.2 = (bf16[32,1024]{1,0:T(8,128)(2,1)S(1)}, bf16[32,1024]{1,0:T(8,128)(2,1)S(1)}, u32[]{:S(2)}, u32[]{:S(2)}) collective-permute-start(bf16[32,1024]{1,0:T(8,128)(2,1)S(1)} %get-tuple-element.10), channel_id=1, source_target_pairs={{0,2},{1,6},{2,10},{3,14},{4,18},{5,22},{6,26},{7,30},{8,34},{9,38... | collective-permute-start | bytes 196616 | tf_op jit(solution)/shard_map/ppermute | solution.py:55
  29.9 87.3 %collective-permute-start.3 = (bf16[32,1024]{1,0:T(8,128)(2,1)S(1)}, bf16[32,1024]{1,0:T(8,128)(2,1)S(1)}, u32[]{:S(2)}, u32[]{:S(2)}) collective-permute-start(bf16[32,1024]{1,0:T(8,128)(2,1)S(1)} %get-tuple-element.9), channel_id=1, source_target_pairs={{0,3},{1,7},{2,11},{3,15},{4,19},{5,23},{6,27},{7,31},{8,35},{9,39... | collective-permute-start | bytes 196616 | tf_op jit(solution)/shard_map/ppermute | solution.py:55
  33.6 83.5 %collective-permute-start = (bf16[32,1024]{1,0:T(8,128)(2,1)S(1)}, bf16[32,1024]{1,0:T(8,128)(2,1)}, u32[]{:S(2)}, u32[]{:S(2)}) collective-permute-start(bf16[32,1024]{1,0:T(8,128)(2,1)S(1)} %get-tuple-element.8), channel_id=1, source_target_pairs={{0,0},{1,4},{2,8},{3,12},{4,16},{5,20},{6,24},{7,28},{8,32},{9,36}... | collective-permute-start | bytes 196616 | tf_op jit(solution)/shard_map/ppermute | solution.py:55
  37.7 82.2 %collective-permute-start.1 = (bf16[32,1024]{1,0:T(8,128)(2,1)S(1)}, bf16[32,1024]{1,0:T(8,128)(2,1)}, u32[]{:S(2)}, u32[]{:S(2)}) collective-permute-start(bf16[32,1024]{1,0:T(8,128)(2,1)S(1)} %get-tuple-element.11), channel_id=1, source_target_pairs={{0,1},{1,5},{2,9},{3,13},{4,17},{5,21},{6,25},{7,29},{8,33},{9,37}... | collective-permute-start | bytes 196616 | tf_op jit(solution)/shard_map/ppermute | solution.py:55
  44.7 0.5 copy-start.5
  112.6 13.8 %all-to-all-start.1 = ((bf16[12,192,128]{2,1,0:T(8,128)(2,1)}), bf16[12,192,128]{2,1,0:T(8,128)(2,1)S(1)}, u32[]{:S(2)}, u32[]{:S(2)}) async-start(bf16[12,192,128]{2,1,0:T(8,128)(2,1)} %broadcast_select_fusion), calls=%async_computation.1 | async-start | bytes 1179648 | tf_op jit(solution)/shard_map/all_to_all | solution.py:19
  160.5 28.4 %all-to-all-start.3 = ((bf16[64,16,256]{2,1,0:T(8,128)(2,1)}), bf16[64,16,256]{2,1,0:T(8,128)(2,1)S(1)}, u32[]{:S(2)}, u32[]{:S(2)}) async-start(bf16[64,16,256]{2,1,0:T(8,128)(2,1)} %broadcast_in_dim.43), calls=%async_computation.3 | async-start | bytes 1048576 | tf_op jit(solution)/shard_map/all_to_all | solution.py:19
  189.8 15.5 %copy-start.1 = (s32[64]{0:T(128)S(1)}, s32[64]{0:T(128)}, u32[]{:S(2)}) copy-start(s32[64]{0:T(128)} %param.15) | copy-start | bytes 772
Sparse Core Ops, SparseCore 0:
  9.9 178.8 all-gather.1

commit v2 on v1

v2 whole, which is shorter than its diff:
```python
import jax
import jax.numpy as jnp
from jax import lax
from jax.sharding import Mesh, PartitionSpec as P

TILE = 128
GRP = 4
YL, ZN, CORES, YH = 2, 8, 2, 2
AXES = ("grp", "ylo", "z", "core", "yhi")
PLANE = ("ylo", "z", "core", "yhi")
SHARES = YL * ZN * CORES * YH
f32 = jnp.float32
bf16 = jnp.bfloat16

adapter_scale = 0.5


def exchange(x, axes):
    return lax.all_to_all(x, axes, split_axis=0, concat_axis=0, tiled=True)


def per_device(
    tokens,
    gate_up_weight,
    down_factor_pool,
    up_factor_pool,
    segment_adapters,
    segment_tile_counts,
    adapter_pool_rows,
):
    token_count, share = tokens.shape
    tile_count = token_count // TILE
    width = gate_up_weight.shape[0]
    local_hidden = gate_up_weight.shape[2]
    twice_rank = down_factor_pool.shape[2]
    rank = twice_rank // 2
    segs = segment_adapters.shape[1]

    gathered = lax.all_gather(tokens, ("yhi", "ylo", "z", "core"), axis=1, tiled=True)
    w = gate_up_weight.reshape(YL * ZN * CORES, YH, share, 2 * local_hidden)
    w = jnp.transpose(w, (1, 0, 2, 3)).reshape(width, 2 * local_hidden)

    chosen_rows = jnp.take(adapter_pool_rows, segment_adapters.reshape(-1), mode="clip")
    up_pieces = exchange(up_factor_pool.reshape(SHARES, rank, rank), PLANE)
    up_chosen = exchange(jnp.take(up_pieces, chosen_rows, axis=0, mode="clip"), "grp")
    up_chosen = up_chosen.reshape(GRP, segs, rank, rank)

    cols = twice_rank // SHARES
    quarter_rows = down_factor_pool.shape[1]
    down_pieces = exchange(down_factor_pool[0].T.reshape(SHARES, cols, quarter_rows), PLANE)
    down_chosen = exchange(jnp.take(down_pieces, chosen_rows, axis=0, mode="clip"), "grp")
    down_chosen = down_chosen.reshape(YL, GRP // YL, segs, cols, -1, CORES, YH, share)
    down_chosen = jnp.transpose(down_chosen, (2, 3, 6, 0, 1, 4, 5, 7)).reshape(segs * cols, width)

    bounds = jnp.cumsum(segment_tile_counts[0])
    positions = jnp.arange(tile_count, dtype=jnp.int32)
    tile_seg = jnp.sum((bounds[None, :] <= positions[:, None]).astype(jnp.int32), axis=1)

    blocks = jnp.transpose(up_chosen, (1, 2, 0, 3)).reshape(segs, rank, GRP, 2, rank // 2)
    gate_blocks = jnp.take(blocks[:, :, :, 0].reshape(segs, rank, local_hidden), tile_seg, axis=0, mode="clip")
    up_blocks = jnp.take(blocks[:, :, :, 1].reshape(segs, rank, local_hidden), tile_seg, axis=0, mode="clip")

    down_chosen, w, gate_blocks, up_blocks = lax.optimization_barrier(
        (down_chosen, w, gate_blocks, up_blocks)
    )

    columns = lax.dot_general(
        down_chosen, gathered, (((1,), (1,)), ((), ())), preferred_element_type=f32
    ).reshape(segs, cols, tile_count, TILE)
    own_seg = tile_seg[None, :] == jnp.arange(segs, dtype=jnp.int32)[:, None]
    columns = jnp.sum(jnp.where(own_seg[:, None, :, None], columns, 0.0), axis=0).astype(bf16)
    columns = columns.reshape(cols, token_count)
    shrunk = exchange(jnp.broadcast_to(columns[None], (SHARES, cols, token_count)), PLANE)
    shrunk = shrunk.reshape(twice_rank, tile_count, TILE)

    frozen = jnp.dot(gathered, w, preferred_element_type=f32)

    gate_delta = jnp.einsum(
        "rtk,trw->tkw", shrunk[:rank], gate_blocks, preferred_element_type=f32
    ).reshape(token_count, local_hidden)
    up_delta = jnp.einsum(
        "rtk,trw->tkw", shrunk[rank:], up_blocks, preferred_element_type=f32
    ).reshape(token_count, local_hidden)
    gate = frozen[:, :local_hidden] + adapter_scale * gate_delta
    up = frozen[:, local_hidden:] + adapter_scale * up_delta
    return (jax.nn.silu(gate) * up).astype(bf16)


def solution(mesh):
    fine = Mesh(mesh.devices.reshape(GRP, YL, ZN, CORES, YH), AXES)
    return jax.shard_map(
        per_device,
        mesh=fine,
        in_specs=(
            P("grp", PLANE),
            P(None, None, PLANE),
            P(PLANE, "grp", None),
            P(PLANE, "grp", None, None, None),
            P(),
            P("grp", None),
            P(),
        ),
        out_specs=P("grp", PLANE),
        check_vma=False,
    )
```

time: 213 us -> 216 us (1.014)
  blocking collectives: 31.2 us -> 45.1 us
  matrix products: 15.5 us -> 26.8 us
  starting transfers between devices: 35.4 us -> 24.9 us
  other arithmetic: 11.1 us -> 2.45 us
  waiting for transfers between devices: 72.2 us -> 69.3 us
    all_to_all x1, blocking collectives: 31.2 us -> 45.1 us  [exchange(): return lax.all_to_all(x, axes, split_axis=0, concat_axis=0, tiled=True)]
    ppermute x4 -> x0, starting transfers between devices: 13.2 us -> none  [per_device(): own_features.append(lax.ppermute(piece, PLANE, pairs))]
    dot_general x3, matrix products: 1.12 us -> 10.9 us  [the longest x1 10.2 us: per_device(): lax.dot_general(down_chosen, gathered, (((1,), (1,)), ((), ())), preferre...]
    concatenate x1 -> x0, other arithmetic: 3.52 us -> none  [per_device(): pieces = exchange(jnp.concatenate([up_pieces, down_pieces], axis=1), PLANE)]
    select_n x6 -> x0, other arithmetic: 2.79 us -> none  [the longest x2 2.68 us: per_device(): chosen = exchange(jnp.take(pieces, chosen_rows, axis=0), 'grp')]
    all_to_all x3 -> x4, starting transfers between devices: 22.2 us -> 24.9 us  [exchange(): return lax.all_to_all(x, axes, split_axis=0, concat_axis=0, tiled=True)]
    ppermute x4 -> x0, waiting for transfers between devices: 2.73 us -> none  [per_device(): own_features.append(lax.ppermute(piece, PLANE, pairs))]
    all_to_all x3 -> x4, waiting for transfers between devices: 68.7 us -> 68.6 us  [exchange(): return lax.all_to_all(x, axes, split_axis=0, concat_axis=0, tiled=True)]
  transfers between devices with their start and end apart: 8 -> 5, of which waited for: 3 -> 3; matrix products, arithmetic and copies ran while one was open for 21% -> 21% of each run, Pallas kernels for 0% -> 0%
where the time goes in v2:
time: 216 us; the launch traced here: 215 us
  waiting for transfers between devices  69.3 us (32%)
  blocking collectives  45.1 us (21%)
  local copies, waits for them, and re-layouts  32.4 us (15%)
  matrix products  26.8 us (12%)
  starting transfers between devices  24.9 us (12%)
  between operations  13.6 us (6%)
  other arithmetic  2.45 us (1%)
    all_to_all x4, waiting for transfers between devices, exchange(): return lax.all_to_all(x, axes, split_axis=0, concat_axis=0, tiled=True)  68.6 us
    all_to_all x1, blocking collectives, exchange(): return lax.all_to_all(x, axes, split_axis=0, concat_axis=0, tiled=True)  45.1 us
    all_to_all x4, starting transfers between devices, exchange(): return lax.all_to_all(x, axes, split_axis=0, concat_axis=0, tiled=True)  24.9 us
    dot_general x1, matrix products, per_device(): frozen = jnp.dot(gathered, w, preferred_element_type=f32)  16 us
    reshape x1, local copies, waits for them, and re-layouts, per_device(): w = gate_up_weight.reshape(YL * ZN * CORES, YH, share, 2 * local_hidden)  14.3 us
    dot_general x1, matrix products, per_device(): lax.dot_general(down_chosen, gathered, (((1,), (1,)), ((), ())), preferre...  10.2 us
    transpose x1, local copies, waits for them, and re-layouts, per_device(): w = jnp.transpose(w, (1, 0, 2, 3)).reshape(width, 2 * local_hidden)  7.77 us
  transfers between devices with their start and end apart: 5, of which 3 were waited for; matrix products, arithmetic and copies ran while one was open for 21% of the time, Pallas kernels for 0%

profile of v2, /device:TPU:1, one launch (start us, length us, event | category | flops | bytes accessed | tf_op | source)
XLA Modules:
  0.0 214.7 jit_solution(16921573233595178930)
XLA Ops:
  6.5 0.7 all-gather.2.cloned.1.call-update
  7.3 1.5 copy.31
  8.8 0.4 reshape.86
  9.2 45.1 %all_to_all.25 = bf16[64,4,2048]{2,1,0:T(4,128)(2,1)S(1)} all-to-all(bf16[64,4,2048]{2,1,0:T(4,128)(2,1)S(1)} %reshape.86), channel_id=1, replica_groups=mesh['grp'=4,'ylo'=2,'z'=8,'core'=2,'yhi'=2] {'ylo','z','core','yhi'}, dimensions={0} | all-to-all | bytes 2097152 | tf_op jit(solution)/shard_map/all_to_all | solution.py:19
  54.3 7.8 %all-to-all-start.2 = ((bf16[64,128,128]{2,1,0:T(8,128)(2,1)}), bf16[64,128,128]{2,1,0:T(8,128)(2,1)S(1)}, u32[]{:S(2)}, u32[]{:S(2)}) async-start(bf16[64,128,128]{2,1,0:T(8,128)(2,1)} %bitcast.41), calls=%async_computation.2 | async-start | bytes 4194304 | tf_op jit(solution)/shard_map/all_to_all | solution.py:19
  62.2 0.7 gather_fusion
  62.9 1.4 gather_fusion.1
  64.3 59.3 %all-to-all-done.2 = bf16[64,128,128]{2,1,0:T(8,128)(2,1)S(1)} async-done(((bf16[64,128,128]{2,1,0:T(8,128)(2,1)}), bf16[64,128,128]{2,1,0:T(8,128)(2,1)S(1)}, u32[]{:S(2)}, u32[]{:S(2)}) %all-to-all-start.2) | async-done | bytes 2097184 | tf_op jit(solution)/shard_map/all_to_all | solution.py:19
  123.6 4.0 %all-to-all-start.1 = ((bf16[12,4,2048]{2,1,0:T(4,128)(2,1)}), bf16[12,4,2048]{2,1,0:T(4,128)(2,1)S(1)}, u32[]{:S(2)}, u32[]{:S(2)}) async-start(bf16[12,4,2048]{2,1,0:T(4,128)(2,1)} %gather_fusion.1), calls=%async_computation.1 | async-start | bytes 393216 | tf_op jit(solution)/shard_map/all_to_all | solution.py:19
  127.7 14.3 %reshape.89 = bf16[32,2,128,512]{3,2,1,0:T(8,128)(2,1)} reshape(bf16[8192,2,256]{2,1,0:T(2,128)(2,1)} %param.8) | data formatting | bytes 16777216 | tf_op jit(solution)/shard_map/reshape | solution.py:40
  141.9 7.8 %copy.33 = bf16[2,32,128,512]{3,2,1,0:T(8,128)(2,1)} copy(bf16[2,32,128,512]{3,2,0,1:T(8,128)(2,1)} %bitcast.35) | data formatting | bytes 16777216 | tf_op jit(solution)/shard_map/transpose | solution.py:41
  149.7 0.2 reduce-window.8
  149.9 1.4 gather_fusion.2
  151.3 4.3 %all-to-all-start.3 = ((bf16[12,128,128]{2,1,0:T(8,128)(2,1)}), bf16[12,128,128]{2,1,0:T(8,128)(2,1)S(1)}, u32[]{:S(2)}, u32[]{:S(2)}) async-start(bf16[12,128,128]{2,1,0:T(8,128)(2,1)} %gather_fusion.2), calls=%async_computation.3 | async-start | bytes 786432 | tf_op jit(solution)/shard_map/all_to_all | solution.py:19
  155.6 0.1 reshape.87
  155.7 0.1 copy.32
  156.0 6.8 %all-to-all-done.3 = bf16[12,128,128]{2,1,0:T(8,128)(2,1)S(1)} async-done(((bf16[12,128,128]{2,1,0:T(8,128)(2,1)}), bf16[12,128,128]{2,1,0:T(8,128)(2,1)S(1)}, u32[]{:S(2)}, u32[]{:S(2)}) %all-to-all-start.3) | async-done | bytes 393248 | tf_op jit(solution)/shard_map/all_to_all | solution.py:19
  162.8 0.2 copy.34
  163.1 0.6 gather_fusion.3
  163.7 0.6 gather_fusion.4
  164.4 10.2 %fusion.6 = f32[12,1024]{1,0:T(8,128)S(1)} fusion(bf16[12,8192]{1,0:T(8,128)(2,1)S(1)} %reshape.88, bf16[1024,8192]{1,0:T(8,128)(2,1)} %all-gather.2.cloned.1.call-done), kind=kOutput, calls=%fused_computation.25 | convolution fusion | flops 201326592 | bytes 17022976 | tf_op jit(solution)/shard_map/dot_general | solution.py:67
  174.7 0.9 broadcast_in_dim.42
  175.7 8.8 %all-to-all-start.4 = ((bf16[64,4,1024]{2,1,0:T(4,128)(2,1)}), bf16[64,4,1024]{2,1,0:T(4,128)(2,1)S(1)}, u32[]{:S(2)}, u32[]{:S(2)}) async-start(bf16[64,4,1024]{2,1,0:T(4,128)(2,1)} %broadcast_in_dim.42), calls=%async_computation.4 | async-start | bytes 1048576 | tf_op jit(solution)/shard_map/all_to_all | solution.py:19
  184.5 16.0 %convolution_bitcast_fusion = f32[1024,512]{0,1:T(8,128)} fusion(bf16[8192,512]{1,0:T(8,128)(2,1)} %bitcast.36, bf16[1024,8192]{1,0:T(8,128)(2,1)} %all-gather.2.cloned.1.call-done), kind=kOutput, calls=%fused_computation.5 | convolution fusion | flops 8589934592 | bytes 27262976 | tf_op jit(solution)/shard_map/dot_general | solution.py:76
  200.5 2.5 %all-to-all-done.4 = bf16[64,4,1024]{2,1,0:T(4,128)(2,1)S(1)} async-done(((bf16[64,4,1024]{2,1,0:T(4,128)(2,1)}), bf16[64,4,1024]{2,1,0:T(4,128)(2,1)S(1)}, u32[]{:S(2)}, u32[]{:S(2)}) %all-to-all-start.4) | async-done | bytes 524320 | tf_op jit(solution)/shard_map/all_to_all | solution.py:19
  203.0 0.2 fusion.4
  203.3 0.3 convolution_multiply_fusion
  203.6 0.3 copy.45
  204.1 0.3 convolution_multiply_fusion.1
  204.4 0.3 copy.44
  204.8 2.1 fusion.1
  206.9 1.0 copy.41
  (23 shorter events, 0.7 us)
Async XLA Ops:
  6.5 55.7 %copy-start = (s32[64]{0:T(128)S(1)}, s32[64]{0:T(128)}, u32[]{:S(2)}) copy-start(s32[64]{0:T(128)} %param.13) | copy-start | bytes 772
  6.5 55.6 %copy-start.1 = (s32[4,3]{1,0:T(4,128)S(1)}, s32[4,3]{1,0:T(4,128)}, u32[]{:S(2)}) copy-start(s32[4,3]{1,0:T(4,128)} %param.11) | copy-start | bytes 148
  6.5 157.9 %all-gather.2.cloned.1.call-start = ((), (), s32[]{:S(2)}) async-start(), calls=%async_computation.5 | async-start | bytes 17039360 | tf_op jit(solution)/shard_map/all_gather | solution.py:39
  54.3 69.3 %all-to-all-start.2 = ((bf16[64,128,128]{2,1,0:T(8,128)(2,1)}), bf16[64,128,128]{2,1,0:T(8,128)(2,1)S(1)}, u32[]{:S(2)}, u32[]{:S(2)}) async-start(bf16[64,128,128]{2,1,0:T(8,128)(2,1)} %bitcast.41), calls=%async_computation.2 | async-start | bytes 4194304 | tf_op jit(solution)/shard_map/all_to_all | solution.py:19
  123.6 27.7 %all-to-all-start.1 = ((bf16[12,4,2048]{2,1,0:T(4,128)(2,1)}), bf16[12,4,2048]{2,1,0:T(4,128)(2,1)S(1)}, u32[]{:S(2)}, u32[]{:S(2)}) async-start(bf16[12,4,2048]{2,1,0:T(4,128)(2,1)} %gather_fusion.1), calls=%async_computation.1 | async-start | bytes 393216 | tf_op jit(solution)/shard_map/all_to_all | solution.py:19
  141.9 7.8 %copy-start.2 = (s32[1,3]{1,0:T(1,128)S(1)}, s32[1,3]{1,0:T(1,128)}, u32[]{:S(2)}) copy-start(s32[1,3]{1,0:T(1,128)} %param.12) | copy-start | bytes 40
  151.3 11.5 %all-to-all-start.3 = ((bf16[12,128,128]{2,1,0:T(8,128)(2,1)}), bf16[12,128,128]{2,1,0:T(8,128)(2,1)S(1)}, u32[]{:S(2)}, u32[]{:S(2)}) async-start(bf16[12,128,128]{2,1,0:T(8,128)(2,1)} %gather_fusion.2), calls=%async_computation.3 | async-start | bytes 786432 | tf_op jit(solution)/shard_map/all_to_all | solution.py:19
  175.7 27.3 %all-to-all-start.4 = ((bf16[64,4,1024]{2,1,0:T(4,128)(2,1)}), bf16[64,4,1024]{2,1,0:T(4,128)(2,1)S(1)}, u32[]{:S(2)}, u32[]{:S(2)}) async-start(bf16[64,4,1024]{2,1,0:T(4,128)(2,1)} %broadcast_in_dim.42), calls=%async_computation.4 | async-start | bytes 1048576 | tf_op jit(solution)/shard_map/all_to_all | solution.py:19
Sparse Core Ops, SparseCore 0:
  9.9 152.0 all-gather.1

commit v3 on v2

v3 whole, which is shorter than its diff:
```python
import jax
import jax.numpy as jnp
from jax import lax
from jax.experimental import pallas as pl
from jax.experimental.pallas import tpu as pltpu
from jax.sharding import Mesh, PartitionSpec as P

TILE = 128
GRP = 4
YL, ZN, CORES, YH = 2, 8, 2, 2
AXES = ("grp", "ylo", "z", "core", "yhi")
PLANE = ("ylo", "z", "core", "yhi")
SHARES = YL * ZN * CORES * YH
f32 = jnp.float32
bf16 = jnp.bfloat16

adapter_scale = 0.5

SLOT = 8
STEPS = 8


def shrink_kernel(tile_seg, tokens, columns, out, total):
    step = pl.program_id(0)

    @pl.when(step == 0)
    def _():
        total[...] = jnp.zeros_like(total)

    total[...] += lax.dot_general(
        tokens[...], columns[...], (((1,), (1,)), ((), ())), preferred_element_type=f32
    )

    @pl.when(step == pl.num_programs(0) - 1)
    def _():
        turned = total[...].T
        for i in range(out.shape[1] // TILE):
            seg = tile_seg[i]
            at = slice(i * TILE, (i + 1) * TILE)
            pick = turned[:SLOT, at]
            for j in range(1, columns.shape[0] // SLOT):
                pick = jnp.where(seg == j, turned[j * SLOT : (j + 1) * SLOT, at], pick)
            out[:, at] = pick


def shrink(tokens, columns, tile_seg):
    count, width = tokens.shape
    slots = columns.shape[0]
    part = width // STEPS
    return pl.pallas_call(
        shrink_kernel,
        out_shape=jax.ShapeDtypeStruct((SLOT, count), f32),
        grid_spec=pltpu.PrefetchScalarGridSpec(
            num_scalar_prefetch=1,
            grid=(STEPS,),
            in_specs=[
                pl.BlockSpec((count, part), lambda k, seg: (0, k)),
                pl.BlockSpec((slots, part), lambda k, seg: (0, k)),
            ],
            out_specs=pl.BlockSpec((SLOT, count), lambda k, seg: (0, 0)),
            scratch_shapes=[pltpu.VMEM((count, slots), f32)],
        ),
        compiler_params=pltpu.CompilerParams(
            dimension_semantics=("arbitrary",), vmem_limit_bytes=60 << 20
        ),
        name="shrink",
    )(tile_seg, tokens, columns)


def frozen_kernel(tokens, weight, out):
    part = jnp.dot(tokens[...], weight[...], preferred_element_type=f32)

    @pl.when(pl.program_id(0) == 0)
    def _():
        out[...] = part

    @pl.when(pl.program_id(0) > 0)
    def _():
        out[...] += part


def frozen_matmul(tokens, weight):
    count, width = tokens.shape
    wide = weight.shape[1]
    part = width // STEPS
    return pl.pallas_call(
        frozen_kernel,
        out_shape=jax.ShapeDtypeStruct((count, wide), f32),
        grid=(STEPS,),
        in_specs=[
            pl.BlockSpec((count, part), lambda k: (0, k)),
            pl.BlockSpec((part, wide), lambda k: (k, 0)),
        ],
        out_specs=pl.BlockSpec((count, wide), lambda k: (0, 0)),
        compiler_params=pltpu.CompilerParams(
            dimension_semantics=("arbitrary",), vmem_limit_bytes=60 << 20
        ),
        name="frozen",
    )(tokens, weight)


def adapt_kernel(tile_seg, frozen, shrunk, factors, out):
    rank = factors.shape[2]
    hidden = out.shape[1]
    low = lax.broadcasted_iota(jnp.int32, (TILE, rank), 1) < rank // 2
    for_gate = shrunk[:rank, :].astype(f32).T.astype(bf16)
    for_up = shrunk[rank:, :].astype(f32).T.astype(bf16)

    def expand(left, m):
        return jnp.dot(left, factors[m, 0], preferred_element_type=f32)

    for a in range(hidden // rank):
        at = slice(a * rank, (a + 1) * rank)
        gate = jnp.where(
            low, expand(for_gate, 2 * a), pltpu.roll(expand(for_gate, 2 * a + 1), rank // 2, 1)
        )
        up = jnp.where(
            low, pltpu.roll(expand(for_up, 2 * a), rank // 2, 1), expand(for_up, 2 * a + 1)
        )
        gate = frozen[:, at] + adapter_scale * gate
        up = frozen[:, hidden + a * rank : hidden + (a + 1) * rank] + adapter_scale * up
        out[:, at] = (gate / (1.0 + jnp.exp(-gate)) * up).astype(bf16)


def adapt(frozen, shrunk, factors, tile_seg):
    count, wide = frozen.shape
    parts, _, rank, _ = factors.shape
    return pl.pallas_call(
        adapt_kernel,
        out_shape=jax.ShapeDtypeStruct((count, wide // 2), bf16),
        grid_spec=pltpu.PrefetchScalarGridSpec(
            num_scalar_prefetch=1,
            grid=(count // TILE,),
            in_specs=[
                pl.BlockSpec((TILE, wide), lambda i, seg: (i, 0)),
                pl.BlockSpec((2 * rank, TILE), lambda i, seg: (0, i)),
                pl.BlockSpec((parts, 1, rank, rank), lambda i, seg: (0, seg[i], 0, 0)),
            ],
            out_specs=pl.BlockSpec((TILE, wide // 2), lambda i, seg: (i, 0)),
        ),
        compiler_params=pltpu.CompilerParams(
            dimension_semantics=("arbitrary",), vmem_limit_bytes=60 << 20
        ),
        name="adapt",
    )(tile_seg, frozen, shrunk, factors)


def exchange(x, axes):
    return lax.all_to_all(x, axes, split_axis=0, concat_axis=0, tiled=True)


def per_device(
    tokens,
    gate_up_weight,
    down_factor_pool,
    up_factor_pool,
    segment_adapters,
    segment_tile_counts,
    adapter_pool_rows,
):
    token_count, share = tokens.shape
    tile_count = token_count // TILE
    width = gate_up_weight.shape[0]
    local_hidden = gate_up_weight.shape[2]
    twice_rank = down_factor_pool.shape[2]
    rank = twice_rank // 2
    segs = segment_adapters.shape[1]

    gathered = lax.all_gather(tokens, ("yhi", "ylo", "z", "core"), axis=1, tiled=True)
    w = gate_up_weight.reshape(YL * ZN * CORES, YH, share, 2 * local_hidden)
    w = jnp.transpose(w, (1, 0, 2, 3)).reshape(width, 2 * local_hidden)

    bounds = jnp.cumsum(segment_tile_counts[0])
    positions = jnp.arange(tile_count, dtype=jnp.int32)
    tile_seg = jnp.sum((bounds[None, :] <= positions[:, None]).astype(jnp.int32), axis=1)
    chosen_rows = jnp.take(adapter_pool_rows, segment_adapters.reshape(-1), mode="clip")

    cols = twice_rank // SHARES
    quarter_rows = down_factor_pool.shape[1]
    down_pieces = exchange(down_factor_pool[0].T.reshape(SHARES, cols, quarter_rows), PLANE)
    columns = exchange(jnp.take(down_pieces, chosen_rows, axis=0, mode="clip"), "grp")
    columns = columns.reshape(YL, GRP // YL, segs, cols, -1, CORES, YH, share)
    columns = jnp.transpose(columns, (2, 3, 6, 0, 1, 4, 5, 7)).reshape(segs, cols, width)
    columns = jnp.pad(columns, ((0, 1), (0, SLOT - cols), (0, 0))).reshape(-1, width)

    up_pieces = exchange(up_factor_pool.reshape(SHARES, rank, rank), PLANE)
    up_chosen = exchange(jnp.take(up_pieces, chosen_rows, axis=0, mode="clip"), "grp")
    up_chosen = up_chosen.reshape(GRP, segs, rank, rank)
    columns, w, up_chosen = lax.optimization_barrier((columns, w, up_chosen))

    own_columns = shrink(gathered, columns, tile_seg)[:cols].astype(bf16)
    shrunk = exchange(jnp.broadcast_to(own_columns[None], (SHARES, cols, token_count)), PLANE)

    frozen = frozen_matmul(gathered, w)
    return adapt(frozen, shrunk.reshape(twice_rank, token_count), up_chosen, tile_seg)


def solution(mesh):
    fine = Mesh(mesh.devices.reshape(GRP, YL, ZN, CORES, YH), AXES)
    return jax.shard_map(
        per_device,
        mesh=fine,
        in_specs=(
            P("grp", PLANE),
            P(None, None, PLANE),
            P(PLANE, "grp", None),
            P(PLANE, "grp", None, None, None),
            P(),
            P("grp", None),
            P(),
        ),
        out_specs=P("grp", PLANE),
        check_vma=False,
    )
```

time: 216 us -> 230 us (1.065)
  blocking collectives: 45.1 us -> 9.02 us
  Pallas kernels: 0 us -> 35.5 us
  waiting for transfers between devices: 69.3 us -> 104 us
  matrix products: 26.8 us -> 0 us
  starting transfers between devices: 24.9 us -> 33.6 us
    all_to_all x1, blocking collectives: 45.1 us -> 9.02 us  [exchange(): return lax.all_to_all(x, axes, split_axis=0, concat_axis=0, tiled=True)]
    pallas_call x0 -> x3, Pallas kernels: none -> 35.5 us  [the longest x1 16.2 us: frozen_matmul(): pl.pallas_call(frozen_kernel, out_shape=jax.ShapeDtypeStruct((count, wide...]
    dot_general x4 -> x0, matrix products: 26.8 us -> none  [the longest x1 16 us: per_device(): frozen = jnp.dot(gathered, w, preferred_element_type=f32)]
    all_gather x1, waiting for transfers between devices: 0.02 us -> 21.8 us  [per_device(): lax.all_gather(tokens, ('yhi', 'ylo', 'z', 'core'), axis=1, tiled=True)]
    all_to_all x4, waiting for transfers between devices: 68.6 us -> 81.9 us  [exchange(): return lax.all_to_all(x, axes, split_axis=0, concat_axis=0, tiled=True)]
    all_to_all x4, starting transfers between devices: 24.9 us -> 33.6 us  [exchange(): return lax.all_to_all(x, axes, split_axis=0, concat_axis=0, tiled=True)]
    transpose x3 -> x1, local copies, waits for them, and re-layouts: 8.14 us -> 0.14 us  [per_device(): jnp.transpose(columns, (2, 3, 6, 0, 1, 4, 5, 7)).reshape(segs, cols, width)]
    reshape x1 -> x2, local copies, waits for them, and re-layouts: 14.3 us -> 21.8 us  [per_device(): w = gate_up_weight.reshape(YL * ZN * CORES, YH, share, 2 * local_hidden)]
  transfers between devices with their start and end apart: 5 -> 5, of which waited for: 3 -> 5; matrix products, arithmetic and copies ran while one was open for 21% -> 13% of each run, Pallas kernels for 0% -> 7%
where the time goes in v3:
time: 230 us; the launch traced here: 229 us
  waiting for transfers between devices  104 us (45%)
  Pallas kernels  35.5 us (15%)
  starting transfers between devices  33.6 us (15%)
  local copies, waits for them, and re-layouts  31.8 us (14%)
  between operations  13.5 us (6%)
  blocking collectives  9.02 us (4%)
    all_to_all x4, waiting for transfers between devices, exchange(): return lax.all_to_all(x, axes, split_axis=0, concat_axis=0, tiled=True)  81.9 us
    all_to_all x4, starting transfers between devices, exchange(): return lax.all_to_all(x, axes, split_axis=0, concat_axis=0, tiled=True)  33.6 us
    reshape x2, local copies, waits for them, and re-layouts, per_device(): w = gate_up_weight.reshape(YL * ZN * CORES, YH, share, 2 * local_hidden)  21.8 us
    all_gather x1, waiting for transfers between devices, per_device(): lax.all_gather(tokens, ('yhi', 'ylo', 'z', 'core'), axis=1, tiled=True)  21.8 us
    pallas_call x1, Pallas kernels, frozen_matmul(): pl.pallas_call(frozen_kernel, out_shape=jax.ShapeDtypeStruct((count, wide...  16.2 us
    pallas_call x1, Pallas kernels, shrink(): pl.pallas_call(shrink_kernel, out_shape=jax.ShapeDtypeStruct((SLOT, count...  11.8 us
    all_to_all x1, blocking collectives, exchange(): return lax.all_to_all(x, axes, split_axis=0, concat_axis=0, tiled=True)  9.02 us
    pallas_call x1, Pallas kernels, adapt(): pl.pallas_call(adapt_kernel, out_shape=jax.ShapeDtypeStruct((count, wide...  7.48 us
  transfers between devices with their start and end apart: 5, of which 5 were waited for; matrix products, arithmetic and copies ran while one was open for 13% of the time, Pallas kernels for 7%

profile of v3, /device:TPU:1, one launch (start us, length us, event | category | flops | bytes accessed | tf_op | source)
XLA Modules:
  0.0 228.6 jit_solution(95474234455855585)
XLA Ops:
  6.5 0.0 all-gather.2.cloned.1.call-start
  6.5 0.7 all-gather.2.cloned.1.call-update
  7.3 1.5 copy.15
  8.8 1.2 reshape.56
  10.0 13.2 %all-to-all-start = ((bf16[64,4,2048]{2,1,0:T(4,128)(2,1)}), bf16[64,4,2048]{2,1,0:T(4,128)(2,1)S(1)}, u32[]{:S(2)}, u32[]{:S(2)}) async-start(bf16[64,4,2048]{2,1,0:T(4,128)(2,1)} %reshape.56), calls=%async_computation | async-start | bytes 2097152 | tf_op jit(solution)/shard_map/all_to_all | solution.py:149
  23.1 0.8 reshape.67
  23.9 0.7 gather_fusion
  24.6 30.7 %all-to-all-done = bf16[64,4,2048]{2,1,0:T(4,128)(2,1)S(1)} async-done(((bf16[64,4,2048]{2,1,0:T(4,128)(2,1)}), bf16[64,4,2048]{2,1,0:T(4,128)(2,1)S(1)}, u32[]{:S(2)}, u32[]{:S(2)}) %all-to-all-start) | async-done | bytes 1048608 | tf_op jit(solution)/shard_map/all_to_all | solution.py:149
  55.3 0.7 gather_fusion.1
  56.0 9.0 %all_to_all.25 = bf16[12,4,2048]{2,1,0:T(4,128)(2,1)S(1)} all-to-all(bf16[12,4,2048]{2,1,0:T(4,128)(2,1)S(1)} %gather_fusion.1), channel_id=1, replica_groups=mesh['grp'=4,'ylo'=2,'z'=8,'core'=2,'yhi'=2] {'grp'}, dimensions={0} | all-to-all | bytes 393216 | tf_op jit(solution)/shard_map/all_to_all | solution.py:149
  65.1 9.6 %all-to-all-start.2 = ((bf16[64,128,128]{2,1,0:T(8,128)(2,1)}), bf16[64,128,128]{2,1,0:T(8,128)(2,1)S(1)}, u32[]{:S(2)}, u32[]{:S(2)}) async-start(bf16[64,128,128]{2,1,0:T(8,128)(2,1)} %bitcast.14), calls=%async_computation.2 | async-start | bytes 4194304 | tf_op jit(solution)/shard_map/all_to_all | solution.py:149
  74.7 14.2 %reshape.60 = bf16[32,2,128,512]{3,2,1,0:T(8,128)(2,1)} reshape(bf16[8192,2,256]{2,1,0:T(2,128)(2,1)} %param.8) | data formatting | bytes 16777216 | tf_op jit(solution)/shard_map/reshape | solution.py:170
  88.9 7.6 %copy.17 = bf16[32,2,128,512]{3,2,0,1:T(8,128)(2,1)} copy(bf16[32,2,128,512]{3,2,1,0:T(8,128)(2,1)} %reshape.60) | data formatting | bytes 16777216 | tf_op jit(solution)/shard_map/reshape | solution.py:170
  96.5 0.2 reduce-window.8
  96.7 0.6 convert_reduce_fusion.tile_seg
  97.2 0.1 reshape.57
  97.4 0.1 copy.16
  97.5 0.1 reshape.58
  97.6 42.0 %all-to-all-done.2 = bf16[64,128,128]{2,1,0:T(8,128)(2,1)S(1)} async-done(((bf16[64,128,128]{2,1,0:T(8,128)(2,1)}), bf16[64,128,128]{2,1,0:T(8,128)(2,1)S(1)}, u32[]{:S(2)}, u32[]{:S(2)}) %all-to-all-start.2) | async-done | bytes 2097184 | tf_op jit(solution)/shard_map/all_to_all | solution.py:149
  139.6 1.4 gather_fusion.2
  141.0 3.5 %all-to-all-start.3 = ((bf16[12,128,128]{2,1,0:T(8,128)(2,1)}), bf16[12,128,128]{2,1,0:T(8,128)(2,1)S(1)}, u32[]{:S(2)}, u32[]{:S(2)}) async-start(bf16[12,128,128]{2,1,0:T(8,128)(2,1)} %gather_fusion.2), calls=%async_computation.3 | async-start | bytes 786432 | tf_op jit(solution)/shard_map/all_to_all | solution.py:149
  144.5 0.9 pad_bitcast_fusion.columns
  145.3 6.9 %all-to-all-done.3 = bf16[12,128,128]{2,1,0:T(8,128)(2,1)S(1)} async-done(((bf16[12,128,128]{2,1,0:T(8,128)(2,1)}), bf16[12,128,128]{2,1,0:T(8,128)(2,1)S(1)}, u32[]{:S(2)}, u32[]{:S(2)}) %all-to-all-start.3) | async-done | bytes 393248 | tf_op jit(solution)/shard_map/all_to_all | solution.py:149
  152.2 21.8 %all-gather.2.cloned.1.call-done.tokens = bf16[1024,8192]{1,0:T(8,128)(2,1)} async-done(((bf16[1024,128]{1,0:T(8,128)(2,1)}), bf16[1024,8192]{1,0:T(8,128)(2,1)}) %all-gather.2.cloned.1.call-update) | async-done | bytes 16777232 | tf_op jit(solution)/shard_map/all_gather | solution.py:169
  174.0 11.8 %shrink.1 = f32[8,1024]{1,0:T(8,128)} custom-call(s32[8]{0:T(128)} %convert_reduce_fusion.tile_seg, bf16[1024,8192]{1,0:T(8,128)(2,1)} %all-gather.2.cloned.1.call-done.tokens, bf16[32,8192]{1,0:T(8,128)(2,1)} %pad_bitcast_fusion.columns), custom_call_target="tpu_custom_call" | custom-call | tf_op jit(solution)/shard_map/shrink/pallas_call | solution.py:50
  185.8 0.8 slice.13
  186.5 0.9 broadcast_in_dim.20
  187.5 7.4 %all-to-all-start.4 = ((bf16[64,4,1024]{2,1,0:T(4,128)(2,1)}), bf16[64,4,1024]{2,1,0:T(4,128)(2,1)S(1)}, u32[]{:S(2)}, u32[]{:S(2)}) async-start(bf16[64,4,1024]{2,1,0:T(4,128)(2,1)} %broadcast_in_dim.20), calls=%async_computation.4 | async-start | bytes 1048576 | tf_op jit(solution)/shard_map/all_to_all | solution.py:149
  194.8 16.2 %frozen.1 = f32[1024,512]{1,0:T(8,128)} custom-call(bf16[1024,8192]{1,0:T(8,128)(2,1)} %all-gather.2.cloned.1.call-done.tokens, bf16[8192,512]{1,0:T(8,128)(2,1)} %bitcast.13), custom_call_target="tpu_custom_call" | custom-call | tf_op jit(solution)/shard_map/frozen/pallas_call | solution.py:86
  211.1 2.2 all-to-all-done.4
  213.3 0.9 reshape.64.shrunk
  214.2 7.5 %adapt.1 = bf16[1024,256]{1,0:T(8,128)(2,1)} custom-call(s32[8]{0:T(128)} %convert_reduce_fusion.tile_seg, f32[1024,512]{1,0:T(8,128)} %frozen.1, bf16[256,1024]{1,0:T(8,128)(2,1)} %reshape.64.shrunk, bf16[4,3,128,128]{3,2,1,0:T(8,128)(2,1)} %bitcast.15), custom_call_target="tpu_custom_call" | custom-call | tf_op jit(solution)/shard_map/adapt/pallas_call | solution.py:128
  (8 shorter events, 0.0 us)
Async XLA Ops:
  6.5 17.4 %copy-start = (s32[64]{0:T(128)S(1)}, s32[64]{0:T(128)}, u32[]{:S(2)}) copy-start(s32[64]{0:T(128)} %param.13) | copy-start | bytes 772
  6.5 167.4 %all-gather.2.cloned.1.call-start = ((), (), s32[]{:S(2)}) async-start(), calls=%async_computation.5 | async-start | bytes 17039360 | tf_op jit(solution)/shard_map/all_gather | solution.py:169
  10.0 45.4 %all-to-all-start = ((bf16[64,4,2048]{2,1,0:T(4,128)(2,1)}), bf16[64,4,2048]{2,1,0:T(4,128)(2,1)S(1)}, u32[]{:S(2)}, u32[]{:S(2)}) async-start(bf16[64,4,2048]{2,1,0:T(4,128)(2,1)} %reshape.56), calls=%async_computation | async-start | bytes 2097152 | tf_op jit(solution)/shard_map/all_to_all | solution.py:149
  65.1 74.6 %all-to-all-start.2 = ((bf16[64,128,128]{2,1,0:T(8,128)(2,1)}), bf16[64,128,128]{2,1,0:T(8,128)(2,1)S(1)}, u32[]{:S(2)}, u32[]{:S(2)}) async-start(bf16[64,128,128]{2,1,0:T(8,128)(2,1)} %bitcast.14), calls=%async_computation.2 | async-start | bytes 4194304 | tf_op jit(solution)/shard_map/all_to_all | solution.py:149
  88.9 7.6 %copy-start.2 = (s32[1,3]{1,0:T(1,128)S(1)}, s32[1,3]{1,0:T(1,128)}, u32[]{:S(2)}) copy-start(s32[1,3]{1,0:T(1,128)} %param.12) | copy-start | bytes 40
  141.0 11.2 %all-to-all-start.3 = ((bf16[12,128,128]{2,1,0:T(8,128)(2,1)}), bf16[12,128,128]{2,1,0:T(8,128)(2,1)S(1)}, u32[]{:S(2)}, u32[]{:S(2)}) async-start(bf16[12,128,128]{2,1,0:T(8,128)(2,1)} %gather_fusion.2), calls=%async_computation.3 | async-start | bytes 786432 | tf_op jit(solution)/shard_map/all_to_all | solution.py:149
  152.2 33.6 %copy-start.1 = (bf16[12,128,128]{2,1,0:T(8,128)(2,1)}, bf16[12,128,128]{2,1,0:T(8,128)(2,1)S(1)}, u32[]{:S(2)}) copy-start(bf16[12,128,128]{2,1,0:T(8,128)(2,1)S(1)} %all-to-all-done.3) | copy-start | bytes 1179652
  187.5 25.8 %all-to-all-start.4 = ((bf16[64,4,1024]{2,1,0:T(4,128)(2,1)}), bf16[64,4,1024]{2,1,0:T(4,128)(2,1)S(1)}, u32[]{:S(2)}, u32[]{:S(2)}) async-start(bf16[64,4,1024]{2,1,0:T(4,128)(2,1)} %broadcast_in_dim.20), calls=%async_computation.4 | async-start | bytes 1048576 | tf_op jit(solution)/shard_map/all_to_all | solution.py:149
Sparse Core Ops, SparseCore 0:
  9.9 164.0 all-gather.1

commit v4 on v3

--- a/solution.py
+++ b/solution.py
@@ -10,6 +10,7 @@
 YL, ZN, CORES, YH = 2, 8, 2, 2
 AXES = ("grp", "ylo", "z", "core", "yhi")
 PLANE = ("ylo", "z", "core", "yhi")
+LINE = ("ylo", "core", "yhi")
 SHARES = YL * ZN * CORES * YH
 f32 = jnp.float32
 bf16 = jnp.bfloat16
@@ -17,29 +18,32 @@
 adapter_scale = 0.5
 
 SLOT = 8
-STEPS = 8
+ROUND = 4
+STEPS = 4
 
 
 def shrink_kernel(tile_seg, tokens, columns, out, total):
     step = pl.program_id(0)
+    part = lax.dot_general(
+        columns[...], tokens[...], (((1,), (1,)), ((), ())), preferred_element_type=f32
+    )
 
     @pl.when(step == 0)
     def _():
-        total[...] = jnp.zeros_like(total)
-
-    total[...] += lax.dot_general(
-        tokens[...], columns[...], (((1,), (1,)), ((), ())), preferred_element_type=f32
-    )
+        total[...] = part
+
+    @pl.when(step > 0)
+    def _():
+        total[...] += part
 
     @pl.when(step == pl.num_programs(0) - 1)
     def _():
-        turned = total[...].T
         for i in range(out.shape[1] // TILE):
             seg = tile_seg[i]
             at = slice(i * TILE, (i + 1) * TILE)
-            pick = turned[:SLOT, at]
+            pick = total[:SLOT, at]
             for j in range(1, columns.shape[0] // SLOT):
-                pick = jnp.where(seg == j, turned[j * SLOT : (j + 1) * SLOT, at], pick)
+                pick = jnp.where(seg == j, total[j * SLOT : (j + 1) * SLOT, at], pick)
             out[:, at] = pick
 
 
@@ -58,7 +62,7 @@
                 pl.BlockSpec((slots, part), lambda k, seg: (0, k)),
             ],
             out_specs=pl.BlockSpec((SLOT, count), lambda k, seg: (0, 0)),
-            scratch_shapes=[pltpu.VMEM((count, slots), f32)],
+            scratch_shapes=[pltpu.VMEM((slots, count), f32)],
         ),
         compiler_params=pltpu.CompilerParams(
             dimension_semantics=("arbitrary",), vmem_limit_bytes=60 << 20
@@ -100,43 +104,43 @@
 
 
 def adapt_kernel(tile_seg, frozen, shrunk, factors, out):
-    rank = factors.shape[2]
+    parts, _, rank, _ = factors.shape
     hidden = out.shape[1]
+    tiles = out.shape[0] // TILE
     low = lax.broadcasted_iota(jnp.int32, (TILE, rank), 1) < rank // 2
-    for_gate = shrunk[:rank, :].astype(f32).T.astype(bf16)
-    for_up = shrunk[rank:, :].astype(f32).T.astype(bf16)
-
-    def expand(left, m):
-        return jnp.dot(left, factors[m, 0], preferred_element_type=f32)
-
-    for a in range(hidden // rank):
-        at = slice(a * rank, (a + 1) * rank)
-        gate = jnp.where(
-            low, expand(for_gate, 2 * a), pltpu.roll(expand(for_gate, 2 * a + 1), rank // 2, 1)
-        )
-        up = jnp.where(
-            low, pltpu.roll(expand(for_up, 2 * a), rank // 2, 1), expand(for_up, 2 * a + 1)
-        )
-        gate = frozen[:, at] + adapter_scale * gate
-        up = frozen[:, hidden + a * rank : hidden + (a + 1) * rank] + adapter_scale * up
-        out[:, at] = (gate / (1.0 + jnp.exp(-gate)) * up).astype(bf16)
+    for t in range(tiles):
+        seg = tile_seg[pl.program_id(0) * tiles + t]
+        rows = slice(t * TILE, (t + 1) * TILE)
+        wide = jnp.concatenate([factors[m, seg] for m in range(parts)], axis=1)
+        left = shrunk[:, rows].astype(f32)
+        for_gate = jnp.dot(left[:rank].T.astype(bf16), wide, preferred_element_type=f32)
+        for_up = jnp.dot(left[rank:].T.astype(bf16), wide, preferred_element_type=f32)
+        for a in range(parts // 2):
+            even = slice(2 * a * rank, (2 * a + 1) * rank)
+            odd = slice((2 * a + 1) * rank, (2 * a + 2) * rank)
+            at = slice(a * rank, (a + 1) * rank)
+            gate = jnp.where(low, for_gate[:, even], pltpu.roll(for_gate[:, odd], rank // 2, 1))
+            up = jnp.where(low, pltpu.roll(for_up[:, even], rank // 2, 1), for_up[:, odd])
+            gate = frozen[rows, at] + adapter_scale * gate
+            up = frozen[rows, hidden + a * rank : hidden + (a + 1) * rank] + adapter_scale * up
+            out[rows, at] = (gate / (1.0 + jnp.exp(-gate)) * up).astype(bf16)
 
 
 def adapt(frozen, shrunk, factors, tile_seg):
     count, wide = frozen.shape
-    parts, _, rank, _ = factors.shape
+    rows = count // STEPS
     return pl.pallas_call(
         adapt_kernel,
         out_shape=jax.ShapeDtypeStruct((count, wide // 2), bf16),
         grid_spec=pltpu.PrefetchScalarGridSpec(
             num_scalar_prefetch=1,
-            grid=(count // TILE,),
+            grid=(STEPS,),
             in_specs=[
-                pl.BlockSpec((TILE, wide), lambda i, seg: (i, 0)),
-                pl.BlockSpec((2 * rank, TILE), lambda i, seg: (0, i)),
-                pl.BlockSpec((parts, 1, rank, rank), lambda i, seg: (0, seg[i], 0, 0)),
+                pl.BlockSpec((rows, wide), lambda i, seg: (i, 0)),
+                pl.BlockSpec((shrunk.shape[0], rows), lambda i, seg: (0, i)),
+                pl.BlockSpec(factors.shape, lambda i, seg: (0, 0, 0, 0)),
             ],
-            out_specs=pl.BlockSpec((TILE, wide // 2), lambda i, seg: (i, 0)),
+            out_specs=pl.BlockSpec((rows, wide // 2), lambda i, seg: (i, 0)),
         ),
         compiler_params=pltpu.CompilerParams(
             dimension_semantics=("arbitrary",), vmem_limit_bytes=60 << 20
@@ -176,17 +180,56 @@
     chosen_rows = jnp.take(adapter_pool_rows, segment_adapters.reshape(-1), mode="clip")
 
     cols = twice_rank // SHARES
-    quarter_rows = down_factor_pool.shape[1]
-    down_pieces = exchange(down_factor_pool[0].T.reshape(SHARES, cols, quarter_rows), PLANE)
-    columns = exchange(jnp.take(down_pieces, chosen_rows, axis=0, mode="clip"), "grp")
-    columns = columns.reshape(YL, GRP // YL, segs, cols, -1, CORES, YH, share)
-    columns = jnp.transpose(columns, (2, 3, 6, 0, 1, 4, 5, 7)).reshape(segs, cols, width)
+    depth = rank + share // 2
+    line = SHARES // ZN
+    down_pool = down_factor_pool[0].T.reshape(SHARES, cols, -1, share)
+    down_pool = jnp.transpose(down_pool, (0, 2, 1, 3)).reshape(SHARES, depth - rank, share)
+    pool = jnp.concatenate([up_factor_pool.reshape(SHARES, rank, rank), down_pool], axis=1)
+
+    pool = pool.reshape(YL, ZN, CORES, YH, depth, share)
+    pool = jnp.transpose(pool, (0, 2, 3, 1, 4, 5)).reshape(line, ZN, depth, share)
+    pool = exchange(pool, LINE)
+    pool, w = lax.optimization_barrier((pool, w))
+
+    row_z = (chosen_rows // (CORES * YH)) % ZN
+    row_at = chosen_rows // (ZN * CORES * YH) * (CORES * YH) + chosen_rows % (CORES * YH)
+    used = (row_z[:, None, None] == jnp.arange(ZN)[None, :, None]) & (
+        row_at[:, None, None] == jnp.arange(line)[None, None, :]
+    )
+    used = jnp.any(used, axis=0).astype(jnp.int32)
+    earlier = jnp.arange(line)[:, None] < jnp.arange(line)[None, :]
+    order = jnp.sum(used[:, :, None] * earlier.astype(jnp.int32)[None], axis=1)
+    rounds = (jnp.max(jnp.sum(used, axis=1)) + ROUND - 1) // ROUND
+    here = (row_z[:, None, None] == jnp.arange(ZN)[None, :, None]) & (
+        row_at[:, None, None] == jnp.arange(line)[None, None, :]
+    )
+    slot_order = jnp.sum(jnp.where(here, order[None], 0), axis=(1, 2))
+    own_line = jnp.arange(ZN)[:, None] == lax.axis_index("z")
+    own_used = jnp.sum(jnp.where(own_line, used, 0), axis=0)
+    own_order = jnp.sum(jnp.where(own_line, order, 0), axis=0)
+
+    def fetch(turn):
+        wanted = turn * ROUND + jnp.arange(ROUND)
+        hit = (own_used[None, :] > 0) & (own_order[None, :] == wanted[:, None])
+        rows = jnp.sum(jnp.where(hit, jnp.arange(line)[None, :], 0), axis=1)
+        sent = jnp.take(pool, rows, axis=0, mode="clip")
+        sent = exchange(jnp.transpose(sent, (1, 0, 2, 3)), "z").reshape(-1, depth, share)
+        at = row_z * ROUND + jnp.clip(slot_order - turn * ROUND, 0, ROUND - 1)
+        return jnp.take(sent, at, axis=0, mode="clip")
+
+    def again(carry):
+        turn, chosen = carry
+        fresh = (slot_order >= turn * ROUND)[:, None, None]
+        return turn + 1, jnp.where(fresh, fetch(turn), chosen)
+
+    chosen = lax.while_loop(lambda carry: carry[0] < rounds, again, (1, fetch(0)))[1]
+
+    chosen = exchange(chosen, "grp").reshape(GRP, segs, depth, share)
+    up_chosen = chosen[:, :, :rank]
+    columns = chosen[:, :, rank:].reshape(YL, GRP // YL, segs, -1, CORES, YH, cols, share)
+    columns = jnp.transpose(columns, (2, 6, 5, 0, 1, 3, 4, 7)).reshape(segs, cols, width)
     columns = jnp.pad(columns, ((0, 1), (0, SLOT - cols), (0, 0))).reshape(-1, width)
-
-    up_pieces = exchange(up_factor_pool.reshape(SHARES, rank, rank), PLANE)
-    up_chosen = exchange(jnp.take(up_pieces, chosen_rows, axis=0, mode="clip"), "grp")
-    up_chosen = up_chosen.reshape(GRP, segs, rank, rank)
-    columns, w, up_chosen = lax.optimization_barrier((columns, w, up_chosen))
+    columns, up_chosen = lax.optimization_barrier((columns, up_chosen))
 
     own_columns = shrink(gathered, columns, tile_seg)[:cols].astype(bf16)
     shrunk = exchange(jnp.broadcast_to(own_columns[None], (SHARES, cols, token_count)), PLANE)

time: 230 us -> 212 us (0.922)
  blocking collectives: 9.02 us -> 0 us
  starting transfers between devices: 33.6 us -> 27.6 us
  Pallas kernels: 35.5 us -> 29.7 us
  local copies, waits for them, and re-layouts: 31.8 us -> 37.6 us
  waiting for transfers between devices: 104 us -> 99.5 us
    all_to_all x1 -> x0, blocking collectives: 9.02 us -> none  [exchange(): return lax.all_to_all(x, axes, split_axis=0, concat_axis=0, tiled=True)]
    all_to_all x4, starting transfers between devices: 33.6 us -> 27.6 us  [exchange(): return lax.all_to_all(x, axes, split_axis=0, concat_axis=0, tiled=True)]
    all_gather x1, waiting for transfers between devices: 21.8 us -> 16.6 us  [per_device(): lax.all_gather(tokens, ('yhi', 'ylo', 'z', 'core'), axis=1, tiled=True)]
    pallas_call x1, Pallas kernels: 7.48 us -> 5.15 us  [adapt(): pl.pallas_call(adapt_kernel, out_shape=jax.ShapeDtypeStruct((count, wide...]
  transfers between devices with their start and end apart: 5 -> 5, of which waited for: 5 -> 5; matrix products, arithmetic and copies ran while one was open for 13% -> 17% of each run, Pallas kernels for 7% -> 7%
where the time goes in v4:
time: 212 us; the launch traced here: 211 us
  waiting for transfers between devices  99.5 us (47%)
  local copies, waits for them, and re-layouts  37.6 us (18%)
  Pallas kernels  29.7 us (14%)
  starting transfers between devices  27.6 us (13%)
  between operations  14.2 us (7%)
  other arithmetic  2.48 us (1%)
    all_to_all x4, waiting for transfers between devices, exchange(): return lax.all_to_all(x, axes, split_axis=0, concat_axis=0, tiled=True)  82.2 us
    all_to_all x4, starting transfers between devices, exchange(): return lax.all_to_all(x, axes, split_axis=0, concat_axis=0, tiled=True)  27.6 us
    reshape x2, local copies, waits for them, and re-layouts, per_device(): w = gate_up_weight.reshape(YL * ZN * CORES, YH, share, 2 * local_hidden)  21.9 us
    all_gather x1, waiting for transfers between devices, per_device(): lax.all_gather(tokens, ('yhi', 'ylo', 'z', 'core'), axis=1, tiled=True)  16.6 us
    pallas_call x1, Pallas kernels, frozen_matmul(): pl.pallas_call(frozen_kernel, out_shape=jax.ShapeDtypeStruct((count, wide...  14.6 us
    pallas_call x1, Pallas kernels, shrink(): pl.pallas_call(shrink_kernel, out_shape=jax.ShapeDtypeStruct((SLOT, count...  9.93 us
    pallas_call x1, Pallas kernels, adapt(): pl.pallas_call(adapt_kernel, out_shape=jax.ShapeDtypeStruct((count, wide...  5.15 us
  transfers between devices with their start and end apart: 5, of which 5 were waited for; matrix products, arithmetic and copies ran while one was open for 17% of the time, Pallas kernels for 7%

profile of v4, /device:TPU:1, one launch (start us, length us, event | category | flops | bytes accessed | tf_op | source)
XLA Modules:
  0.0 211.1 jit_solution(18097351902939811475)
XLA Ops:
  6.5 0.7 all-gather.2.cloned.1.call-update
  7.3 1.5 copy.33
  8.8 0.2 copy.41
  9.0 0.5 copy.34
  9.6 0.8 copy-done.2
  10.3 0.3 pad_maximum_fusion
  10.7 1.8 copy.40
  12.5 7.7 %all-to-all-start.1 = ((bf16[8,8,192,128]{3,2,1,0:T(8,128)(2,1)}), bf16[8,8,192,128]{3,2,1,0:T(8,128)(2,1)}, u32[]{:S(2)}, u32[]{:S(2)}) async-start(bf16[8,8,192,128]{3,2,1,0:T(8,128)(2,1)} %bitcast.10), calls=%async_computation.1 | async-start | bytes 6291456 | tf_op jit(solution)/shard_map/all_to_all | solution.py:153
  20.3 0.7 gather_fusion.2
  21.2 14.2 %reshape.335 = bf16[32,2,128,512]{3,2,1,0:T(8,128)(2,1)} reshape(bf16[8192,2,256]{2,1,0:T(2,128)(2,1)} %param.10) | data formatting | bytes 16777216 | tf_op jit(solution)/shard_map/reshape | solution.py:174
  35.4 7.7 %copy.37 = bf16[32,2,128,512]{3,2,0,1:T(8,128)(2,1)} copy(bf16[32,2,128,512]{3,2,1,0:T(8,128)(2,1)} %reshape.335) | data formatting | bytes 16777216 | tf_op jit(solution)/shard_map/reshape | solution.py:174
  43.5 18.5 %all-to-all-done.1 = bf16[8,8,192,128]{3,2,1,0:T(8,128)(2,1)} async-done(((bf16[8,8,192,128]{3,2,1,0:T(8,128)(2,1)}), bf16[8,8,192,128]{3,2,1,0:T(8,128)(2,1)}, u32[]{:S(2)}, u32[]{:S(2)}) %all-to-all-start.1) | async-done | bytes 3145760 | tf_op jit(solution)/shard_map/all_to_all | solution.py:153
  62.0 2.7 %gather_fusion.3 = bf16[4,8,192,128]{3,2,1,0:T(8,128)(2,1)S(1)} fusion(bf16[8,8,192,128]{3,2,1,0:T(8,128)(2,1)} %all-to-all-done.1, s32[1024]{0:T(1024)S(1)} %pad_clamp_fusion.3), kind=kCustom, calls=%fused_computation.3 | custom fusion | bytes 3145744 | tf_op jit(solution)/shard_map/jit(_take)/gather | solution.py:215
  64.7 1.4 copy.38
  66.1 6.6 %all-to-all-start.2 = ((bf16[8,4,192,128]{3,2,1,0:T(8,128)(2,1)}), bf16[8,4,192,128]{3,2,1,0:T(8,128)(2,1)S(1)}, u32[]{:S(2)}, u32[]{:S(2)}) async-start(bf16[8,4,192,128]{3,2,1,0:T(8,128)(2,1)} %copy.38), calls=%async_computation.2 | async-start | bytes 3145728 | tf_op jit(solution)/shard_map/all_to_all | solution.py:153
  72.7 0.6 reduce_max.9
  74.1 52.1 %all-to-all-done.2 = bf16[8,4,192,128]{3,2,1,0:T(8,128)(2,1)S(1)} async-done(((bf16[8,4,192,128]{3,2,1,0:T(8,128)(2,1)}), bf16[8,4,192,128]{3,2,1,0:T(8,128)(2,1)S(1)}, u32[]{:S(2)}, u32[]{:S(2)}) %all-to-all-start.2) | async-done | bytes 1572896 | tf_op jit(solution)/shard_map/all_to_all | solution.py:153
  126.2 1.4 gather_fusion.4
  127.7 4.6 %all-to-all-start.3 = ((bf16[12,192,128]{2,1,0:T(8,128)(2,1)}), bf16[12,192,128]{2,1,0:T(8,128)(2,1)S(1)}, u32[]{:S(2)}, u32[]{:S(2)}) async-start(bf16[12,192,128]{2,1,0:T(8,128)(2,1)} %get-tuple-element.54), calls=%async_computation.3 | async-start | bytes 1179648 | tf_op jit(solution)/shard_map/all_to_all | solution.py:153
  132.5 0.6 convert_reduce_fusion.1.tile_seg
  133.1 7.8 %all-to-all-done.3 = bf16[12,192,128]{2,1,0:T(8,128)(2,1)S(1)} async-done(((bf16[12,192,128]{2,1,0:T(8,128)(2,1)}), bf16[12,192,128]{2,1,0:T(8,128)(2,1)S(1)}, u32[]{:S(2)}, u32[]{:S(2)}) %all-to-all-start.3) | async-done | bytes 589856 | tf_op jit(solution)/shard_map/all_to_all | solution.py:153
  140.9 0.8 slice.24.factors
  142.0 0.9 pad_bitcast_fusion.columns
  142.8 16.6 %all-gather.2.cloned.1.call-done.tokens = bf16[1024,8192]{1,0:T(8,128)(2,1)} async-done(((bf16[1024,128]{1,0:T(8,128)(2,1)}), bf16[1024,8192]{1,0:T(8,128)(2,1)}) %all-gather.2.cloned.1.call-update) | async-done | bytes 16777232 | tf_op jit(solution)/shard_map/all_gather | solution.py:173
  159.4 9.9 %shrink.1 = f32[8,1024]{1,0:T(8,128)} custom-call(s32[8]{0:T(128)} %convert_reduce_fusion.1.tile_seg, bf16[1024,8192]{1,0:T(8,128)(2,1)} %all-gather.2.cloned.1.call-done.tokens, bf16[32,8192]{1,0:T(8,128)(2,1)} %pad_bitcast_fusion.columns), custom_call_target="tpu_custom_call" | custom-call | tf_op jit(solution)/shard_map/shrink/pallas_call | solution.py:54
  169.3 0.8 slice.27
  170.1 0.9 broadcast_in_dim.115
  171.0 8.7 %all-to-all-start.4 = ((bf16[64,4,1024]{2,1,0:T(4,128)(2,1)}), bf16[64,4,1024]{2,1,0:T(4,128)(2,1)S(1)}, u32[]{:S(2)}, u32[]{:S(2)}) async-start(bf16[64,4,1024]{2,1,0:T(4,128)(2,1)} %broadcast_in_dim.115), calls=%async_computation.4 | async-start | bytes 1048576 | tf_op jit(solution)/shard_map/all_to_all | solution.py:153
  179.7 14.6 %frozen.1 = f32[1024,512]{1,0:T(8,128)} custom-call(bf16[1024,8192]{1,0:T(8,128)(2,1)} %all-gather.2.cloned.1.call-done.tokens, bf16[8192,512]{1,0:T(8,128)(2,1)} %bitcast.53), custom_call_target="tpu_custom_call" | custom-call | tf_op jit(solution)/shard_map/frozen/pallas_call | solution.py:90
  194.4 3.8 %all-to-all-done.4 = bf16[64,4,1024]{2,1,0:T(4,128)(2,1)S(1)} async-done(((bf16[64,4,1024]{2,1,0:T(4,128)(2,1)}), bf16[64,4,1024]{2,1,0:T(4,128)(2,1)S(1)}, u32[]{:S(2)}, u32[]{:S(2)}) %all-to-all-start.4) | async-done | bytes 524320 | tf_op jit(solution)/shard_map/all_to_all | solution.py:153
  198.2 0.9 reshape.342.shrunk
  199.1 5.2 %adapt.1 = bf16[1024,256]{1,0:T(8,128)(2,1)} custom-call(s32[8]{0:T(128)} %convert_reduce_fusion.1.tile_seg, f32[1024,512]{1,0:T(8,128)} %frozen.1, bf16[256,1024]{1,0:T(8,128)(2,1)} %reshape.342.shrunk, bf16[4,3,128,128]{3,2,1,0:T(8,128)(2,1)} %slice.24.factors), custom_call_target="tpu_custom_call" | custom-call | tf_op jit(solution)/shard_map/adapt/pallas_call | solution.py:132
  (31 shorter events, 1.3 us)
Async XLA Ops:
  6.5 13.8 %copy-start = (s32[64]{0:T(128)S(1)}, s32[64]{0:T(128)}, u32[]{:S(2)}) copy-start(s32[64]{0:T(128)} %param.15) | copy-start | bytes 772
  6.5 152.9 %all-gather.2.cloned.1.call-start = ((), (), s32[]{:S(2)}) async-start(), calls=%async_computation.5 | async-start | bytes 17039360 | tf_op jit(solution)/shard_map/all_gather | solution.py:173
  8.8 1.6 copy-start.2
  12.5 7.7 %copy-start.3 = (s32[4,3]{1,0:T(4,128)S(1)}, s32[4,3]{1,0:T(4,128)}, u32[]{:S(2)}) copy-start(s32[4,3]{1,0:T(4,128)} %param.13) | copy-start | bytes 148
  12.5 49.5 %all-to-all-start.1 = ((bf16[8,8,192,128]{3,2,1,0:T(8,128)(2,1)}), bf16[8,8,192,128]{3,2,1,0:T(8,128)(2,1)}, u32[]{:S(2)}, u32[]{:S(2)}) async-start(bf16[8,8,192,128]{3,2,1,0:T(8,128)(2,1)} %bitcast.10), calls=%async_computation.1 | async-start | bytes 6291456 | tf_op jit(solution)/shard_map/all_to_all | solution.py:153
  66.1 60.1 %all-to-all-start.2 = ((bf16[8,4,192,128]{3,2,1,0:T(8,128)(2,1)}), bf16[8,4,192,128]{3,2,1,0:T(8,128)(2,1)S(1)}, u32[]{:S(2)}, u32[]{:S(2)}) async-start(bf16[8,4,192,128]{3,2,1,0:T(8,128)(2,1)} %copy.38), calls=%async_computation.2 | async-start | bytes 3145728 | tf_op jit(solution)/shard_map/all_to_all | solution.py:153
  127.7 4.6 %copy-start.4 = (s32[1,3]{1,0:T(1,128)S(1)}, s32[1,3]{1,0:T(1,128)}, u32[]{:S(2)}) copy-start(s32[1,3]{1,0:T(1,128)} %param.14) | copy-start | bytes 40
  127.7 13.2 %all-to-all-start.3 = ((bf16[12,192,128]{2,1,0:T(8,128)(2,1)}), bf16[12,192,128]{2,1,0:T(8,128)(2,1)S(1)}, u32[]{:S(2)}, u32[]{:S(2)}) async-start(bf16[12,192,128]{2,1,0:T(8,128)(2,1)} %get-tuple-element.54), calls=%async_computation.3 | async-start | bytes 1179648 | tf_op jit(solution)/shard_map/all_to_all | solution.py:153
  171.0 27.2 %all-to-all-start.4 = ((bf16[64,4,1024]{2,1,0:T(4,128)(2,1)}), bf16[64,4,1024]{2,1,0:T(4,128)(2,1)S(1)}, u32[]{:S(2)}, u32[]{:S(2)}) async-start(bf16[64,4,1024]{2,1,0:T(4,128)(2,1)} %broadcast_in_dim.115), calls=%async_computation.4 | async-start | bytes 1048576 | tf_op jit(solution)/shard_map/all_to_all | solution.py:153
  179.7 24.5 %copy-start.1 = (s32[64]{0:T(128)S(1)}, s32[64]{0:T(128)}, u32[]{:S(2)}) copy-start(s32[64]{0:T(128)} %param.15) | copy-start | bytes 772
Sparse Core Ops, SparseCore 0:
  9.9 149.4 all-gather.1

commit v5 on v2

v5 whole, which is shorter than its diff:
```python
import functools

import jax
import jax.numpy as jnp
from jax import lax
from jax.experimental import pallas as pl
from jax.experimental.pallas import tpu as pltpu
from jax.sharding import Mesh, PartitionSpec as P

TILE = 128
GRP = 4
YL, ZN, CORES, YH = 2, 8, 2, 2
AXES = ("grp", "ylo", "z", "core", "yhi")
PLANE = ("ylo", "z", "core", "yhi")
CHIPS = ("ylo", "z", "yhi")
SHARES = YL * ZN * CORES * YH
f32 = jnp.float32
bf16 = jnp.bfloat16

adapter_scale = 0.5

SLOT = 8
DEEP = 4


def pieces_of(refs, counts, halved):
    parts, at = [], 0
    for n, half in zip(counts, halved):
        if half:
            top, bottom = refs[at], refs[at + 1]
            at += 2
            rows = top.shape[1]
            parts += [[(top, i, 0, rows), (bottom, i, rows, rows)] for i in range(n)]
        else:
            rows = refs[at].shape[1]
            parts += [[(refs[at], i, 0, rows)] for i in range(n)]
            at += 1
    return parts


def shrink_kernel(counts, halved, chip, tile_seg, columns, *refs):
    chunks, out, buffer, sems = refs[:-3], refs[-3], refs[-2], refs[-1]
    parts = pieces_of(chunks, counts, halved)

    def copies(k):
        slot = k % DEEP
        return [
            pltpu.make_async_copy(
                ref.at[i], buffer.at[slot, pl.ds(first, rows)], sems.at[slot, j]
            )
            for j, (ref, i, first, rows) in enumerate(parts[k])
        ]

    for k in range(DEEP):
        for copy in copies(k):
            copy.start()
    total = jnp.zeros((columns.shape[1], buffer.shape[1]), f32)
    for k in range(len(parts)):
        for copy in copies(k):
            copy.wait()
        total += lax.dot_general(
            columns[chip[k]],
            buffer[k % DEEP],
            (((1,), (1,)), ((), ())),
            preferred_element_type=f32,
        )
        if k + DEEP < len(parts):
            for copy in copies(k + DEEP):
                copy.start()
    per = columns.shape[1] // CORES
    for c in range(CORES):
        for i in range(out.shape[2] // TILE):
            seg = tile_seg[i]
            at = slice(i * TILE, (i + 1) * TILE)
            pick = total[c * per : c * per + SLOT, at]
            for j in range(1, per // SLOT):
                low = c * per + j * SLOT
                pick = jnp.where(seg == j, total[low : low + SLOT, at], pick)
            out[c, :, at] = pick


def shrink(chunks, counts, halved, columns, chip, tile_seg, rows, width):
    most = 2
    return pl.pallas_call(
        functools.partial(shrink_kernel, counts, halved),
        out_shape=jax.ShapeDtypeStruct((CORES, SLOT, rows), f32),
        grid_spec=pltpu.PrefetchScalarGridSpec(
            num_scalar_prefetch=2,
            grid=(1,),
            in_specs=[pl.BlockSpec(columns.shape, lambda i, a, b: (0, 0, 0))]
            + [pl.BlockSpec(memory_space=pl.ANY)] * len(chunks),
            out_specs=pl.BlockSpec((CORES, SLOT, rows), lambda i, a, b: (0, 0, 0)),
            scratch_shapes=[
                pltpu.VMEM((DEEP, rows, width), bf16),
                pltpu.SemaphoreType.DMA((DEEP, most)),
            ],
        ),
        compiler_params=pltpu.CompilerParams(vmem_limit_bytes=56 << 20),
        name="shrink",
    )(chip, tile_seg, columns, *chunks)


def frozen_kernel(counts, halved, first_block, own, other, *refs):
    chunks = refs[:-4]
    out, buffer, weights, sems = refs[-4:]
    parts = pieces_of(chunks, counts, halved)
    share = own.shape[1]

    def copies(k):
        slot = k % DEEP
        made = [
            (ref.at[i], buffer.at[slot, pl.ds(first, rows)])
            for ref, i, first, rows in parts[k]
        ]
        for c in range(CORES):
            block = first_block[k] + YH * c
            for which, source in enumerate((own, other)):
                made.append(
                    (source.at[block], weights.at[slot, which, pl.ds(c * share, share)])
                )
        return [
            pltpu.make_async_copy(a, b, sems.at[slot, j]) for j, (a, b) in enumerate(made)
        ]

    for k in range(DEEP):
        for copy in copies(k):
            copy.start()
    for k in range(len(parts)):
        for copy in copies(k):
            copy.wait()
        slot = k % DEEP
        for which in range(CORES):
            part = jnp.dot(buffer[slot], weights[slot, which], preferred_element_type=f32)
            if k == 0:
                out[which] = part
            else:
                out[which] += part
        if k + DEEP < len(parts):
            for copy in copies(k + DEEP):
                copy.start()


def frozen_matmul(chunks, counts, halved, own, other, first_block, rows, width):
    share, wide = own.shape[1:]
    shape = (CORES, rows, wide)
    return pl.pallas_call(
        functools.partial(frozen_kernel, counts, halved),
        out_shape=jax.ShapeDtypeStruct(shape, f32),
        grid_spec=pltpu.PrefetchScalarGridSpec(
            num_scalar_prefetch=1,
            grid=(1,),
            in_specs=[pl.BlockSpec(memory_space=pl.ANY)] * (2 + len(chunks)),
            out_specs=pl.BlockSpec(shape, lambda i, a: (0, 0, 0)),
            scratch_shapes=[
                pltpu.VMEM((DEEP, rows, width), bf16),
                pltpu.VMEM((DEEP, CORES, width, wide), bf16),
                pltpu.SemaphoreType.DMA((DEEP, 2 + 2 * CORES)),
            ],
        ),
        compiler_params=pltpu.CompilerParams(vmem_limit_bytes=56 << 20),
        name="frozen",
    )(first_block, own, other, *chunks)


def adapt_kernel(tile_seg, frozen, shrunk, own, other, out):
    parts, _, rank, _ = own.shape
    hidden = out.shape[2]
    low = lax.broadcasted_iota(jnp.int32, (TILE, rank), 1) < rank // 2
    seg = tile_seg[pl.program_id(0)]
    left = shrunk[...].astype(f32)
    gate_left = left[:rank].T.astype(bf16)
    up_left = left[rank:].T.astype(bf16)
    for which, factors in enumerate((own, other)):
        wide = jnp.concatenate([factors[m, seg] for m in range(parts)], axis=1)
        for_gate = jnp.dot(gate_left, wide, preferred_element_type=f32)
        for_up = jnp.dot(up_left, wide, preferred_element_type=f32)
        for a in range(parts // 2):
            even = slice(2 * a * rank, (2 * a + 1) * rank)
            odd = slice((2 * a + 1) * rank, (2 * a + 2) * rank)
            at = slice(a * rank, (a + 1) * rank)
            gate = jnp.where(low, for_gate[:, even], pltpu.roll(for_gate[:, odd], rank // 2, 1))
            up = jnp.where(low, pltpu.roll(for_up[:, even], rank // 2, 1), for_up[:, odd])
            gate = frozen[which, :, at] + adapter_scale * gate
            up = frozen[which, :, hidden + a * rank : hidden + (a + 1) * rank] + adapter_scale * up
            out[which, :, at] = (gate / (1.0 + jnp.exp(-gate)) * up).astype(bf16)


def adapt(frozen, shrunk, own, other, tile_seg):
    both, count, wide = frozen.shape
    whole = pl.BlockSpec(own.shape, lambda i, seg: (0, 0, 0, 0))
    return pl.pallas_call(
        adapt_kernel,
        out_shape=jax.ShapeDtypeStruct((both, count, wide // 2), bf16),
        grid_spec=pltpu.PrefetchScalarGridSpec(
            num_scalar_prefetch=1,
            grid=(count // TILE,),
            in_specs=[
                pl.BlockSpec((both, TILE, wide), lambda i, seg: (0, i, 0)),
                pl.BlockSpec((shrunk.shape[0], TILE), lambda i, seg: (0, i)),
                whole,
                whole,
            ],
            out_specs=pl.BlockSpec((both, TILE, wide // 2), lambda i, seg: (0, i, 0)),
        ),
        compiler_params=pltpu.CompilerParams(
            dimension_semantics=("arbitrary",), vmem_limit_bytes=56 << 20
        ),
        name="adapt",
    )(tile_seg, frozen, shrunk, own, other)


def exchange(x, axes):
    return lax.all_to_all(x, axes, split_axis=0, concat_axis=0, tiled=True)


def swap(x):
    return lax.ppermute(x, "core", [(0, 1), (1, 0)])


def shift_z(x, by):
    return lax.ppermute(x, "z", [(i, (i + by) % ZN) for i in range(ZN)])


def shift_y(x, by):
    at = [y % YL * YH + y // YL for y in range(YL * YH)]
    return lax.ppermute(x, ("ylo", "yhi"), [(at[y], at[(y + by) % len(at)]) for y in range(len(at))])


def per_device(
    tokens,
    gate_up_weight,
    down_factor_pool,
    up_factor_pool,
    segment_adapters,
    segment_tile_counts,
    adapter_pool_rows,
):
    core = lax.axis_index("core")
    my_z = lax.axis_index("z")
    my_y = lax.axis_index("yhi") * YL + lax.axis_index("ylo")
    token_count, share = tokens.shape
    tile_count = token_count // TILE
    width = gate_up_weight.shape[0]
    wide = 2 * gate_up_weight.shape[2]
    twice_rank = down_factor_pool.shape[2]
    rank = twice_rank // 2
    segs = segment_adapters.shape[1]
    rows = token_count // CORES
    both = CORES * share

    kept = lax.dynamic_slice_in_dim(tokens, core * rows, rows, axis=0)
    given = swap(lax.dynamic_slice_in_dim(tokens, (1 - core) * rows, rows, axis=0))
    first = core == 0
    start = jnp.concatenate(
        [jnp.where(first, kept, given), jnp.where(first, given, kept)], axis=1
    )[None]

    cols = twice_rank // SHARES
    depth = rank + share // 2
    down_pool, start = lax.optimization_barrier((down_factor_pool[0], start))
    down_pool = down_pool.T.reshape(SHARES, cols, -1, share)
    down_pool = jnp.transpose(down_pool, (0, 2, 1, 3)).reshape(SHARES, depth - rank, share)
    pool = jnp.concatenate([up_factor_pool.reshape(SHARES, rank, rank), down_pool], axis=1)

    half = rows // 2
    ahead, back = [start], [start]
    for k in range(ZN // 2 - 1):
        ahead.append(shift_z(ahead[-1], 1))
        back.append(shift_z(back[-1], -1))
        if k == 0:
            pool, gate_up_weight, ahead[1], back[1] = lax.optimization_barrier(
                (pool, gate_up_weight, ahead[1], back[1])
            )
            own_weight = gate_up_weight.reshape(SHARES, share, wide)
            near = jnp.concatenate([start, ahead[1], back[1]])
        if k == 1:
            near, own_weight, ahead[2], back[2] = lax.optimization_barrier(
                (near, own_weight, ahead[2], back[2])
            )
    far = jnp.concatenate(
        [shift_z(ahead[-1][:, :half], 1), shift_z(back[-1][:, half:], -1)], axis=1
    )
    sets = [
        (near, (0, -1, 1)),
        (jnp.concatenate([ahead[2], back[2], ahead[3], back[3]]), (-2, 2, -3, 3)),
        (far, (4,)),
    ]

    chunks, counts, halved, steps = [], [], [], []
    for group, away in sets:
        if len(chunks) == 5:
            group, chunks[1], chunks[2] = lax.optimization_barrier((group, chunks[1], chunks[2]))
        ahead_y, back_y = shift_y(group, 1), shift_y(group, -1)
        far_y = [shift_y(ahead_y[:, :half], 1), shift_y(back_y[:, half:], -1)]
        chunks += [group, ahead_y, back_y] + far_y
        counts += [len(away)] * 4
        halved += [False, False, False, True]
        steps += [(dy, dz) for dy in (0, -1, 1, 2) for dz in away]
    counts, halved = tuple(counts), tuple(halved)
    chunk_y = (my_y + jnp.array([dy for dy, _ in steps], jnp.int32)) % (YL * YH)
    chunk_z = (my_z + jnp.array([dz for _, dz in steps], jnp.int32)) % ZN
    chip = (chunk_y % YL * ZN + chunk_z) * YH + chunk_y // YL
    first_block = (chunk_y % YL * ZN + chunk_z) * CORES * YH + chunk_y // YL

    pool = exchange(pool, PLANE)
    pool, chunks[3:5], chunks[6:10] = lax.optimization_barrier((pool, chunks[3:5], chunks[6:10]))

    other_weight = swap(own_weight)

    chosen_rows = jnp.take(adapter_pool_rows, segment_adapters.reshape(-1), mode="clip")
    chosen = exchange(jnp.take(pool, chosen_rows, axis=0, mode="clip"), "grp")
    chosen = chosen.reshape(GRP, segs, depth, share)
    other_chosen = swap(chosen)
    by_core = (jnp.where(first, chosen, other_chosen), jnp.where(first, other_chosen, chosen))
    columns = []
    for part in by_core:
        part = part[:, :, rank:].reshape(YL, GRP // YL, segs, -1, CORES, YH, cols, share)
        part = jnp.transpose(part, (0, 1, 3, 5, 2, 6, 4, 7))
        part = part.reshape(SHARES // CORES, segs, cols, both)
        part = jnp.pad(part, ((0, 0), (0, 1), (0, SLOT - cols), (0, 0)))
        columns.append(part.reshape(SHARES // CORES, -1, both))
    columns = jnp.concatenate(columns, axis=1)
    own_factors, other_factors = chosen[:, :, :rank], other_chosen[:, :, :rank]

    bounds = jnp.cumsum(segment_tile_counts[0])
    positions = jnp.arange(tile_count, dtype=jnp.int32)
    tile_seg = jnp.sum((bounds[None, :] <= positions[:, None]).astype(jnp.int32), axis=1)
    tile_seg = lax.dynamic_slice_in_dim(tile_seg, core * (tile_count // CORES), tile_count // CORES)

    columns, own_factors, other_factors, own_weight, other_weight = lax.optimization_barrier(
        (columns, own_factors, other_factors, own_weight, other_weight)
    )

    own_columns = shrink(chunks, counts, halved, columns, chip, tile_seg, rows, both)
    own_columns = own_columns[:, :cols].astype(bf16)
    chips = SHARES // CORES
    shrunk = exchange(jnp.broadcast_to(own_columns[None], (chips, CORES, cols, rows)), CHIPS)
    shrunk = jnp.transpose(shrunk.reshape(YL * ZN, YH, CORES, cols, rows), (0, 2, 1, 3, 4))
    shrunk = shrunk.reshape(twice_rank, rows)

    frozen = frozen_matmul(
        chunks, counts, halved, own_weight, other_weight, first_block, rows, both
    )
    hidden = adapt(frozen, shrunk, own_factors, other_factors, tile_seg)

    other_rows = swap(hidden[1])
    return jnp.concatenate(
        [jnp.where(first, hidden[0], other_rows), jnp.where(first, other_rows, hidden[0])]
    )


def solution(mesh):
    fine = Mesh(mesh.devices.reshape(GRP, YL, ZN, CORES, YH), AXES)
    return jax.shard_map(
        per_device,
        mesh=fine,
        in_specs=(
            P("grp", PLANE),
            P(None, None, PLANE),
            P(PLANE, "grp", None),
            P(PLANE, "grp", None, None, None),
            P(),
            P("grp", None),
            P(),
        ),
        out_specs=P("grp", PLANE),
        check_vma=False,
    )
```

time: 216 us -> 261 us (1.21)
  waiting for transfers between devices: 69.3 us -> 122 us
  blocking collectives: 45.1 us -> 0 us
  starting transfers between devices: 24.9 us -> 60.1 us
  Pallas kernels: 0 us -> 30.7 us
  matrix products: 26.8 us -> 0 us
  between operations: 13.6 us -> 0.45 us
  other arithmetic: 2.45 us -> 9.61 us
  local copies, waits for them, and re-layouts: 32.4 us -> 35.9 us
    ppermute x0 -> x24, waiting for transfers between devices: none -> 116 us  [the longest x8 75.1 us: shift_z(): return lax.ppermute(x, 'z', [(i, (i + by) % ZN) for i in range(ZN)])]
    all_to_all x4 -> x3, waiting for transfers between devices: 68.6 us -> 6.02 us  [exchange(): return lax.all_to_all(x, axes, split_axis=0, concat_axis=0, tiled=True)]
    all_to_all x1 -> x0, blocking collectives: 45.1 us -> none  [exchange(): return lax.all_to_all(x, axes, split_axis=0, concat_axis=0, tiled=True)]
    ppermute x0 -> x24, starting transfers between devices: none -> 39.7 us  [the longest x12 17.6 us: shift_y(): lax.ppermute(x, ('ylo', 'yhi'), [(at[y], at[(y + by) % len(at)]) for y in...]
    pallas_call x0 -> x3, Pallas kernels: none -> 30.7 us  [the longest x1 14.3 us: frozen_matmul(): pl.pallas_call(functools.partial(frozen_kernel, counts, halved), out_shap...]
    dot_general x4 -> x0, matrix products: 26.8 us -> none  [the longest x1 16 us: per_device(): frozen = jnp.dot(gathered, w, preferred_element_type=f32)]
    slice x4 -> x11, local copies, waits for them, and re-layouts: 0.42 us -> 8.46 us  [the longest x6 3.32 us: per_device(): far_y = [shift_y(ahead_y[:, :half], 1), shift_y(back_y[:, half:], -1)]]
    transpose x4 -> x3, local copies, waits for them, and re-layouts: 9.63 us -> 2.27 us  [the longest x1 1.48 us: per_device(): down_pool = down_pool.T.reshape(SHARES, cols, -1, share)]
  transfers between devices with their start and end apart: 5 -> 27, of which waited for: 3 -> 10; matrix products, arithmetic and copies ran while one was open for 21% -> 15% of each run, Pallas kernels for 0% -> 6%
where the time goes in v5:
time: 261 us; the launch traced here: 259 us
  waiting for transfers between devices  122 us (47%)
  starting transfers between devices  60.1 us (23%)
  local copies, waits for them, and re-layouts  35.9 us (14%)
  Pallas kernels  30.7 us (12%)
  other arithmetic  9.61 us (4%)
    ppermute x8, waiting for transfers between devices, shift_z(): return lax.ppermute(x, 'z', [(i, (i + by) % ZN) for i in range(ZN)])  75.1 us
    ppermute x12, waiting for transfers between devices, shift_y(): lax.ppermute(x, ('ylo', 'yhi'), [(at[y], at[(y + by) % len(at)]) for y in...  39 us
    all_to_all x3, starting transfers between devices, exchange(): return lax.all_to_all(x, axes, split_axis=0, concat_axis=0, tiled=True)  20.4 us
    ppermute x12, starting transfers between devices, shift_y(): lax.ppermute(x, ('ylo', 'yhi'), [(at[y], at[(y + by) % len(at)]) for y in...  17.6 us
    pallas_call x1, Pallas kernels, frozen_matmul(): pl.pallas_call(functools.partial(frozen_kernel, counts, halved), out_shap...  14.3 us
    reshape x1, local copies, waits for them, and re-layouts, per_device(): own_weight = gate_up_weight.reshape(SHARES, share, wide)  14.1 us
    ppermute x4, starting transfers between devices, swap(): return lax.ppermute(x, 'core', [(0, 1), (1, 0)])  11.2 us
    pallas_call x1, Pallas kernels, shrink(): pl.pallas_call(functools.partial(shrink_kernel, counts, halved), out_shap...  11.2 us
  transfers between devices with their start and end apart: 27, of which 10 were waited for; matrix products, arithmetic and copies ran while one was open for 15% of the time, Pallas kernels for 6%

profile of v5, /device:TPU:1, one launch (start us, length us, event | category | flops | bytes accessed | tf_op | source)
XLA Modules:
  0.0 259.0 jit_solution(17468994264346070358)
XLA Ops:
  0.9 3.3 %collective-permute-start = (bf16[512,128]{1,0:T(8,128)(2,1)S(1)}, bf16[512,128]{1,0:T(8,128)(2,1)S(1)}, u32[]{:S(2)}, u32[]{:S(2)}) collective-permute-start(bf16[512,128]{1,0:T(8,128)(2,1)S(1)} %constant_dynamic-slice_fusion), channel_id=1, source_target_pairs={{0,2},{2,0},{1,3},{3,1},{4,6},{6,4},{5,7},{7,5},{8,10},{10,8},{9,1... | collective-permute-start | bytes 393224 | tf_op jit(solution)/shard_map/ppermute | solution.py:217
  6.3 3.9 %collective-permute-start.2 = (bf16[1,512,256]{2,1,0:T(8,128)(2,1)S(1)}, bf16[1,512,256]{2,1,0:T(8,128)(2,1)S(1)}, u32[]{:S(2)}, u32[]{:S(2)}) collective-permute-start(bf16[1,512,256]{2,1,0:T(8,128)(2,1)S(1)} %maximum_bitcast_fusion), channel_id=1, source_target_pairs={{0,28},{4,0},{8,4},{12,8},{16,12},{20,16},{24,20},{28,24},{1,29},{... | collective-permute-start | bytes 786440 | tf_op jit(solution)/shard_map/ppermute | solution.py:221
  10.3 1.5 copy.25
  13.4 1.9 pad_maximum_fusion
  15.2 1.3 collective-permute-done.1
  16.6 2.7 %collective-permute-start.4 = (bf16[1,512,256]{2,1,0:T(8,128)(2,1)S(1)}, bf16[1,512,256]{2,1,0:T(8,128)(2,1)S(1)}, u32[]{:S(2)}, u32[]{:S(2)}) collective-permute-start(bf16[1,512,256]{2,1,0:T(8,128)(2,1)S(1)} %collective-permute-done.2), channel_id=1, source_target_pairs={{0,28},{4,0},{8,4},{12,8},{16,12},{20,16},{24,20},{28,24},{1,29},{... | collective-permute-start | bytes 786440 | tf_op jit(solution)/shard_map/ppermute | solution.py:221
  19.2 14.1 %reshape.71.own = bf16[64,128,512]{2,1,0:T(8,128)(2,1)} reshape(bf16[8192,2,256]{2,1,0:T(2,128)(2,1)} %param.10) | data formatting | bytes 16777216 | tf_op jit(solution)/shard_map/reshape | solution.py:274
  33.4 1.5 collective-permute-start.16
  35.0 9.0 %all-to-all-start = ((bf16[64,192,128]{2,1,0:T(8,128)(2,1)}), bf16[64,192,128]{2,1,0:T(8,128)(2,1)}, u32[]{:S(2)}, u32[]{:S(2)}) async-start(bf16[64,192,128]{2,1,0:T(8,128)(2,1)} %pad_maximum_fusion), calls=%async_computation | async-start | bytes 6291456 | tf_op jit(solution)/shard_map/all_to_all | solution.py:213
  44.0 1.6 collective-permute-start.5
  46.9 2.6 collective-permute-start.10
  49.5 69.4 %collective-permute-done.10 = bf16[1,512,256]{2,1,0:T(8,128)(2,1)S(1)} collective-permute-done((bf16[1,512,256]{2,1,0:T(8,128)(2,1)S(1)}, bf16[1,512,256]{2,1,0:T(8,128)(2,1)S(1)}, u32[]{:S(2)}, u32[]{:S(2)}) %collective-permute-start.10) | collective-permute-done | bytes 262176 | tf_op jit(solution)/shard_map/ppermute | solution.py:221
  120.3 1.5 collective-permute-start.11
  121.8 1.5 collective-permute-start.12
  123.3 22.1 %collective-permute-done.11.refs_6_ = bf16[4,512,256]{2,1,0:T(8,128)(2,1)S(1)} collective-permute-done((bf16[4,512,256]{2,1,0:T(8,128)(2,1)S(1)}, bf16[4,512,256]{2,1,0:T(8,128)(2,1)S(1)}, u32[]{:S(2)}, u32[]{:S(2)}) %collective-permute-start.11) | collective-permute-done | bytes 1048608 | tf_op jit(solution)/shard_map/ppermute | solution.py:226
  147.4 2.5 collective-permute-start.14
  151.4 2.7 %collective-permute-start.8 = (bf16[3,256,256]{2,1,0:T(8,128)(2,1)}, bf16[3,256,256]{2,1,0:T(8,128)(2,1)}, u32[]{:S(2)}, u32[]{:S(2)}) collective-permute-start(bf16[3,256,256]{2,1,0:T(8,128)(2,1)} %slice.67), channel_id=1, source_target_pairs={{0,33},{32,0},{1,32},{33,1},{2,35},{34,2},{3,34},{35,3},{4,37},{36... | collective-permute-start | bytes 1179656 | tf_op jit(solution)/shard_map/ppermute | solution.py:226
  154.9 12.9 %collective-permute-done.6.refs_3_ = bf16[3,256,256]{2,1,0:T(8,128)(2,1)S(1)} collective-permute-done((bf16[3,256,256]{2,1,0:T(8,128)(2,1)}, bf16[3,256,256]{2,1,0:T(8,128)(2,1)S(1)}, u32[]{:S(2)}, u32[]{:S(2)}) %collective-permute-start.6) | collective-permute-done | bytes 393248 | tf_op jit(solution)/shard_map/ppermute | solution.py:226
  167.8 3.5 %gather_fusion.1 = bf16[12,192,128]{2,1,0:T(8,128)(2,1)} fusion(bf16[64,192,128]{2,1,0:T(8,128)(2,1)} %all-to-all-done, s32[1024]{0:T(1024)S(1)} %pad_clamp_fusion), kind=kCustom, calls=%fused_computation.1 | custom fusion | bytes 1179696 | tf_op jit(solution)/shard_map/jit(_take)/gather | solution.py:311
  171.3 4.2 %all-to-all-start.1 = ((bf16[12,192,128]{2,1,0:T(8,128)(2,1)}), bf16[12,192,128]{2,1,0:T(8,128)(2,1)}, u32[]{:S(2)}, u32[]{:S(2)}) async-start(bf16[12,192,128]{2,1,0:T(8,128)(2,1)} %gather_fusion.1), calls=%async_computation.1 | async-start | bytes 1179648 | tf_op jit(solution)/shard_map/all_to_all | solution.py:213
  176.8 6.0 %all-to-all-done.1 = bf16[12,192,128]{2,1,0:T(8,128)(2,1)} async-done(((bf16[12,192,128]{2,1,0:T(8,128)(2,1)}), bf16[12,192,128]{2,1,0:T(8,128)(2,1)}, u32[]{:S(2)}, u32[]{:S(2)}) %all-to-all-start.1) | async-done | bytes 589856 | tf_op jit(solution)/shard_map/all_to_all | solution.py:213
  182.8 4.1 %collective-permute-start.15 = (bf16[4,3,192,128]{3,2,1,0:T(8,128)(2,1)}, bf16[4,3,192,128]{3,2,1,0:T(8,128)(2,1)S(1)}, u32[]{:S(2)}, u32[]{:S(2)}) collective-permute-start(bf16[4,3,192,128]{3,2,1,0:T(8,128)(2,1)} %bitcast.8), channel_id=1, source_target_pairs={{0,2},{2,0},{1,3},{3,1},{4,6},{6,4},{5,7},{7,5},{8,10},{10,8},{9,1... | collective-permute-start | bytes 1769480 | tf_op jit(solution)/shard_map/ppermute | solution.py:217
  190.0 3.1 %collective-permute-done.18 = bf16[1,256,256]{2,1,0:T(8,128)(2,1)S(1)} collective-permute-done((bf16[1,256,256]{2,1,0:T(8,128)(2,1)S(1)}, bf16[1,256,256]{2,1,0:T(8,128)(2,1)S(1)}, u32[]{:S(2)}, u32[]{:S(2)}) %collective-permute-start.18) | collective-permute-done | bytes 131104 | tf_op jit(solution)/shard_map/ppermute | solution.py:221
  193.9 2.8 %collective-permute-start.20 = (bf16[1,512,256]{2,1,0:T(8,128)(2,1)S(1)}, bf16[1,512,256]{2,1,0:T(8,128)(2,1)S(1)}, u32[]{:S(2)}, u32[]{:S(2)}) collective-permute-start(bf16[1,512,256]{2,1,0:T(8,128)(2,1)S(1)} %constant_dynamic-update-slice_fusion.refs_10_), channel_id=1, source_target_pairs={{0,33},{32,0},{1,32},{33,1},{2,35},{34,2},{3,34},{35,3},{4,37},{36... | collective-permute-start | bytes 786440 | tf_op jit(solution)/shard_map/ppermute | solution.py:226
  198.6 3.9 %collective-permute-done.19.refs_11_ = bf16[1,512,256]{2,1,0:T(8,128)(2,1)S(1)} collective-permute-done((bf16[1,512,256]{2,1,0:T(8,128)(2,1)S(1)}, bf16[1,512,256]{2,1,0:T(8,128)(2,1)S(1)}, u32[]{:S(2)}, u32[]{:S(2)}) %collective-permute-start.19) | collective-permute-done | bytes 262176 | tf_op jit(solution)/shard_map/ppermute | solution.py:226
  202.6 2.7 %collective-permute-start.22 = (bf16[1,256,256]{2,1,0:T(8,128)(2,1)S(1)}, bf16[1,256,256]{2,1,0:T(8,128)(2,1)S(1)}, u32[]{:S(2)}, u32[]{:S(2)}) collective-permute-start(bf16[1,256,256]{2,1,0:T(8,128)(2,1)S(1)} %slice.79), channel_id=1, source_target_pairs={{0,33},{32,0},{1,32},{33,1},{2,35},{34,2},{3,34},{35,3},{4,37},{36... | collective-permute-start | bytes 393224 | tf_op jit(solution)/shard_map/ppermute | solution.py:226
  205.4 1.8 slice.74.own
  211.9 11.2 %shrink.1 = f32[2,8,512]{2,1,0:T(8,128)} custom-call(s32[32]{0:T(128)} %get-tuple-element.55.chip, s32[4]{0:T(128)} %dynamic_slice.9.tile_seg, bf16[32,64,256]{2,1,0:T(8,128)(2,1)} %pad_maximum_fusion.2.columns, bf16[3,512,256]{2,1,0:T(8,128)(2,1)} %copy-done.2, bf16[3,512,256]{2,1,0:T(8,128)(2,1)} %copy-done.5, bf16[3,512,256]{2,1,0:T(8,128)(2,1)} %copy-done.6, ...), custom_call_target="tpu_custom_call" | custom-call | tf_op jit(solution)/shard_map/shrink/pallas_call | solution.py:84
  224.6 7.2 %all-to-all-start.2 = ((bf16[32,2,4,512]{3,2,1,0:T(4,128)(2,1)}), bf16[32,2,4,512]{3,2,1,0:T(4,128)(2,1)S(1)}, u32[]{:S(2)}, u32[]{:S(2)}) async-start(bf16[32,2,4,512]{3,2,1,0:T(4,128)(2,1)} %broadcast_in_dim.22), calls=%async_computation.2 | async-start | bytes 524288 | tf_op jit(solution)/shard_map/all_to_all | solution.py:213
  232.3 14.3 %frozen.1 = f32[2,512,512]{2,1,0:T(8,128)} custom-call(s32[32]{0:T(128)} %multiply_add_fusion.1.first_block, bf16[64,128,512]{2,1,0:T(8,128)(2,1)} %reshape.71.own, bf16[64,128,512]{2,1,0:T(8,128)(2,1)} %collective-permute-done.16.other, bf16[3,512,256]{2,1,0:T(8,128)(2,1)} %copy-done.2, bf16[3,512,256]{2,1,0:T(8,128)(2,1)} %copy-done.5, ...), custom_call_target="tpu_custom_call" | custom-call | tf_op jit(solution)/shard_map/frozen/pallas_call | solution.py:146
  247.6 5.2 %adapt.1 = bf16[2,512,256]{2,1,0:T(8,128)(2,1)} custom-call(s32[4]{0:T(128)} %dynamic_slice.9.tile_seg, f32[2,512,512]{2,1,0:T(8,128)} %frozen.1, bf16[256,512]{1,0:T(8,128)(2,1)} %reshape.80.shrunk, bf16[4,3,128,128]{3,2,1,0:T(8,128)(2,1)} %slice.74.own, bf16[4,3,128,128]{3,2,1,0:T(8,128)(2,1)} %slice.75.other), custom_call_target="tpu_custom_call" | custom-call | tf_op jit(solution)/shard_map/adapt/pallas_call | solution.py:191
  253.8 2.3 collective-permute-start.23
  (110 shorter events, 30.4 us)
Async XLA Ops:
  0.0 154.2 %copy-start = (s32[64]{0:T(128)S(1)}, s32[64]{0:T(128)}, u32[]{:S(2)}) copy-start(s32[64]{0:T(128)} %param.15) | copy-start | bytes 772
  0.9 4.3 %collective-permute-start = (bf16[512,128]{1,0:T(8,128)(2,1)S(1)}, bf16[512,128]{1,0:T(8,128)(2,1)S(1)}, u32[]{:S(2)}, u32[]{:S(2)}) collective-permute-start(bf16[512,128]{1,0:T(8,128)(2,1)S(1)} %constant_dynamic-slice_fusion), channel_id=1, source_target_pairs={{0,2},{2,0},{1,3},{3,1},{4,6},{6,4},{5,7},{7,5},{8,10},{10,8},{9,1... | collective-permute-start | bytes 393224 | tf_op jit(solution)/shard_map/ppermute | solution.py:217
  6.3 10.3 %collective-permute-start.1 = (bf16[1,512,256]{2,1,0:T(8,128)(2,1)S(1)}, bf16[1,512,256]{2,1,0:T(8,128)(2,1)S(1)}, u32[]{:S(2)}, u32[]{:S(2)}) collective-permute-start(bf16[1,512,256]{2,1,0:T(8,128)(2,1)S(1)} %maximum_bitcast_fusion), channel_id=1, source_target_pairs={{0,4},{4,8},{8,12},{12,16},{16,20},{20,24},{24,28},{28,0},{1,5},{5... | collective-permute-start | bytes 786440 | tf_op jit(solution)/shard_map/ppermute | solution.py:221
  6.3 10.2 %collective-permute-start.2 = (bf16[1,512,256]{2,1,0:T(8,128)(2,1)S(1)}, bf16[1,512,256]{2,1,0:T(8,128)(2,1)S(1)}, u32[]{:S(2)}, u32[]{:S(2)}) collective-permute-start(bf16[1,512,256]{2,1,0:T(8,128)(2,1)S(1)} %maximum_bitcast_fusion), channel_id=1, source_target_pairs={{0,28},{4,0},{8,4},{12,8},{16,12},{20,16},{24,20},{28,24},{1,29},{... | collective-permute-start | bytes 786440 | tf_op jit(solution)/shard_map/ppermute | solution.py:221
  16.6 16.8 %collective-permute-start.3 = (bf16[1,512,256]{2,1,0:T(8,128)(2,1)S(1)}, bf16[1,512,256]{2,1,0:T(8,128)(2,1)S(1)}, u32[]{:S(2)}, u32[]{:S(2)}) collective-permute-start(bf16[1,512,256]{2,1,0:T(8,128)(2,1)S(1)} %collective-permute-done.1), channel_id=1, source_target_pairs={{0,4},{4,8},{8,12},{12,16},{16,20},{20,24},{24,28},{28,0},{1,5},{5... | collective-permute-start | bytes 786440 | tf_op jit(solution)/shard_map/ppermute | solution.py:221
  16.6 16.9 %collective-permute-start.4 = (bf16[1,512,256]{2,1,0:T(8,128)(2,1)S(1)}, bf16[1,512,256]{2,1,0:T(8,128)(2,1)S(1)}, u32[]{:S(2)}, u32[]{:S(2)}) collective-permute-start(bf16[1,512,256]{2,1,0:T(8,128)(2,1)S(1)} %collective-permute-done.2), channel_id=1, source_target_pairs={{0,28},{4,0},{8,4},{12,8},{16,12},{20,16},{24,20},{28,24},{1,29},{... | collective-permute-start | bytes 786440 | tf_op jit(solution)/shard_map/ppermute | solution.py:221
  33.4 177.7 %collective-permute-start.16 = (bf16[64,128,512]{2,1,0:T(8,128)(2,1)}, bf16[64,128,512]{2,1,0:T(8,128)(2,1)}, u32[]{:S(2)}, u32[]{:S(2)}) collective-permute-start(bf16[64,128,512]{2,1,0:T(8,128)(2,1)} %reshape.71.own), channel_id=1, source_target_pairs={{0,2},{2,0},{1,3},{3,1},{4,6},{6,4},{5,7},{7,5},{8,10},{10,8},{9,1... | collective-permute-start | bytes 25165832 | tf_op jit(solution)/shard_map/ppermute | solution.py:217
  35.0 132.9 %all-to-all-start = ((bf16[64,192,128]{2,1,0:T(8,128)(2,1)}), bf16[64,192,128]{2,1,0:T(8,128)(2,1)}, u32[]{:S(2)}, u32[]{:S(2)}) async-start(bf16[64,192,128]{2,1,0:T(8,128)(2,1)} %pad_maximum_fusion), calls=%async_computation | async-start | bytes 6291456 | tf_op jit(solution)/shard_map/all_to_all | solution.py:213
  44.0 110.1 %copy-start.16 = (s32[4,3]{1,0:T(4,128)S(1)}, s32[4,3]{1,0:T(4,128)}, u32[]{:S(2)}) copy-start(s32[4,3]{1,0:T(4,128)} %param.13) | copy-start | bytes 148
  44.0 76.3 %collective-permute-start.5 = (bf16[3,512,256]{2,1,0:T(8,128)(2,1)S(1)}, bf16[3,512,256]{2,1,0:T(8,128)(2,1)S(1)}, u32[]{:S(2)}, u32[]{:S(2)}) collective-permute-start(bf16[3,512,256]{2,1,0:T(8,128)(2,1)S(1)} %pad_maximum_fusion.3.refs_0_), channel_id=1, source_target_pairs={{0,32},{32,1},{1,33},{33,0},{2,34},{34,3},{3,35},{35,2},{4,36},{36... | collective-permute-start | bytes 2359304 | tf_op jit(solution)/shard_map/ppermute | solution.py:226
  45.6 74.7 %collective-permute-start.7 = (bf16[3,512,256]{2,1,0:T(8,128)(2,1)S(1)}, bf16[3,512,256]{2,1,0:T(8,128)(2,1)S(1)}, u32[]{:S(2)}, u32[]{:S(2)}) collective-permute-start(bf16[3,512,256]{2,1,0:T(8,128)(2,1)S(1)} %pad_maximum_fusion.3.refs_0_), channel_id=1, source_target_pairs={{0,33},{32,0},{1,32},{33,1},{2,35},{34,2},{3,34},{35,3},{4,37},{36... | collective-permute-start | bytes 2359304 | tf_op jit(solution)/shard_map/ppermute | solution.py:226
  46.9 72.0 %collective-permute-start.10 = (bf16[1,512,256]{2,1,0:T(8,128)(2,1)S(1)}, bf16[1,512,256]{2,1,0:T(8,128)(2,1)S(1)}, u32[]{:S(2)}, u32[]{:S(2)}) collective-permute-start(bf16[1,512,256]{2,1,0:T(8,128)(2,1)S(1)} %collective-permute-done.4), channel_id=1, source_target_pairs={{0,28},{4,0},{8,4},{12,8},{16,12},{20,16},{24,20},{28,24},{1,29},{... | collective-permute-start | bytes 786440 | tf_op jit(solution)/shard_map/ppermute | solution.py:221
  49.5 70.7 %collective-permute-start.9 = (bf16[1,512,256]{2,1,0:T(8,128)(2,1)S(1)}, bf16[1,512,256]{2,1,0:T(8,128)(2,1)S(1)}, u32[]{:S(2)}, u32[]{:S(2)}) collective-permute-start(bf16[1,512,256]{2,1,0:T(8,128)(2,1)S(1)} %collective-permute-done.3), channel_id=1, source_target_pairs={{0,4},{4,8},{8,12},{12,16},{16,20},{20,24},{24,28},{28,0},{1,5},{5... | collective-permute-start | bytes 786440 | tf_op jit(solution)/shard_map/ppermute | solution.py:221
  120.3 51.0 %copy-start.1 = (bf16[4,512,256]{2,1,0:T(8,128)(2,1)}, bf16[4,512,256]{2,1,0:T(8,128)(2,1)S(1)}, u32[]{:S(2)}) copy-start(bf16[4,512,256]{2,1,0:T(8,128)(2,1)S(1)} %pad_maximum_fusion.1.refs_5_) | copy-start | bytes 3145732
  120.3 25.1 %collective-permute-start.11 = (bf16[4,512,256]{2,1,0:T(8,128)(2,1)S(1)}, bf16[4,512,256]{2,1,0:T(8,128)(2,1)S(1)}, u32[]{:S(2)}, u32[]{:S(2)}) collective-permute-start(bf16[4,512,256]{2,1,0:T(8,128)(2,1)S(1)} %pad_maximum_fusion.1.refs_5_), channel_id=1, source_target_pairs={{0,32},{32,1},{1,33},{33,0},{2,34},{34,3},{3,35},{35,2},{4,36},{36... | collective-permute-start | bytes 3145736 | tf_op jit(solution)/shard_map/ppermute | solution.py:226
  121.8 24.7 %collective-permute-start.12 = (bf16[4,512,256]{2,1,0:T(8,128)(2,1)S(1)}, bf16[4,512,256]{2,1,0:T(8,128)(2,1)S(1)}, u32[]{:S(2)}, u32[]{:S(2)}) collective-permute-start(bf16[4,512,256]{2,1,0:T(8,128)(2,1)S(1)} %pad_maximum_fusion.1.refs_5_), channel_id=1, source_target_pairs={{0,33},{32,0},{1,32},{33,1},{2,35},{34,2},{3,34},{35,3},{4,37},{36... | collective-permute-start | bytes 3145736 | tf_op jit(solution)/shard_map/ppermute | solution.py:226
  146.3 51.1 %copy-start.17 = (s32[32]{0:T(128)S(1)}, s32[32]{0:T(128)}, u32[]{:S(2)}) copy-start(s32[32]{0:T(128)} %constant.87.clone) | copy-start | bytes 388
  146.3 21.5 %collective-permute-start.13 = (bf16[4,256,256]{2,1,0:T(8,128)(2,1)}, bf16[4,256,256]{2,1,0:T(8,128)(2,1)}, u32[]{:S(2)}, u32[]{:S(2)}) collective-permute-start(bf16[4,256,256]{2,1,0:T(8,128)(2,1)} %slice.68), channel_id=1, source_target_pairs={{0,32},{32,1},{1,33},{33,0},{2,34},{34,3},{3,35},{35,2},{4,36},{36... | collective-permute-start | bytes 1572872 | tf_op jit(solution)/shard_map/ppermute | solution.py:226
  146.5 43.5 %copy-start.4 = (bf16[4,512,256]{2,1,0:T(8,128)(2,1)}, bf16[4,512,256]{2,1,0:T(8,128)(2,1)S(1)}, u32[]{:S(2)}) copy-start(bf16[4,512,256]{2,1,0:T(8,128)(2,1)S(1)} %collective-permute-done.12.refs_7_) | copy-start | bytes 3145732
  147.4 20.4 %collective-permute-start.14 = (bf16[4,256,256]{2,1,0:T(8,128)(2,1)}, bf16[4,256,256]{2,1,0:T(8,128)(2,1)}, u32[]{:S(2)}, u32[]{:S(2)}) collective-permute-start(bf16[4,256,256]{2,1,0:T(8,128)(2,1)} %slice.69), channel_id=1, source_target_pairs={{0,33},{32,0},{1,32},{33,1},{2,35},{34,2},{3,34},{35,3},{4,37},{36... | collective-permute-start | bytes 1572872 | tf_op jit(solution)/shard_map/ppermute | solution.py:226
  150.6 17.1 %collective-permute-start.6 = (bf16[3,256,256]{2,1,0:T(8,128)(2,1)}, bf16[3,256,256]{2,1,0:T(8,128)(2,1)S(1)}, u32[]{:S(2)}, u32[]{:S(2)}) collective-permute-start(bf16[3,256,256]{2,1,0:T(8,128)(2,1)} %slice.66), channel_id=1, source_target_pairs={{0,32},{32,1},{1,33},{33,0},{2,34},{34,3},{3,35},{35,2},{4,36},{36... | collective-permute-start | bytes 1179656 | tf_op jit(solution)/shard_map/ppermute | solution.py:226
  151.4 16.4 %collective-permute-start.8 = (bf16[3,256,256]{2,1,0:T(8,128)(2,1)}, bf16[3,256,256]{2,1,0:T(8,128)(2,1)}, u32[]{:S(2)}, u32[]{:S(2)}) collective-permute-start(bf16[3,256,256]{2,1,0:T(8,128)(2,1)} %slice.67), channel_id=1, source_target_pairs={{0,33},{32,0},{1,32},{33,1},{2,35},{34,2},{3,34},{35,3},{4,37},{36... | collective-permute-start | bytes 1179656 | tf_op jit(solution)/shard_map/ppermute | solution.py:226
  171.3 11.5 %all-to-all-start.1 = ((bf16[12,192,128]{2,1,0:T(8,128)(2,1)}), bf16[12,192,128]{2,1,0:T(8,128)(2,1)}, u32[]{:S(2)}, u32[]{:S(2)}) async-start(bf16[12,192,128]{2,1,0:T(8,128)(2,1)} %gather_fusion.1), calls=%async_computation.1 | async-start | bytes 1179648 | tf_op jit(solution)/shard_map/all_to_all | solution.py:213
  176.4 13.5 %collective-permute-start.17 = (bf16[1,256,256]{2,1,0:T(8,128)(2,1)S(1)}, bf16[1,256,256]{2,1,0:T(8,128)(2,1)S(1)}, u32[]{:S(2)}, u32[]{:S(2)}) collective-permute-start(bf16[1,256,256]{2,1,0:T(8,128)(2,1)S(1)} %slice.76), channel_id=1, source_target_pairs={{0,4},{4,8},{8,12},{12,16},{16,20},{20,24},{24,28},{28,0},{1,5},{5... | collective-permute-start | bytes 393224 | tf_op jit(solution)/shard_map/ppermute | solution.py:221
  182.8 24.3 %collective-permute-start.15 = (bf16[4,3,192,128]{3,2,1,0:T(8,128)(2,1)}, bf16[4,3,192,128]{3,2,1,0:T(8,128)(2,1)S(1)}, u32[]{:S(2)}, u32[]{:S(2)}) collective-permute-start(bf16[4,3,192,128]{3,2,1,0:T(8,128)(2,1)} %bitcast.8), channel_id=1, source_target_pairs={{0,2},{2,0},{1,3},{3,1},{4,6},{6,4},{5,7},{7,5},{8,10},{10,8},{9,1... | collective-permute-start | bytes 1769480 | tf_op jit(solution)/shard_map/ppermute | solution.py:217
  187.9 5.2 %collective-permute-start.18 = (bf16[1,256,256]{2,1,0:T(8,128)(2,1)S(1)}, bf16[1,256,256]{2,1,0:T(8,128)(2,1)S(1)}, u32[]{:S(2)}, u32[]{:S(2)}) collective-permute-start(bf16[1,256,256]{2,1,0:T(8,128)(2,1)S(1)} %slice.77), channel_id=1, source_target_pairs={{0,28},{4,0},{8,4},{12,8},{16,12},{20,16},{24,20},{28,24},{1,29},{... | collective-permute-start | bytes 393224 | tf_op jit(solution)/shard_map/ppermute | solution.py:221
  193.1 9.4 %collective-permute-start.19 = (bf16[1,512,256]{2,1,0:T(8,128)(2,1)S(1)}, bf16[1,512,256]{2,1,0:T(8,128)(2,1)S(1)}, u32[]{:S(2)}, u32[]{:S(2)}) collective-permute-start(bf16[1,512,256]{2,1,0:T(8,128)(2,1)S(1)} %constant_dynamic-update-slice_fusion.refs_10_), channel_id=1, source_target_pairs={{0,32},{32,1},{1,33},{33,0},{2,34},{34,3},{3,35},{35,2},{4,36},{36... | collective-permute-start | bytes 786440 | tf_op jit(solution)/shard_map/ppermute | solution.py:226
  193.9 8.7 %collective-permute-start.20 = (bf16[1,512,256]{2,1,0:T(8,128)(2,1)S(1)}, bf16[1,512,256]{2,1,0:T(8,128)(2,1)S(1)}, u32[]{:S(2)}, u32[]{:S(2)}) collective-permute-start(bf16[1,512,256]{2,1,0:T(8,128)(2,1)S(1)} %constant_dynamic-update-slice_fusion.refs_10_), channel_id=1, source_target_pairs={{0,33},{32,0},{1,32},{33,1},{2,35},{34,2},{3,34},{35,3},{4,37},{36... | collective-permute-start | bytes 786440 | tf_op jit(solution)/shard_map/ppermute | solution.py:226
  202.5 8.7 %collective-permute-start.21 = (bf16[1,256,256]{2,1,0:T(8,128)(2,1)S(1)}, bf16[1,256,256]{2,1,0:T(8,128)(2,1)S(1)}, u32[]{:S(2)}, u32[]{:S(2)}) collective-permute-start(bf16[1,256,256]{2,1,0:T(8,128)(2,1)S(1)} %slice.78), channel_id=1, source_target_pairs={{0,32},{32,1},{1,33},{33,0},{2,34},{34,3},{3,35},{35,2},{4,36},{36... | collective-permute-start | bytes 393224 | tf_op jit(solution)/shard_map/ppermute | solution.py:226
  202.6 8.5 %collective-permute-start.22 = (bf16[1,256,256]{2,1,0:T(8,128)(2,1)S(1)}, bf16[1,256,256]{2,1,0:T(8,128)(2,1)S(1)}, u32[]{:S(2)}, u32[]{:S(2)}) collective-permute-start(bf16[1,256,256]{2,1,0:T(8,128)(2,1)S(1)} %slice.79), channel_id=1, source_target_pairs={{0,33},{32,0},{1,32},{33,1},{2,35},{34,2},{3,34},{35,3},{4,37},{36... | collective-permute-start | bytes 393224 | tf_op jit(solution)/shard_map/ppermute | solution.py:226
  224.6 22.1 %all-to-all-start.2 = ((bf16[32,2,4,512]{3,2,1,0:T(4,128)(2,1)}), bf16[32,2,4,512]{3,2,1,0:T(4,128)(2,1)S(1)}, u32[]{:S(2)}, u32[]{:S(2)}) async-start(bf16[32,2,4,512]{3,2,1,0:T(4,128)(2,1)} %broadcast_in_dim.22), calls=%async_computation.2 | async-start | bytes 524288 | tf_op jit(solution)/shard_map/all_to_all | solution.py:213
  253.8 3.4 %collective-permute-start.23 = (bf16[512,256]{1,0:T(8,128)(2,1)S(1)}, bf16[512,256]{1,0:T(8,128)(2,1)S(1)}, u32[]{:S(2)}, u32[]{:S(2)}) collective-permute-start(bf16[512,256]{1,0:T(8,128)(2,1)S(1)} %slice_bitcast_fusion), channel_id=1, source_target_pairs={{0,2},{2,0},{1,3},{3,1},{4,6},{6,4},{5,7},{7,5},{8,10},{10,8},{9,1... | collective-permute-start | bytes 786440 | tf_op jit(solution)/shard_map/ppermute | solution.py:217
  (13 other events, 206.3 us)

commit v6 on v2

v6 whole, which is shorter than its diff:
```python
import jax
import jax.numpy as jnp
from jax import lax
from jax.experimental import pallas as pl
from jax.experimental.pallas import tpu as pltpu
from jax.sharding import Mesh, PartitionSpec as P

TILE = 128
GRP = 4
YL, ZN, CORES, YH = 2, 8, 2, 2
AXES = ("grp", "ylo", "z", "core", "yhi")
PLANE = ("ylo", "z", "core", "yhi")
CHIPS = ("ylo", "z", "yhi")
SHARES = YL * ZN * CORES * YH
f32 = jnp.float32
bf16 = jnp.bfloat16

adapter_scale = 0.5

SLOT = 8
STEPS = 4


def shrink_kernel(tile_seg, tokens, columns, out, total):
    step = pl.program_id(0)
    part = lax.dot_general(
        columns[...], tokens[...], (((1,), (1,)), ((), ())), preferred_element_type=f32
    )

    @pl.when(step == 0)
    def _():
        total[...] = part

    @pl.when(step > 0)
    def _():
        total[...] += part

    @pl.when(step == pl.num_programs(0) - 1)
    def _():
        per = columns.shape[0] // CORES
        for c in range(CORES):
            for i in range(out.shape[2] // TILE):
                seg = tile_seg[i]
                at = slice(i * TILE, (i + 1) * TILE)
                pick = total[c * per : c * per + SLOT, at]
                for j in range(1, per // SLOT):
                    low = c * per + j * SLOT
                    pick = jnp.where(seg == j, total[low : low + SLOT, at], pick)
                out[c, :, at] = pick


def shrink(tokens, columns, tile_seg):
    count, width = tokens.shape
    slots = columns.shape[0]
    part = width // STEPS
    return pl.pallas_call(
        shrink_kernel,
        out_shape=jax.ShapeDtypeStruct((CORES, SLOT, count), f32),
        grid_spec=pltpu.PrefetchScalarGridSpec(
            num_scalar_prefetch=1,
            grid=(STEPS,),
            in_specs=[
                pl.BlockSpec((count, part), lambda k, seg: (0, k)),
                pl.BlockSpec((slots, part), lambda k, seg: (0, k)),
            ],
            out_specs=pl.BlockSpec((CORES, SLOT, count), lambda k, seg: (0, 0, 0)),
            scratch_shapes=[pltpu.VMEM((slots, count), f32)],
        ),
        compiler_params=pltpu.CompilerParams(
            dimension_semantics=("arbitrary",), vmem_limit_bytes=56 << 20
        ),
        name="shrink",
    )(tile_seg, tokens, columns)


def frozen_kernel(tokens, own, other, out):
    step = pl.program_id(0)
    for which, weight in enumerate((own, other)):
        part = jnp.dot(tokens[...], weight[...], preferred_element_type=f32)

        @pl.when(step == 0)
        def _():
            out[which] = part

        @pl.when(step > 0)
        def _():
            out[which] += part


def frozen_matmul(tokens, own, other):
    count, width = tokens.shape
    wide = own.shape[1]
    part = width // STEPS
    shape = (CORES, count, wide)
    weight = pl.BlockSpec((part, wide), lambda k: (k, 0))
    return pl.pallas_call(
        frozen_kernel,
        out_shape=jax.ShapeDtypeStruct(shape, f32),
        grid=(STEPS,),
        in_specs=[pl.BlockSpec((count, part), lambda k: (0, k)), weight, weight],
        out_specs=pl.BlockSpec(shape, lambda k: (0, 0, 0)),
        compiler_params=pltpu.CompilerParams(
            dimension_semantics=("arbitrary",), vmem_limit_bytes=56 << 20
        ),
        name="frozen",
    )(tokens, own, other)


def adapt_kernel(tile_seg, frozen, shrunk, own, other, out):
    parts, _, rank, _ = own.shape
    hidden = out.shape[2]
    low = lax.broadcasted_iota(jnp.int32, (TILE, rank), 1) < rank // 2
    seg = tile_seg[pl.program_id(0)]
    left = shrunk[...].astype(f32)
    gate_left = left[:rank].T.astype(bf16)
    up_left = left[rank:].T.astype(bf16)
    for which, factors in enumerate((own, other)):
        wide = jnp.concatenate([factors[m, seg] for m in range(parts)], axis=1)
        for_gate = jnp.dot(gate_left, wide, preferred_element_type=f32)
        for_up = jnp.dot(up_left, wide, preferred_element_type=f32)
        for a in range(parts // 2):
            even = slice(2 * a * rank, (2 * a + 1) * rank)
            odd = slice((2 * a + 1) * rank, (2 * a + 2) * rank)
            at = slice(a * rank, (a + 1) * rank)
            gate = jnp.where(low, for_gate[:, even], pltpu.roll(for_gate[:, odd], rank // 2, 1))
            up = jnp.where(low, pltpu.roll(for_up[:, even], rank // 2, 1), for_up[:, odd])
            gate = frozen[which, :, at] + adapter_scale * gate
            up = frozen[which, :, hidden + a * rank : hidden + (a + 1) * rank] + adapter_scale * up
            out[which, :, at] = (gate / (1.0 + jnp.exp(-gate)) * up).astype(bf16)


def adapt(frozen, shrunk, own, other, tile_seg):
    both, count, wide = frozen.shape
    whole = pl.BlockSpec(own.shape, lambda i, seg: (0, 0, 0, 0))
    return pl.pallas_call(
        adapt_kernel,
        out_shape=jax.ShapeDtypeStruct((both, count, wide // 2), bf16),
        grid_spec=pltpu.PrefetchScalarGridSpec(
            num_scalar_prefetch=1,
            grid=(count // TILE,),
            in_specs=[
                pl.BlockSpec((both, TILE, wide), lambda i, seg: (0, i, 0)),
                pl.BlockSpec((shrunk.shape[0], TILE), lambda i, seg: (0, i)),
                whole,
                whole,
            ],
            out_specs=pl.BlockSpec((both, TILE, wide // 2), lambda i, seg: (0, i, 0)),
        ),
        compiler_params=pltpu.CompilerParams(
            dimension_semantics=("arbitrary",), vmem_limit_bytes=56 << 20
        ),
        name="adapt",
    )(tile_seg, frozen, shrunk, own, other)


def exchange(x, axes):
    return lax.all_to_all(x, axes, split_axis=0, concat_axis=0, tiled=True)


def swap(x):
    return lax.ppermute(x, "core", [(0, 1), (1, 0)])


def per_device(
    tokens,
    gate_up_weight,
    down_factor_pool,
    up_factor_pool,
    segment_adapters,
    segment_tile_counts,
    adapter_pool_rows,
):
    core = lax.axis_index("core")
    first = core == 0
    token_count, share = tokens.shape
    tile_count = token_count // TILE
    width = gate_up_weight.shape[0]
    wide = 2 * gate_up_weight.shape[2]
    twice_rank = down_factor_pool.shape[2]
    rank = twice_rank // 2
    segs = segment_adapters.shape[1]
    rows = token_count // CORES

    kept = lax.dynamic_slice_in_dim(tokens, core * rows, rows, axis=0)
    given = swap(lax.dynamic_slice_in_dim(tokens, (1 - core) * rows, rows, axis=0))
    start = jnp.concatenate(
        [jnp.where(first, kept, given), jnp.where(first, given, kept)], axis=1
    )
    down_pool, start = lax.optimization_barrier((down_factor_pool[0], start))
    gathered = lax.all_gather(start, ("yhi", "ylo", "z"), axis=1, tiled=True)

    cols = twice_rank // SHARES
    depth = rank + share // 2
    down_pool = down_pool.T.reshape(SHARES, cols, -1, share)
    down_pool = jnp.transpose(down_pool, (0, 2, 1, 3)).reshape(SHARES, depth - rank, share)
    pool = jnp.concatenate([up_factor_pool.reshape(SHARES, rank, rank), down_pool], axis=1)
    pool = exchange(pool, PLANE)

    w = gate_up_weight.reshape(YL * ZN * CORES, YH, share, wide)
    own_weight = jnp.transpose(w, (1, 0, 2, 3)).reshape(width, wide)
    pool, own_weight = lax.optimization_barrier((pool, own_weight))
    other_weight = swap(own_weight)

    chosen_rows = jnp.take(adapter_pool_rows, segment_adapters.reshape(-1), mode="clip")
    chosen = exchange(jnp.take(pool, chosen_rows, axis=0, mode="clip"), "grp")
    chosen = chosen.reshape(GRP, segs, depth, share)
    other_chosen = swap(chosen)
    columns = []
    for part in (jnp.where(first, chosen, other_chosen), jnp.where(first, other_chosen, chosen)):
        part = part[:, :, rank:].reshape(YL, GRP // YL, segs, -1, CORES, YH, cols, share)
        part = jnp.transpose(part, (2, 6, 5, 0, 1, 3, 4, 7)).reshape(segs, cols, width)
        columns.append(jnp.pad(part, ((0, 1), (0, SLOT - cols), (0, 0))).reshape(-1, width))
    columns = jnp.concatenate(columns)
    own_factors, other_factors = chosen[:, :, :rank], other_chosen[:, :, :rank]

    bounds = jnp.cumsum(segment_tile_counts[0])
    positions = jnp.arange(tile_count, dtype=jnp.int32)
    tile_seg = jnp.sum((bounds[None, :] <= positions[:, None]).astype(jnp.int32), axis=1)
    tile_seg = lax.dynamic_slice_in_dim(tile_seg, core * (tile_count // CORES), tile_count // CORES)

    columns, own_factors, other_factors, other_weight = lax.optimization_barrier(
        (columns, own_factors, other_factors, other_weight)
    )

    own_columns = shrink(gathered, columns, tile_seg)[:, :cols].astype(bf16)
    chips = SHARES // CORES
    shrunk = exchange(jnp.broadcast_to(own_columns[None], (chips, CORES, cols, rows)), CHIPS)
    shrunk = jnp.transpose(shrunk.reshape(YL * ZN, YH, CORES, cols, rows), (0, 2, 1, 3, 4))
    shrunk = shrunk.reshape(twice_rank, rows)

    frozen = frozen_matmul(gathered, own_weight, other_weight)
    hidden = adapt(frozen, shrunk, own_factors, other_factors, tile_seg)

    other_rows = swap(hidden[1])
    return jnp.concatenate(
        [jnp.where(first, hidden[0], other_rows), jnp.where(first, other_rows, hidden[0])]
    )


def solution(mesh):
    fine = Mesh(mesh.devices.reshape(GRP, YL, ZN, CORES, YH), AXES)
    return jax.shard_map(
        per_device,
        mesh=fine,
        in_specs=(
            P("grp", PLANE),
            P(None, None, PLANE),
            P(PLANE, "grp", None),
            P(PLANE, "grp", None, None, None),
            P(),
            P("grp", None),
            P(),
        ),
        out_specs=P("grp", PLANE),
        check_vma=False,
    )
```

time: 216 us -> 207 us (0.958)
  blocking collectives: 45.1 us -> 13.5 us
  Pallas kernels: 0 us -> 27.3 us
  matrix products: 26.8 us -> 0 us
  waiting for transfers between devices: 69.3 us -> 84.7 us
  other arithmetic: 2.45 us -> 6.92 us
    all_to_all x1, blocking collectives: 45.1 us -> 13.5 us  [exchange(): return lax.all_to_all(x, axes, split_axis=0, concat_axis=0, tiled=True)]
    pallas_call x0 -> x3, Pallas kernels: none -> 27.3 us  [the longest x1 15.1 us: frozen_matmul(): pl.pallas_call(frozen_kernel, out_shape=jax.ShapeDtypeStruct(shape, f32),...]
    dot_general x4 -> x0, matrix products: 26.8 us -> none  [the longest x1 16 us: per_device(): frozen = jnp.dot(gathered, w, preferred_element_type=f32)]
    all_gather x1, waiting for transfers between devices: 0.02 us -> 19.8 us  [per_device(): gathered = lax.all_gather(start, ('yhi', 'ylo', 'z'), axis=1, tiled=True)]
    ppermute x0 -> x4, starting transfers between devices: none -> 8.87 us  [swap(): return lax.ppermute(x, 'core', [(0, 1), (1, 0)])]
    reshape x4 -> x9, local copies, waits for them, and re-layouts: 14.9 us -> 23.8 us  [the longest x2 21.7 us: per_device(): w = gate_up_weight.reshape(YL * ZN * CORES, YH, share, wide)]
    all_to_all x4 -> x2, starting transfers between devices: 24.9 us -> 17 us  [exchange(): return lax.all_to_all(x, axes, split_axis=0, concat_axis=0, tiled=True)]
    transpose x4 -> x3, local copies, waits for them, and re-layouts: 9.63 us -> 2.27 us  [the longest x1 1.49 us: per_device(): down_pool = down_pool.T.reshape(SHARES, cols, -1, share)]
  transfers between devices with their start and end apart: 5 -> 7, of which waited for: 3 -> 4; matrix products, arithmetic and copies ran while one was open for 21% -> 16% of each run, Pallas kernels for 0% -> 7%
where the time goes in v6:
time: 207 us; the launch traced here: 206 us
  waiting for transfers between devices  84.7 us (41%)
  local copies, waits for them, and re-layouts  34.2 us (17%)
  Pallas kernels  27.3 us (13%)
  starting transfers between devices  25.8 us (12%)
  blocking collectives  13.5 us (7%)
  between operations  13.5 us (7%)
  other arithmetic  6.92 us (3%)
    all_to_all x2, waiting for transfers between devices, exchange(): return lax.all_to_all(x, axes, split_axis=0, concat_axis=0, tiled=True)  62.7 us
    reshape x2, local copies, waits for them, and re-layouts, per_device(): w = gate_up_weight.reshape(YL * ZN * CORES, YH, share, wide)  21.7 us
    all_gather x1, waiting for transfers between devices, per_device(): gathered = lax.all_gather(start, ('yhi', 'ylo', 'z'), axis=1, tiled=True)  19.8 us
    all_to_all x2, starting transfers between devices, exchange(): return lax.all_to_all(x, axes, split_axis=0, concat_axis=0, tiled=True)  17 us
    pallas_call x1, Pallas kernels, frozen_matmul(): pl.pallas_call(frozen_kernel, out_shape=jax.ShapeDtypeStruct(shape, f32),...  15.1 us
    all_to_all x1, blocking collectives, exchange(): return lax.all_to_all(x, axes, split_axis=0, concat_axis=0, tiled=True)  13.5 us
    ppermute x4, starting transfers between devices, swap(): return lax.ppermute(x, 'core', [(0, 1), (1, 0)])  8.87 us
    pallas_call x1, Pallas kernels, shrink(): pl.pallas_call(shrink_kernel, out_shape=jax.ShapeDtypeStruct((CORES, SLOT...  6.99 us
  transfers between devices with their start and end apart: 7, of which 4 were waited for; matrix products, arithmetic and copies ran while one was open for 16% of the time, Pallas kernels for 7%

profile of v6, /device:TPU:1, one launch (start us, length us, event | category | flops | bytes accessed | tf_op | source)
XLA Modules:
  0.0 206.0 jit_solution(14113695219404548366)
XLA Ops:
  6.5 0.9 constant_dynamic-slice_fusion
  7.5 3.3 %collective-permute-start = (bf16[512,128]{1,0:T(8,128)(2,1)S(1)}, bf16[512,128]{1,0:T(8,128)(2,1)S(1)}, u32[]{:S(2)}, u32[]{:S(2)}) collective-permute-start(bf16[512,128]{1,0:T(8,128)(2,1)S(1)} %constant_dynamic-slice_fusion), channel_id=1, source_target_pairs={{0,2},{2,0},{1,3},{3,1},{4,6},{6,4},{5,7},{7,5},{8,10},{10,8},{9,1... | collective-permute-start | bytes 393224 | tf_op jit(solution)/shard_map/ppermute | solution.py:161
  10.8 1.0 collective-permute-done
  11.8 1.0 broadcast_select_fusion.5
  12.8 0.7 pad_maximum_fusion.3
  13.5 1.5 copy.22
  15.3 0.7 copy.23
  15.9 0.7 copy.24
  16.6 1.9 pad_maximum_fusion
  18.6 10.3 %all-to-all-start = ((bf16[64,192,128]{2,1,0:T(8,128)(2,1)}), bf16[64,192,128]{2,1,0:T(8,128)(2,1)S(1)}, u32[]{:S(2)}, u32[]{:S(2)}) async-start(bf16[64,192,128]{2,1,0:T(8,128)(2,1)} %pad_maximum_fusion), calls=%async_computation | async-start | bytes 6291456 | tf_op jit(solution)/shard_map/all_to_all | solution.py:157
  28.8 14.1 %reshape.74 = bf16[32,2,128,512]{3,2,1,0:T(8,128)(2,1)} reshape(bf16[8192,2,256]{2,1,0:T(2,128)(2,1)} %param.8) | data formatting | bytes 16777216 | tf_op jit(solution)/shard_map/reshape | solution.py:199
  42.9 7.7 %copy.25 = bf16[32,2,128,512]{3,2,0,1:T(8,128)(2,1)} copy(bf16[32,2,128,512]{3,2,1,0:T(8,128)(2,1)} %reshape.74) | data formatting | bytes 16777216 | tf_op jit(solution)/shard_map/reshape | solution.py:199
  50.6 62.7 %all-to-all-done = bf16[64,192,128]{2,1,0:T(8,128)(2,1)S(1)} async-done(((bf16[64,192,128]{2,1,0:T(8,128)(2,1)}), bf16[64,192,128]{2,1,0:T(8,128)(2,1)S(1)}, u32[]{:S(2)}, u32[]{:S(2)}) %all-to-all-start) | async-done | bytes 3145760 | tf_op jit(solution)/shard_map/all_to_all | solution.py:157
  114.1 1.5 gather_fusion.1
  115.6 13.5 %all_to_all.15 = bf16[12,192,128]{2,1,0:T(8,128)(2,1)S(1)} all-to-all(bf16[12,192,128]{2,1,0:T(8,128)(2,1)} %gather_fusion.1), channel_id=1, replica_groups=mesh['grp'=4,'ylo'=2,'z'=8,'core'=2,'yhi'=2] {'grp'}, dimensions={0} | all-to-all | bytes 1179648 | tf_op jit(solution)/shard_map/all_to_all | solution.py:157
  129.1 1.7 collective-permute-start.1
  131.7 0.8 slice.38.own
  133.0 0.8 slice.39.other
  133.9 1.1 pad_maximum_fusion.1.columns
  135.0 19.8 %all-gather.2.cloned.1.call-done.tokens = bf16[512,8192]{1,0:T(8,128)(2,1)} async-done(((bf16[512,256]{1,0:T(8,128)(2,1)}), bf16[512,8192]{1,0:T(8,128)(2,1)}) %all-gather.2.cloned.1.call-update) | async-done | bytes 8388624 | tf_op jit(solution)/shard_map/all_gather | solution.py:190
  154.8 7.0 %shrink.1 = f32[2,8,512]{2,1,0:T(8,128)} custom-call(s32[4]{0:T(128)} %dynamic_slice.9.tile_seg, bf16[512,8192]{1,0:T(8,128)(2,1)} %all-gather.2.cloned.1.call-done.tokens, bf16[64,8192]{1,0:T(8,128)(2,1)} %pad_maximum_fusion.1.columns), custom_call_target="tpu_custom_call" | custom-call | tf_op jit(solution)/shard_map/shrink/pallas_call | solution.py:56
  161.8 0.8 slice.54
  162.6 0.8 broadcast_in_dim.18
  163.4 6.7 %all-to-all-start.2 = ((bf16[32,2,4,512]{3,2,1,0:T(4,128)(2,1)}), bf16[32,2,4,512]{3,2,1,0:T(4,128)(2,1)S(1)}, u32[]{:S(2)}, u32[]{:S(2)}) async-start(bf16[32,2,4,512]{3,2,1,0:T(4,128)(2,1)} %broadcast_in_dim.18), calls=%async_computation.2 | async-start | bytes 524288 | tf_op jit(solution)/shard_map/all_to_all | solution.py:157
  170.1 15.1 %frozen.1 = f32[2,512,512]{2,1,0:T(8,128)} custom-call(bf16[512,8192]{1,0:T(8,128)(2,1)} %all-gather.2.cloned.1.call-done.tokens, bf16[8192,512]{1,0:T(8,128)(2,1)} %bitcast.39, bf16[8192,512]{1,0:T(8,128)(2,1)} %collective-permute-done.2.other), custom_call_target="tpu_custom_call" | custom-call | tf_op jit(solution)/shard_map/frozen/pallas_call | solution.py:96
  185.3 0.8 reshape.84.shrunk
  186.0 5.2 %adapt.1 = bf16[2,512,256]{2,1,0:T(8,128)(2,1)} custom-call(s32[4]{0:T(128)} %dynamic_slice.9.tile_seg, f32[2,512,512]{2,1,0:T(8,128)} %frozen.1, bf16[256,512]{1,0:T(8,128)(2,1)} %reshape.84.shrunk, bf16[4,3,128,128]{3,2,1,0:T(8,128)(2,1)} %slice.38.own, bf16[4,3,128,128]{3,2,1,0:T(8,128)(2,1)} %slice.39.other), custom_call_target="tpu_custom_call" | custom-call | tf_op jit(solution)/shard_map/adapt/pallas_call | solution.py:135
  191.3 1.0 slice_bitcast_fusion
  192.2 3.9 %collective-permute-start.3 = (bf16[512,256]{1,0:T(8,128)(2,1)S(1)}, bf16[512,256]{1,0:T(8,128)(2,1)S(1)}, u32[]{:S(2)}, u32[]{:S(2)}) collective-permute-start(bf16[512,256]{1,0:T(8,128)(2,1)S(1)} %slice_bitcast_fusion), channel_id=1, source_target_pairs={{0,2},{2,0},{1,3},{3,1},{4,6},{6,4},{5,7},{7,5},{8,10},{10,8},{9,1... | collective-permute-start | bytes 786440 | tf_op jit(solution)/shard_map/ppermute | solution.py:161
  196.1 1.2 collective-permute-done.3
  197.3 1.0 broadcast_select_fusion.1
  198.3 0.8 pad_maximum_fusion.2
  (31 shorter events, 2.6 us)
Async XLA Ops:
  6.5 106.9 %copy-start = (s32[64]{0:T(128)S(1)}, s32[64]{0:T(128)}, u32[]{:S(2)}) copy-start(s32[64]{0:T(128)} %param.13) | copy-start | bytes 772
  6.5 148.3 %all-gather.2.cloned.1.call-start = ((), (), s32[]{:S(2)}) async-start(), calls=%async_computation.3 | async-start | bytes 8650752 | tf_op jit(solution)/shard_map/all_gather | solution.py:190
  7.5 4.3 %collective-permute-start = (bf16[512,128]{1,0:T(8,128)(2,1)S(1)}, bf16[512,128]{1,0:T(8,128)(2,1)S(1)}, u32[]{:S(2)}, u32[]{:S(2)}) collective-permute-start(bf16[512,128]{1,0:T(8,128)(2,1)S(1)} %constant_dynamic-slice_fusion), channel_id=1, source_target_pairs={{0,2},{2,0},{1,3},{3,1},{4,6},{6,4},{5,7},{7,5},{8,10},{10,8},{9,1... | collective-permute-start | bytes 393224 | tf_op jit(solution)/shard_map/ppermute | solution.py:161
  15.0 1.6 copy-start.2
  18.6 94.7 %all-to-all-start = ((bf16[64,192,128]{2,1,0:T(8,128)(2,1)}), bf16[64,192,128]{2,1,0:T(8,128)(2,1)S(1)}, u32[]{:S(2)}, u32[]{:S(2)}) async-start(bf16[64,192,128]{2,1,0:T(8,128)(2,1)} %pad_maximum_fusion), calls=%async_computation | async-start | bytes 6291456 | tf_op jit(solution)/shard_map/all_to_all | solution.py:157
  42.9 70.4 %copy-start.3 = (s32[4,3]{1,0:T(4,128)S(1)}, s32[4,3]{1,0:T(4,128)}, u32[]{:S(2)}) copy-start(s32[4,3]{1,0:T(4,128)} %param.11) | copy-start | bytes 148
  42.9 87.9 %copy-start.4 = (s32[1,3]{1,0:T(1,128)S(1)}, s32[1,3]{1,0:T(1,128)}, u32[]{:S(2)}) copy-start(s32[1,3]{1,0:T(1,128)} %param.12) | copy-start | bytes 40
  113.3 21.7 %collective-permute-start.2 = (bf16[8192,512]{1,0:T(8,128)(2,1)}, bf16[8192,512]{1,0:T(8,128)(2,1)}, u32[]{:S(2)}, u32[]{:S(2)}) collective-permute-start(bf16[8192,512]{1,0:T(8,128)(2,1)} %bitcast.38), channel_id=1, source_target_pairs={{0,2},{2,0},{1,3},{3,1},{4,6},{6,4},{5,7},{7,5},{8,10},{10,8},{9,1... | collective-permute-start | bytes 25165832 | tf_op jit(solution)/shard_map/ppermute | solution.py:161
  129.1 3.4 %collective-permute-start.1 = (bf16[4,3,192,128]{3,2,1,0:T(8,128)(2,1)S(1)}, bf16[4,3,192,128]{3,2,1,0:T(8,128)(2,1)S(1)}, u32[]{:S(2)}, u32[]{:S(2)}) collective-permute-start(bf16[4,3,192,128]{3,2,1,0:T(8,128)(2,1)S(1)} %bitcast.43), channel_id=1, source_target_pairs={{0,2},{2,0},{1,3},{3,1},{4,6},{6,4},{5,7},{7,5},{8,10},{10,8},{9,1... | collective-permute-start | bytes 1769480 | tf_op jit(solution)/shard_map/ppermute | solution.py:161
  163.4 21.8 %all-to-all-start.2 = ((bf16[32,2,4,512]{3,2,1,0:T(4,128)(2,1)}), bf16[32,2,4,512]{3,2,1,0:T(4,128)(2,1)S(1)}, u32[]{:S(2)}, u32[]{:S(2)}) async-start(bf16[32,2,4,512]{3,2,1,0:T(4,128)(2,1)} %broadcast_in_dim.18), calls=%async_computation.2 | async-start | bytes 524288 | tf_op jit(solution)/shard_map/all_to_all | solution.py:157
  185.3 13.8 %copy-start.1 = (s32[64]{0:T(128)S(1)}, s32[64]{0:T(128)}, u32[]{:S(2)}) copy-start(s32[64]{0:T(128)} %param.13) | copy-start | bytes 772
  192.2 5.0 %collective-permute-start.3 = (bf16[512,256]{1,0:T(8,128)(2,1)S(1)}, bf16[512,256]{1,0:T(8,128)(2,1)S(1)}, u32[]{:S(2)}, u32[]{:S(2)}) collective-permute-start(bf16[512,256]{1,0:T(8,128)(2,1)S(1)} %slice_bitcast_fusion), channel_id=1, source_target_pairs={{0,2},{2,0},{1,3},{3,1},{4,6},{6,4},{5,7},{7,5},{8,10},{10,8},{9,1... | collective-permute-start | bytes 786440 | tf_op jit(solution)/shard_map/ppermute | solution.py:161
Sparse Core Ops, SparseCore 0:
  13.6 141.1 all-gather.1

commit v7 on v6

--- a/solution.py
+++ b/solution.py
@@ -23,8 +23,9 @@
 
 def shrink_kernel(tile_seg, tokens, columns, out, total):
     step = pl.program_id(0)
+    block = jnp.concatenate([tokens[i] for i in range(tokens.shape[0])], axis=1)
     part = lax.dot_general(
-        columns[...], tokens[...], (((1,), (1,)), ((), ())), preferred_element_type=f32
+        columns[...], block, (((1,), (1,)), ((), ())), preferred_element_type=f32
     )
 
     @pl.when(step == 0)
@@ -50,8 +51,8 @@
 
 
 def shrink(tokens, columns, tile_seg):
-    count, width = tokens.shape
-    slots = columns.shape[0]
+    chips, count, both = tokens.shape
+    slots, width = columns.shape
     part = width // STEPS
     return pl.pallas_call(
         shrink_kernel,
@@ -60,7 +61,7 @@
             num_scalar_prefetch=1,
             grid=(STEPS,),
             in_specs=[
-                pl.BlockSpec((count, part), lambda k, seg: (0, k)),
+                pl.BlockSpec((chips // STEPS, count, both), lambda k, seg: (k, 0, 0)),
                 pl.BlockSpec((slots, part), lambda k, seg: (0, k)),
             ],
             out_specs=pl.BlockSpec((CORES, SLOT, count), lambda k, seg: (0, 0, 0)),
@@ -75,8 +76,9 @@
 
 def frozen_kernel(tokens, own, other, out):
     step = pl.program_id(0)
+    block = jnp.concatenate([tokens[i] for i in range(tokens.shape[0])], axis=1)
     for which, weight in enumerate((own, other)):
-        part = jnp.dot(tokens[...], weight[...], preferred_element_type=f32)
+        part = jnp.dot(block, weight[...], preferred_element_type=f32)
 
         @pl.when(step == 0)
         def _():
@@ -88,8 +90,8 @@
 
 
 def frozen_matmul(tokens, own, other):
-    count, width = tokens.shape
-    wide = own.shape[1]
+    chips, count, both = tokens.shape
+    width, wide = own.shape
     part = width // STEPS
     shape = (CORES, count, wide)
     weight = pl.BlockSpec((part, wide), lambda k: (k, 0))
@@ -97,7 +99,11 @@
         frozen_kernel,
         out_shape=jax.ShapeDtypeStruct(shape, f32),
         grid=(STEPS,),
-        in_specs=[pl.BlockSpec((count, part), lambda k: (0, k)), weight, weight],
+        in_specs=[
+            pl.BlockSpec((chips // STEPS, count, both), lambda k: (k, 0, 0)),
+            weight,
+            weight,
+        ],
         out_specs=pl.BlockSpec(shape, lambda k: (0, 0, 0)),
         compiler_params=pltpu.CompilerParams(
             dimension_semantics=("arbitrary",), vmem_limit_bytes=56 << 20
@@ -106,15 +112,15 @@
     )(tokens, own, other)
 
 
-def adapt_kernel(tile_seg, frozen, shrunk, own, other, out):
+def adapt_kernel(tile_seg, frozen, shrunk, own, other, own_out, other_out):
     parts, _, rank, _ = own.shape
-    hidden = out.shape[2]
+    hidden = own_out.shape[1]
     low = lax.broadcasted_iota(jnp.int32, (TILE, rank), 1) < rank // 2
     seg = tile_seg[pl.program_id(0)]
     left = shrunk[...].astype(f32)
     gate_left = left[:rank].T.astype(bf16)
     up_left = left[rank:].T.astype(bf16)
-    for which, factors in enumerate((own, other)):
+    for which, (factors, out) in enumerate(((own, own_out), (other, other_out))):
         wide = jnp.concatenate([factors[m, seg] for m in range(parts)], axis=1)
         for_gate = jnp.dot(gate_left, wide, preferred_element_type=f32)
         for_up = jnp.dot(up_left, wide, preferred_element_type=f32)
@@ -126,7 +132,7 @@
             up = jnp.where(low, pltpu.roll(for_up[:, even], rank // 2, 1), for_up[:, odd])
             gate = frozen[which, :, at] + adapter_scale * gate
             up = frozen[which, :, hidden + a * rank : hidden + (a + 1) * rank] + adapter_scale * up
-            out[which, :, at] = (gate / (1.0 + jnp.exp(-gate)) * up).astype(bf16)
+            out[:, at] = (gate / (1.0 + jnp.exp(-gate)) * up).astype(bf16)
 
 
 def adapt(frozen, shrunk, own, other, tile_seg):
@@ -134,7 +140,7 @@
     whole = pl.BlockSpec(own.shape, lambda i, seg: (0, 0, 0, 0))
     return pl.pallas_call(
         adapt_kernel,
-        out_shape=jax.ShapeDtypeStruct((both, count, wide // 2), bf16),
+        out_shape=[jax.ShapeDtypeStruct((count, wide // 2), bf16)] * both,
         grid_spec=pltpu.PrefetchScalarGridSpec(
             num_scalar_prefetch=1,
             grid=(count // TILE,),
@@ -144,7 +150,7 @@
                 whole,
                 whole,
             ],
-            out_specs=pl.BlockSpec((both, TILE, wide // 2), lambda i, seg: (0, i, 0)),
+            out_specs=[pl.BlockSpec((TILE, wide // 2), lambda i, seg: (i, 0))] * both,
         ),
         compiler_params=pltpu.CompilerParams(
             dimension_semantics=("arbitrary",), vmem_limit_bytes=56 << 20
@@ -187,7 +193,8 @@
         [jnp.where(first, kept, given), jnp.where(first, given, kept)], axis=1
     )
     down_pool, start = lax.optimization_barrier((down_factor_pool[0], start))
-    gathered = lax.all_gather(start, ("yhi", "ylo", "z"), axis=1, tiled=True)
+    gathered = lax.all_gather(start, ("yhi", "ylo", "z"))
+    gathered = gathered.reshape(SHARES // CORES, rows, CORES * share)
 
     cols = twice_rank // SHARES
     depth = rank + share // 2
@@ -229,12 +236,11 @@
     shrunk = shrunk.reshape(twice_rank, rows)
 
     frozen = frozen_matmul(gathered, own_weight, other_weight)
-    hidden = adapt(frozen, shrunk, own_factors, other_factors, tile_seg)
-
-    other_rows = swap(hidden[1])
-    return jnp.concatenate(
-        [jnp.where(first, hidden[0], other_rows), jnp.where(first, other_rows, hidden[0])]
-    )
+    own_rows, for_other = adapt(frozen, shrunk, own_factors, other_factors, tile_seg)
+
+    hidden = jnp.zeros((token_count, wide // 2), bf16)
+    hidden = lax.dynamic_update_slice_in_dim(hidden, own_rows, core * rows, axis=0)
+    return lax.dynamic_update_slice_in_dim(hidden, swap(for_other), (1 - core) * rows, axis=0)
 
 
 def solution(mesh):

time: 207 us -> 197 us (0.952)
  waiting for transfers between devices: 84.7 us -> 75.3 us
    all_gather x1, waiting for transfers between devices: 19.8 us -> 4.7 us  [per_device(): gathered = lax.all_gather(start, ('yhi', 'ylo', 'z'))]
    all_to_all x2, waiting for transfers between devices: 62.7 us -> 69.2 us  [exchange(): return lax.all_to_all(x, axes, split_axis=0, concat_axis=0, tiled=True)]
  transfers between devices with their start and end apart: 7 -> 7, of which waited for: 4 -> 4; matrix products, arithmetic and copies ran while one was open for 16% -> 17% of each run, Pallas kernels for 7% -> 8%
where the time goes in v7:
time: 197 us; the launch traced here: 196 us
  waiting for transfers between devices  75.3 us (38%)
  local copies, waits for them, and re-layouts  35.4 us (18%)
  Pallas kernels  27.2 us (14%)
  starting transfers between devices  25.8 us (13%)
  blocking collectives  13.7 us (7%)
  between operations  13.5 us (7%)
  other arithmetic  5.07 us (3%)
    all_to_all x2, waiting for transfers between devices, exchange(): return lax.all_to_all(x, axes, split_axis=0, concat_axis=0, tiled=True)  69.2 us
    reshape x2, local copies, waits for them, and re-layouts, per_device(): w = gate_up_weight.reshape(YL * ZN * CORES, YH, share, wide)  21.8 us
    all_to_all x2, starting transfers between devices, exchange(): return lax.all_to_all(x, axes, split_axis=0, concat_axis=0, tiled=True)  17.2 us
    pallas_call x1, Pallas kernels, frozen_matmul(): pl.pallas_call(frozen_kernel, out_shape=jax.ShapeDtypeStruct(shape, f32),...  15.1 us
    all_to_all x1, blocking collectives, exchange(): return lax.all_to_all(x, axes, split_axis=0, concat_axis=0, tiled=True)  13.7 us
    ppermute x4, starting transfers between devices, swap(): return lax.ppermute(x, 'core', [(0, 1), (1, 0)])  8.61 us
    pallas_call x1, Pallas kernels, shrink(): pl.pallas_call(shrink_kernel, out_shape=jax.ShapeDtypeStruct((CORES, SLOT...  6.96 us
    pallas_call x1, Pallas kernels, adapt(): pl.pallas_call(adapt_kernel, out_shape=[jax.ShapeDtypeStruct((count, wide...  5.16 us
  transfers between devices with their start and end apart: 7, of which 4 were waited for; matrix products, arithmetic and copies ran while one was open for 17% of the time, Pallas kernels for 8%

profile of v7, /device:TPU:1, one launch (start us, length us, event | category | flops | bytes accessed | tf_op | source)
XLA Modules:
  0.0 196.0 jit_solution(14675701453426470525)
XLA Ops:
  6.5 0.9 constant_dynamic-slice_fusion
  7.5 3.3 %collective-permute-start = (bf16[512,128]{1,0:T(8,128)(2,1)S(1)}, bf16[512,128]{1,0:T(8,128)(2,1)S(1)}, u32[]{:S(2)}, u32[]{:S(2)}) collective-permute-start(bf16[512,128]{1,0:T(8,128)(2,1)S(1)} %constant_dynamic-slice_fusion), channel_id=1, source_target_pairs={{0,2},{2,0},{1,3},{3,1},{4,6},{6,4},{5,7},{7,5},{8,10},{10,8},{9,1... | collective-permute-start | bytes 393224 | tf_op jit(solution)/shard_map/ppermute | solution.py:167
  10.8 1.0 collective-permute-done
  11.8 1.0 broadcast_select_fusion.3
  12.8 0.7 pad_maximum_fusion.2
  13.5 1.5 copy.22
  15.2 0.7 copy.23
  15.9 0.7 copy.24
  16.6 1.9 pad_maximum_fusion
  18.6 10.3 %all-to-all-start = ((bf16[64,192,128]{2,1,0:T(8,128)(2,1)}), bf16[64,192,128]{2,1,0:T(8,128)(2,1)S(1)}, u32[]{:S(2)}, u32[]{:S(2)}) async-start(bf16[64,192,128]{2,1,0:T(8,128)(2,1)} %pad_maximum_fusion), calls=%async_computation | async-start | bytes 6291456 | tf_op jit(solution)/shard_map/all_to_all | solution.py:163
  28.8 14.1 %reshape.74 = bf16[32,2,128,512]{3,2,1,0:T(8,128)(2,1)} reshape(bf16[8192,2,256]{2,1,0:T(2,128)(2,1)} %param.8) | data formatting | bytes 16777216 | tf_op jit(solution)/shard_map/reshape | solution.py:206
  42.9 7.7 %copy.25 = bf16[32,2,128,512]{3,2,0,1:T(8,128)(2,1)} copy(bf16[32,2,128,512]{3,2,1,0:T(8,128)(2,1)} %reshape.74) | data formatting | bytes 16777216 | tf_op jit(solution)/shard_map/reshape | solution.py:206
  50.6 69.2 %all-to-all-done = bf16[64,192,128]{2,1,0:T(8,128)(2,1)S(1)} async-done(((bf16[64,192,128]{2,1,0:T(8,128)(2,1)}), bf16[64,192,128]{2,1,0:T(8,128)(2,1)S(1)}, u32[]{:S(2)}, u32[]{:S(2)}) %all-to-all-start) | async-done | bytes 3145760 | tf_op jit(solution)/shard_map/all_to_all | solution.py:163
  119.9 3.2 %collective-permute-start.2 = (bf16[8192,512]{1,0:T(8,128)(2,1)}, bf16[8192,512]{1,0:T(8,128)(2,1)}, u32[]{:S(2)}, u32[]{:S(2)}) collective-permute-start(bf16[8192,512]{1,0:T(8,128)(2,1)} %bitcast.33), channel_id=1, source_target_pairs={{0,2},{2,0},{1,3},{3,1},{4,6},{6,4},{5,7},{7,5},{8,10},{10,8},{9,1... | collective-permute-start | bytes 25165832 | tf_op jit(solution)/shard_map/ppermute | solution.py:167
  123.1 0.7 gather_fusion
  123.8 1.5 gather_fusion.1
  125.3 13.7 %all_to_all.15 = bf16[12,192,128]{2,1,0:T(8,128)(2,1)S(1)} all-to-all(bf16[12,192,128]{2,1,0:T(8,128)(2,1)} %gather_fusion.1), channel_id=1, replica_groups=mesh['grp'=4,'ylo'=2,'z'=8,'core'=2,'yhi'=2] {'grp'}, dimensions={0} | all-to-all | bytes 1179648 | tf_op jit(solution)/shard_map/all_to_all | solution.py:163
  139.0 1.4 collective-permute-start.1
  141.3 0.8 slice.29.own
  142.5 0.8 slice.30.other
  143.5 1.1 pad_maximum_fusion.1.columns
  144.6 4.7 %all-gather.3.cloned.1.call-done = bf16[16384,256]{1,0:T(8,128)(2,1)} async-done(((bf16[512,256]{1,0:T(8,128)(2,1)}), bf16[16384,256]{1,0:T(8,128)(2,1)}) %all-gather.3.cloned.1.call-update) | async-done | bytes 8388624 | tf_op jit(solution)/shard_map/all_gather | solution.py:196
  149.3 7.0 %shrink.1 = f32[2,8,512]{2,1,0:T(8,128)} custom-call(s32[4]{0:T(128)} %dynamic_slice.9.tile_seg, bf16[32,512,256]{2,1,0:T(8,128)(2,1)} %bitcast.31, bf16[64,8192]{1,0:T(8,128)(2,1)} %pad_maximum_fusion.1.columns), custom_call_target="tpu_custom_call" | custom-call | tf_op jit(solution)/shard_map/shrink/pallas_call | solution.py:57
  156.3 0.8 slice.37
  157.1 0.8 broadcast_in_dim.22
  157.8 7.0 %all-to-all-start.2 = ((bf16[32,2,4,512]{3,2,1,0:T(4,128)(2,1)}), bf16[32,2,4,512]{3,2,1,0:T(4,128)(2,1)S(1)}, u32[]{:S(2)}, u32[]{:S(2)}) async-start(bf16[32,2,4,512]{3,2,1,0:T(4,128)(2,1)} %broadcast_in_dim.22), calls=%async_computation.2 | async-start | bytes 524288 | tf_op jit(solution)/shard_map/all_to_all | solution.py:163
  164.8 15.1 %frozen.1 = f32[2,512,512]{2,1,0:T(8,128)} custom-call(bf16[32,512,256]{2,1,0:T(8,128)(2,1)} %bitcast.32, bf16[8192,512]{1,0:T(8,128)(2,1)} %bitcast.34, bf16[8192,512]{1,0:T(8,128)(2,1)} %collective-permute-done.2.other), custom_call_target="tpu_custom_call" | custom-call | tf_op jit(solution)/shard_map/frozen/pallas_call | solution.py:98
  180.0 0.8 reshape.84.shrunk
  180.8 5.2 %adapt.1 = (bf16[512,256]{1,0:T(8,128)(2,1)}, bf16[512,256]{1,0:T(8,128)(2,1)}) custom-call(s32[4]{0:T(128)} %dynamic_slice.9.tile_seg, f32[2,512,512]{2,1,0:T(8,128)} %frozen.1, bf16[256,512]{1,0:T(8,128)(2,1)} %reshape.84.shrunk, bf16[4,3,128,128]{3,2,1,0:T(8,128)(2,1)} %slice.29.own, bf16[4,3,128,128]{3,2,1,0:T(8,128)(2,1)} %slice.30.other), custom_call_target="tpu_custom_call" | custom-call | tf_op jit(solution)/shard_map/adapt/pallas_call | solution.py:141
  185.9 0.7 collective-permute-start.3
  186.7 1.0 constant_dynamic-update-slice_fusion.1
  188.5 0.7 constant_dynamic-update-slice_fusion
  (31 shorter events, 2.8 us)
Async XLA Ops:
  6.5 116.6 %copy-start = (s32[64]{0:T(128)S(1)}, s32[64]{0:T(128)}, u32[]{:S(2)}) copy-start(s32[64]{0:T(128)} %param.13) | copy-start | bytes 772
  6.5 142.8 %all-gather.3.cloned.1.call-start = ((), (), s32[]{:S(2)}) async-start(), calls=%async_computation.3 | async-start | bytes 8650752 | tf_op jit(solution)/shard_map/all_gather | solution.py:196
  7.5 4.3 %collective-permute-start = (bf16[512,128]{1,0:T(8,128)(2,1)S(1)}, bf16[512,128]{1,0:T(8,128)(2,1)S(1)}, u32[]{:S(2)}, u32[]{:S(2)}) collective-permute-start(bf16[512,128]{1,0:T(8,128)(2,1)S(1)} %constant_dynamic-slice_fusion), channel_id=1, source_target_pairs={{0,2},{2,0},{1,3},{3,1},{4,6},{6,4},{5,7},{7,5},{8,10},{10,8},{9,1... | collective-permute-start | bytes 393224 | tf_op jit(solution)/shard_map/ppermute | solution.py:167
  15.0 1.6 copy-start.1
  18.6 101.3 %all-to-all-start = ((bf16[64,192,128]{2,1,0:T(8,128)(2,1)}), bf16[64,192,128]{2,1,0:T(8,128)(2,1)S(1)}, u32[]{:S(2)}, u32[]{:S(2)}) async-start(bf16[64,192,128]{2,1,0:T(8,128)(2,1)} %pad_maximum_fusion), calls=%async_computation | async-start | bytes 6291456 | tf_op jit(solution)/shard_map/all_to_all | solution.py:163
  42.9 80.1 %copy-start.3 = (s32[4,3]{1,0:T(4,128)S(1)}, s32[4,3]{1,0:T(4,128)}, u32[]{:S(2)}) copy-start(s32[4,3]{1,0:T(4,128)} %param.11) | copy-start | bytes 148
  42.9 97.5 %copy-start.4 = (s32[1,3]{1,0:T(1,128)S(1)}, s32[1,3]{1,0:T(1,128)}, u32[]{:S(2)}) copy-start(s32[1,3]{1,0:T(1,128)} %param.12) | copy-start | bytes 40
  119.9 24.8 %collective-permute-start.2 = (bf16[8192,512]{1,0:T(8,128)(2,1)}, bf16[8192,512]{1,0:T(8,128)(2,1)}, u32[]{:S(2)}, u32[]{:S(2)}) collective-permute-start(bf16[8192,512]{1,0:T(8,128)(2,1)} %bitcast.33), channel_id=1, source_target_pairs={{0,2},{2,0},{1,3},{3,1},{4,6},{6,4},{5,7},{7,5},{8,10},{10,8},{9,1... | collective-permute-start | bytes 25165832 | tf_op jit(solution)/shard_map/ppermute | solution.py:167
  139.0 3.0 %collective-permute-start.1 = (bf16[4,3,192,128]{3,2,1,0:T(8,128)(2,1)S(1)}, bf16[4,3,192,128]{3,2,1,0:T(8,128)(2,1)S(1)}, u32[]{:S(2)}, u32[]{:S(2)}) collective-permute-start(bf16[4,3,192,128]{3,2,1,0:T(8,128)(2,1)S(1)} %bitcast.38), channel_id=1, source_target_pairs={{0,2},{2,0},{1,3},{3,1},{4,6},{6,4},{5,7},{7,5},{8,10},{10,8},{9,1... | collective-permute-start | bytes 1769480 | tf_op jit(solution)/shard_map/ppermute | solution.py:167
  157.8 22.1 %all-to-all-start.2 = ((bf16[32,2,4,512]{3,2,1,0:T(4,128)(2,1)}), bf16[32,2,4,512]{3,2,1,0:T(4,128)(2,1)S(1)}, u32[]{:S(2)}, u32[]{:S(2)}) async-start(bf16[32,2,4,512]{3,2,1,0:T(4,128)(2,1)} %broadcast_in_dim.22), calls=%async_computation.2 | async-start | bytes 524288 | tf_op jit(solution)/shard_map/all_to_all | solution.py:163
  185.9 2.1 %collective-permute-start.3 = (bf16[512,256]{1,0:T(8,128)(2,1)}, bf16[512,256]{1,0:T(8,128)(2,1)S(1)}, u32[]{:S(2)}, u32[]{:S(2)}) collective-permute-start(bf16[512,256]{1,0:T(8,128)(2,1)} %get-tuple-element.24), channel_id=1, source_target_pairs={{0,2},{2,0},{1,3},{3,1},{4,6},{6,4},{5,7},{7,5},{8,10},{10,8},{9,1... | collective-permute-start | bytes 786440 | tf_op jit(solution)/shard_map/ppermute | solution.py:167
  187.7 0.8 copy-start.2
Sparse Core Ops, SparseCore 0:
  13.6 135.6 all-gather.2

commit v8 on v7

--- a/solution.py
+++ b/solution.py
@@ -19,6 +19,7 @@
 
 SLOT = 8
 STEPS = 4
+HALVES = 2
 
 
 def shrink_kernel(tile_seg, tokens, columns, out, total):
@@ -40,31 +41,33 @@
     def _():
         per = columns.shape[0] // CORES
         for c in range(CORES):
-            for i in range(out.shape[2] // TILE):
+            for i in range(out.shape[3] // TILE):
                 seg = tile_seg[i]
                 at = slice(i * TILE, (i + 1) * TILE)
                 pick = total[c * per : c * per + SLOT, at]
                 for j in range(1, per // SLOT):
                     low = c * per + j * SLOT
                     pick = jnp.where(seg == j, total[low : low + SLOT, at], pick)
-                out[c, :, at] = pick
-
-
-def shrink(tokens, columns, tile_seg):
+                pick = pick[: out.shape[2]].astype(bf16)
+                for chip in range(out.shape[0]):
+                    out[chip, c, :, at] = pick
+
+
+def shrink(tokens, columns, tile_seg, cols):
     chips, count, both = tokens.shape
     slots, width = columns.shape
-    part = width // STEPS
+    part = width // HALVES
     return pl.pallas_call(
         shrink_kernel,
-        out_shape=jax.ShapeDtypeStruct((CORES, SLOT, count), f32),
+        out_shape=jax.ShapeDtypeStruct((chips, CORES, cols, count), bf16),
         grid_spec=pltpu.PrefetchScalarGridSpec(
             num_scalar_prefetch=1,
-            grid=(STEPS,),
+            grid=(HALVES,),
             in_specs=[
-                pl.BlockSpec((chips // STEPS, count, both), lambda k, seg: (k, 0, 0)),
+                pl.BlockSpec((chips // HALVES, count, both), lambda k, seg: (k, 0, 0)),
                 pl.BlockSpec((slots, part), lambda k, seg: (0, k)),
             ],
-            out_specs=pl.BlockSpec((CORES, SLOT, count), lambda k, seg: (0, 0, 0)),
+            out_specs=pl.BlockSpec((chips, CORES, cols, count), lambda k, seg: (0, 0, 0, 0)),
             scratch_shapes=[pltpu.VMEM((slots, count), f32)],
         ),
         compiler_params=pltpu.CompilerParams(
@@ -115,42 +118,51 @@
 def adapt_kernel(tile_seg, frozen, shrunk, own, other, own_out, other_out):
     parts, _, rank, _ = own.shape
     hidden = own_out.shape[1]
+    tiles = own_out.shape[0] // TILE
     low = lax.broadcasted_iota(jnp.int32, (TILE, rank), 1) < rank // 2
-    seg = tile_seg[pl.program_id(0)]
-    left = shrunk[...].astype(f32)
-    gate_left = left[:rank].T.astype(bf16)
-    up_left = left[rank:].T.astype(bf16)
-    for which, (factors, out) in enumerate(((own, own_out), (other, other_out))):
-        wide = jnp.concatenate([factors[m, seg] for m in range(parts)], axis=1)
-        for_gate = jnp.dot(gate_left, wide, preferred_element_type=f32)
-        for_up = jnp.dot(up_left, wide, preferred_element_type=f32)
-        for a in range(parts // 2):
-            even = slice(2 * a * rank, (2 * a + 1) * rank)
-            odd = slice((2 * a + 1) * rank, (2 * a + 2) * rank)
-            at = slice(a * rank, (a + 1) * rank)
-            gate = jnp.where(low, for_gate[:, even], pltpu.roll(for_gate[:, odd], rank // 2, 1))
-            up = jnp.where(low, pltpu.roll(for_up[:, even], rank // 2, 1), for_up[:, odd])
-            gate = frozen[which, :, at] + adapter_scale * gate
-            up = frozen[which, :, hidden + a * rank : hidden + (a + 1) * rank] + adapter_scale * up
-            out[:, at] = (gate / (1.0 + jnp.exp(-gate)) * up).astype(bf16)
+    for t in range(tiles):
+        seg = tile_seg[pl.program_id(0) * tiles + t]
+        row = slice(t * TILE, (t + 1) * TILE)
+        left = shrunk[:, row].astype(f32)
+        gate_left = left[:rank].T.astype(bf16)
+        up_left = left[rank:].T.astype(bf16)
+        for which, (factors, out) in enumerate(((own, own_out), (other, other_out))):
+            wide = jnp.concatenate([factors[m, seg] for m in range(parts)], axis=1)
+            for_gate = jnp.dot(gate_left, wide, preferred_element_type=f32)
+            for_up = jnp.dot(up_left, wide, preferred_element_type=f32)
+            for a in range(parts // 2):
+                even = slice(2 * a * rank, (2 * a + 1) * rank)
+                odd = slice((2 * a + 1) * rank, (2 * a + 2) * rank)
+                at = slice(a * rank, (a + 1) * rank)
+                gate = jnp.where(
+                    low, for_gate[:, even], pltpu.roll(for_gate[:, odd], rank // 2, 1)
+                )
+                up = jnp.where(low, pltpu.roll(for_up[:, even], rank // 2, 1), for_up[:, odd])
+                gate = frozen[which, row, at] + adapter_scale * gate
+                up = (
+                    frozen[which, row, hidden + a * rank : hidden + (a + 1) * rank]
+                    + adapter_scale * up
+                )
+                out[row, at] = (gate / (1.0 + jnp.exp(-gate)) * up).astype(bf16)
 
 
 def adapt(frozen, shrunk, own, other, tile_seg):
     both, count, wide = frozen.shape
+    rows = count // HALVES
     whole = pl.BlockSpec(own.shape, lambda i, seg: (0, 0, 0, 0))
     return pl.pallas_call(
         adapt_kernel,
         out_shape=[jax.ShapeDtypeStruct((count, wide // 2), bf16)] * both,
         grid_spec=pltpu.PrefetchScalarGridSpec(
             num_scalar_prefetch=1,
-            grid=(count // TILE,),
+            grid=(HALVES,),
             in_specs=[
-                pl.BlockSpec((both, TILE, wide), lambda i, seg: (0, i, 0)),
-                pl.BlockSpec((shrunk.shape[0], TILE), lambda i, seg: (0, i)),
+                pl.BlockSpec((both, rows, wide), lambda i, seg: (0, i, 0)),
+                pl.BlockSpec((shrunk.shape[0], rows), lambda i, seg: (0, i)),
                 whole,
                 whole,
             ],
-            out_specs=[pl.BlockSpec((TILE, wide // 2), lambda i, seg: (i, 0))] * both,
+            out_specs=[pl.BlockSpec((rows, wide // 2), lambda i, seg: (i, 0))] * both,
         ),
         compiler_params=pltpu.CompilerParams(
             dimension_semantics=("arbitrary",), vmem_limit_bytes=56 << 20
@@ -229,9 +241,7 @@
         (columns, own_factors, other_factors, other_weight)
     )
 
-    own_columns = shrink(gathered, columns, tile_seg)[:, :cols].astype(bf16)
-    chips = SHARES // CORES
-    shrunk = exchange(jnp.broadcast_to(own_columns[None], (chips, CORES, cols, rows)), CHIPS)
+    shrunk = exchange(shrink(gathered, columns, tile_seg, cols), CHIPS)
     shrunk = jnp.transpose(shrunk.reshape(YL * ZN, YH, CORES, cols, rows), (0, 2, 1, 3, 4))
     shrunk = shrunk.reshape(twice_rank, rows)
 

time: 197 us -> 194 us (0.985)
  transfers between devices with their start and end apart: 7 -> 7, of which waited for: 4 -> 4; matrix products, arithmetic and copies ran while one was open for 17% -> 18% of each run, Pallas kernels for 8% -> 8%
where the time goes in v8:
time: 194 us; the launch traced here: 193 us
  waiting for transfers between devices  75.3 us (39%)
  local copies, waits for them, and re-layouts  33.8 us (17%)
  starting transfers between devices  25.8 us (13%)
  Pallas kernels  25.6 us (13%)
  blocking collectives  13.7 us (7%)
  between operations  13.5 us (7%)
  other arithmetic  5.07 us (3%)
    all_to_all x2, waiting for transfers between devices, exchange(): return lax.all_to_all(x, axes, split_axis=0, concat_axis=0, tiled=True)  69.2 us
    reshape x2, local copies, waits for them, and re-layouts, per_device(): w = gate_up_weight.reshape(YL * ZN * CORES, YH, share, wide)  21.8 us
    all_to_all x2, starting transfers between devices, exchange(): return lax.all_to_all(x, axes, split_axis=0, concat_axis=0, tiled=True)  17.2 us
    pallas_call x1, Pallas kernels, frozen_matmul(): pl.pallas_call(frozen_kernel, out_shape=jax.ShapeDtypeStruct(shape, f32),...  15.1 us
    all_to_all x1, blocking collectives, exchange(): return lax.all_to_all(x, axes, split_axis=0, concat_axis=0, tiled=True)  13.7 us
    ppermute x4, starting transfers between devices, swap(): return lax.ppermute(x, 'core', [(0, 1), (1, 0)])  8.61 us
    pallas_call x1, Pallas kernels, shrink(): pl.pallas_call(shrink_kernel, out_shape=jax.ShapeDtypeStruct((chips, CORE...  6.55 us
    all_gather x1, waiting for transfers between devices, per_device(): gathered = lax.all_gather(start, ('yhi', 'ylo', 'z'))  4.7 us
  transfers between devices with their start and end apart: 7, of which 4 were waited for; matrix products, arithmetic and copies ran while one was open for 18% of the time, Pallas kernels for 8%

profile of v8, /device:TPU:1, one launch (start us, length us, event | category | flops | bytes accessed | tf_op | source)
XLA Modules:
  0.0 192.9 jit_solution(18048194814174697937)
XLA Ops:
  6.5 0.9 constant_dynamic-slice_fusion
  7.5 3.3 %collective-permute-start = (bf16[512,128]{1,0:T(8,128)(2,1)S(1)}, bf16[512,128]{1,0:T(8,128)(2,1)S(1)}, u32[]{:S(2)}, u32[]{:S(2)}) collective-permute-start(bf16[512,128]{1,0:T(8,128)(2,1)S(1)} %constant_dynamic-slice_fusion), channel_id=1, source_target_pairs={{0,2},{2,0},{1,3},{3,1},{4,6},{6,4},{5,7},{7,5},{8,10},{10,8},{9,1... | collective-permute-start | bytes 393224 | tf_op jit(solution)/shard_map/ppermute | solution.py:179
  10.8 1.0 collective-permute-done
  11.8 1.0 broadcast_select_fusion.3
  12.8 0.7 pad_maximum_fusion.2
  13.5 1.5 copy.23
  15.2 0.7 copy.24
  15.9 0.7 copy.25
  16.6 1.9 pad_maximum_fusion
  18.6 10.3 %all-to-all-start = ((bf16[64,192,128]{2,1,0:T(8,128)(2,1)}), bf16[64,192,128]{2,1,0:T(8,128)(2,1)S(1)}, u32[]{:S(2)}, u32[]{:S(2)}) async-start(bf16[64,192,128]{2,1,0:T(8,128)(2,1)} %pad_maximum_fusion), calls=%async_computation | async-start | bytes 6291456 | tf_op jit(solution)/shard_map/all_to_all | solution.py:175
  28.8 14.1 %reshape.73 = bf16[32,2,128,512]{3,2,1,0:T(8,128)(2,1)} reshape(bf16[8192,2,256]{2,1,0:T(2,128)(2,1)} %param.8) | data formatting | bytes 16777216 | tf_op jit(solution)/shard_map/reshape | solution.py:218
  42.9 7.7 %copy.26 = bf16[32,2,128,512]{3,2,0,1:T(8,128)(2,1)} copy(bf16[32,2,128,512]{3,2,1,0:T(8,128)(2,1)} %reshape.73) | data formatting | bytes 16777216 | tf_op jit(solution)/shard_map/reshape | solution.py:218
  50.6 69.2 %all-to-all-done = bf16[64,192,128]{2,1,0:T(8,128)(2,1)S(1)} async-done(((bf16[64,192,128]{2,1,0:T(8,128)(2,1)}), bf16[64,192,128]{2,1,0:T(8,128)(2,1)S(1)}, u32[]{:S(2)}, u32[]{:S(2)}) %all-to-all-start) | async-done | bytes 3145760 | tf_op jit(solution)/shard_map/all_to_all | solution.py:175
  119.9 3.2 %collective-permute-start.2 = (bf16[8192,512]{1,0:T(8,128)(2,1)}, bf16[8192,512]{1,0:T(8,128)(2,1)}, u32[]{:S(2)}, u32[]{:S(2)}) collective-permute-start(bf16[8192,512]{1,0:T(8,128)(2,1)} %bitcast.34), channel_id=1, source_target_pairs={{0,2},{2,0},{1,3},{3,1},{4,6},{6,4},{5,7},{7,5},{8,10},{10,8},{9,1... | collective-permute-start | bytes 25165832 | tf_op jit(solution)/shard_map/ppermute | solution.py:179
  123.1 0.7 gather_fusion
  123.8 1.5 gather_fusion.1
  125.3 13.7 %all_to_all.15 = bf16[12,192,128]{2,1,0:T(8,128)(2,1)S(1)} all-to-all(bf16[12,192,128]{2,1,0:T(8,128)(2,1)} %gather_fusion.1), channel_id=1, replica_groups=mesh['grp'=4,'ylo'=2,'z'=8,'core'=2,'yhi'=2] {'grp'}, dimensions={0} | all-to-all | bytes 1179648 | tf_op jit(solution)/shard_map/all_to_all | solution.py:175
  139.0 1.4 collective-permute-start.1
  140.7 0.6 dynamic_slice.9.tile_seg
  141.3 0.8 slice.24.own
  142.5 0.8 slice.25.other
  143.5 1.1 pad_maximum_fusion.1.columns
  144.6 4.7 %all-gather.3.cloned.1.call-done = bf16[16384,256]{1,0:T(8,128)(2,1)} async-done(((bf16[512,256]{1,0:T(8,128)(2,1)}), bf16[16384,256]{1,0:T(8,128)(2,1)}) %all-gather.3.cloned.1.call-update) | async-done | bytes 8388624 | tf_op jit(solution)/shard_map/all_gather | solution.py:208
  149.3 6.5 %shrink.1 = bf16[32,2,4,512]{3,2,1,0:T(4,128)(2,1)} custom-call(s32[4]{0:T(128)} %dynamic_slice.9.tile_seg, bf16[32,512,256]{2,1,0:T(8,128)(2,1)} %bitcast.32, bf16[64,8192]{1,0:T(8,128)(2,1)} %pad_maximum_fusion.1.columns), custom_call_target="tpu_custom_call" | custom-call | tf_op jit(solution)/shard_map/shrink/pallas_call | solution.py:60
  155.9 7.0 %all-to-all-start.2 = ((bf16[32,2,4,512]{3,2,1,0:T(4,128)(2,1)}), bf16[32,2,4,512]{3,2,1,0:T(4,128)(2,1)S(1)}, u32[]{:S(2)}, u32[]{:S(2)}) async-start(bf16[32,2,4,512]{3,2,1,0:T(4,128)(2,1)} %shrink.1), calls=%async_computation.2 | async-start | bytes 524288 | tf_op jit(solution)/shard_map/all_to_all | solution.py:175
  162.8 15.1 %frozen.1 = f32[2,512,512]{2,1,0:T(8,128)} custom-call(bf16[32,512,256]{2,1,0:T(8,128)(2,1)} %bitcast.33, bf16[8192,512]{1,0:T(8,128)(2,1)} %bitcast.35, bf16[8192,512]{1,0:T(8,128)(2,1)} %collective-permute-done.2.other), custom_call_target="tpu_custom_call" | custom-call | tf_op jit(solution)/shard_map/frozen/pallas_call | solution.py:101
  178.0 0.8 reshape.83.shrunk
  178.8 4.0 %adapt.1 = (bf16[512,256]{1,0:T(8,128)(2,1)}, bf16[512,256]{1,0:T(8,128)(2,1)}) custom-call(s32[4]{0:T(128)} %dynamic_slice.9.tile_seg, f32[2,512,512]{2,1,0:T(8,128)} %frozen.1, bf16[256,512]{1,0:T(8,128)(2,1)} %reshape.83.shrunk, bf16[4,3,128,128]{3,2,1,0:T(8,128)(2,1)} %slice.24.own, bf16[4,3,128,128]{3,2,1,0:T(8,128)(2,1)} %slice.25.other), custom_call_target="tpu_custom_call" | custom-call | tf_op jit(solution)/shard_map/adapt/pallas_call | solution.py:153
  182.8 0.7 collective-permute-start.3
  183.6 1.0 constant_dynamic-update-slice_fusion.1
  184.9 0.4 copy-done.2
  185.4 0.7 constant_dynamic-update-slice_fusion
  (29 shorter events, 1.7 us)
Async XLA Ops:
  6.5 116.6 %copy-start = (s32[64]{0:T(128)S(1)}, s32[64]{0:T(128)}, u32[]{:S(2)}) copy-start(s32[64]{0:T(128)} %param.13) | copy-start | bytes 772
  6.5 142.8 %all-gather.3.cloned.1.call-start = ((), (), s32[]{:S(2)}) async-start(), calls=%async_computation.3 | async-start | bytes 8650752 | tf_op jit(solution)/shard_map/all_gather | solution.py:208
  7.5 4.3 %collective-permute-start = (bf16[512,128]{1,0:T(8,128)(2,1)S(1)}, bf16[512,128]{1,0:T(8,128)(2,1)S(1)}, u32[]{:S(2)}, u32[]{:S(2)}) collective-permute-start(bf16[512,128]{1,0:T(8,128)(2,1)S(1)} %constant_dynamic-slice_fusion), channel_id=1, source_target_pairs={{0,2},{2,0},{1,3},{3,1},{4,6},{6,4},{5,7},{7,5},{8,10},{10,8},{9,1... | collective-permute-start | bytes 393224 | tf_op jit(solution)/shard_map/ppermute | solution.py:179
  15.0 1.6 copy-start.1
  18.6 101.3 %all-to-all-start = ((bf16[64,192,128]{2,1,0:T(8,128)(2,1)}), bf16[64,192,128]{2,1,0:T(8,128)(2,1)S(1)}, u32[]{:S(2)}, u32[]{:S(2)}) async-start(bf16[64,192,128]{2,1,0:T(8,128)(2,1)} %pad_maximum_fusion), calls=%async_computation | async-start | bytes 6291456 | tf_op jit(solution)/shard_map/all_to_all | solution.py:175
  42.9 80.1 %copy-start.3 = (s32[4,3]{1,0:T(4,128)S(1)}, s32[4,3]{1,0:T(4,128)}, u32[]{:S(2)}) copy-start(s32[4,3]{1,0:T(4,128)} %param.11) | copy-start | bytes 148
  42.9 97.5 %copy-start.4 = (s32[1,3]{1,0:T(1,128)S(1)}, s32[1,3]{1,0:T(1,128)}, u32[]{:S(2)}) copy-start(s32[1,3]{1,0:T(1,128)} %param.12) | copy-start | bytes 40
  119.9 24.8 %collective-permute-start.2 = (bf16[8192,512]{1,0:T(8,128)(2,1)}, bf16[8192,512]{1,0:T(8,128)(2,1)}, u32[]{:S(2)}, u32[]{:S(2)}) collective-permute-start(bf16[8192,512]{1,0:T(8,128)(2,1)} %bitcast.34), channel_id=1, source_target_pairs={{0,2},{2,0},{1,3},{3,1},{4,6},{6,4},{5,7},{7,5},{8,10},{10,8},{9,1... | collective-permute-start | bytes 25165832 | tf_op jit(solution)/shard_map/ppermute | solution.py:179
  139.0 3.0 %collective-permute-start.1 = (bf16[4,3,192,128]{3,2,1,0:T(8,128)(2,1)S(1)}, bf16[4,3,192,128]{3,2,1,0:T(8,128)(2,1)S(1)}, u32[]{:S(2)}, u32[]{:S(2)}) collective-permute-start(bf16[4,3,192,128]{3,2,1,0:T(8,128)(2,1)S(1)} %bitcast.39), channel_id=1, source_target_pairs={{0,2},{2,0},{1,3},{3,1},{4,6},{6,4},{5,7},{7,5},{8,10},{10,8},{9,1... | collective-permute-start | bytes 1769480 | tf_op jit(solution)/shard_map/ppermute | solution.py:179
  155.9 22.0 %all-to-all-start.2 = ((bf16[32,2,4,512]{3,2,1,0:T(4,128)(2,1)}), bf16[32,2,4,512]{3,2,1,0:T(4,128)(2,1)S(1)}, u32[]{:S(2)}, u32[]{:S(2)}) async-start(bf16[32,2,4,512]{3,2,1,0:T(4,128)(2,1)} %shrink.1), calls=%async_computation.2 | async-start | bytes 524288 | tf_op jit(solution)/shard_map/all_to_all | solution.py:175
  182.8 2.1 %collective-permute-start.3 = (bf16[512,256]{1,0:T(8,128)(2,1)}, bf16[512,256]{1,0:T(8,128)(2,1)S(1)}, u32[]{:S(2)}, u32[]{:S(2)}) collective-permute-start(bf16[512,256]{1,0:T(8,128)(2,1)} %get-tuple-element.24), channel_id=1, source_target_pairs={{0,2},{2,0},{1,3},{3,1},{4,6},{6,4},{5,7},{7,5},{8,10},{10,8},{9,1... | collective-permute-start | bytes 786440 | tf_op jit(solution)/shard_map/ppermute | solution.py:179
  184.6 0.8 copy-start.2
Sparse Core Ops, SparseCore 0:
  13.6 135.6 all-gather.2

commit v9 on v8

--- a/solution.py
+++ b/solution.py
@@ -115,7 +115,7 @@
     )(tokens, own, other)
 
 
-def adapt_kernel(tile_seg, frozen, shrunk, own, other, own_out, other_out):
+def adapt_kernel(tile_seg, place, frozen, shrunk, own, other, own_out, other_out):
     parts, _, rank, _ = own.shape
     hidden = own_out.shape[1]
     tiles = own_out.shape[0] // TILE
@@ -146,29 +146,35 @@
                 out[row, at] = (gate / (1.0 + jnp.exp(-gate)) * up).astype(bf16)
 
 
-def adapt(frozen, shrunk, own, other, tile_seg):
+def adapt(frozen, shrunk, own, other, tile_seg, core):
     both, count, wide = frozen.shape
     rows = count // HALVES
-    whole = pl.BlockSpec(own.shape, lambda i, seg: (0, 0, 0, 0))
+    whole = pl.BlockSpec(own.shape, lambda i, seg, at: (0, 0, 0, 0))
     return pl.pallas_call(
         adapt_kernel,
-        out_shape=[jax.ShapeDtypeStruct((count, wide // 2), bf16)] * both,
+        out_shape=[
+            jax.ShapeDtypeStruct((CORES * count, wide // 2), bf16),
+            jax.ShapeDtypeStruct((count, wide // 2), bf16),
+        ],
         grid_spec=pltpu.PrefetchScalarGridSpec(
-            num_scalar_prefetch=1,
+            num_scalar_prefetch=2,
             grid=(HALVES,),
             in_specs=[
-                pl.BlockSpec((both, rows, wide), lambda i, seg: (0, i, 0)),
-                pl.BlockSpec((shrunk.shape[0], rows), lambda i, seg: (0, i)),
+                pl.BlockSpec((both, rows, wide), lambda i, seg, at: (0, i, 0)),
+                pl.BlockSpec((shrunk.shape[0], rows), lambda i, seg, at: (0, i)),
                 whole,
                 whole,
             ],
-            out_specs=[pl.BlockSpec((rows, wide // 2), lambda i, seg: (i, 0))] * both,
+            out_specs=[
+                pl.BlockSpec((rows, wide // 2), lambda i, seg, at: (at[0] + i, 0)),
+                pl.BlockSpec((rows, wide // 2), lambda i, seg, at: (i, 0)),
+            ],
         ),
         compiler_params=pltpu.CompilerParams(
             dimension_semantics=("arbitrary",), vmem_limit_bytes=56 << 20
         ),
         name="adapt",
-    )(tile_seg, frozen, shrunk, own, other)
+    )(tile_seg, (core * HALVES).reshape(1), frozen, shrunk, own, other)
 
 
 def exchange(x, axes):
@@ -201,8 +207,10 @@
 
     kept = lax.dynamic_slice_in_dim(tokens, core * rows, rows, axis=0)
     given = swap(lax.dynamic_slice_in_dim(tokens, (1 - core) * rows, rows, axis=0))
-    start = jnp.concatenate(
-        [jnp.where(first, kept, given), jnp.where(first, given, kept)], axis=1
+    start = jnp.where(
+        first,
+        jnp.concatenate([kept, given], axis=1),
+        jnp.concatenate([given, kept], axis=1),
     )
     down_pool, start = lax.optimization_barrier((down_factor_pool[0], start))
     gathered = lax.all_gather(start, ("yhi", "ylo", "z"))
@@ -246,10 +254,7 @@
     shrunk = shrunk.reshape(twice_rank, rows)
 
     frozen = frozen_matmul(gathered, own_weight, other_weight)
-    own_rows, for_other = adapt(frozen, shrunk, own_factors, other_factors, tile_seg)
-
-    hidden = jnp.zeros((token_count, wide // 2), bf16)
-    hidden = lax.dynamic_update_slice_in_dim(hidden, own_rows, core * rows, axis=0)
+    hidden, for_other = adapt(frozen, shrunk, own_factors, other_factors, tile_seg, core)
     return lax.dynamic_update_slice_in_dim(hidden, swap(for_other), (1 - core) * rows, axis=0)
 
 

time: 194 us -> 192 us (0.990)
  transfers between devices with their start and end apart: 7 -> 7, of which waited for: 4 -> 4; matrix products, arithmetic and copies ran while one was open for 18% -> 17% of each run, Pallas kernels for 8% -> 8%
where the time goes in v9:
time: 192 us
  waiting for transfers between devices  76.3 us (40%)
  local copies, waits for them, and re-layouts  32.5 us (17%)
  starting transfers between devices  25.9 us (13%)
  Pallas kernels  25.6 us (13%)
  blocking collectives  13.7 us (7%)
  between operations  13.5 us (7%)
  other arithmetic  4.16 us (2%)
    all_to_all x2, waiting for transfers between devices, exchange(): return lax.all_to_all(x, axes, split_axis=0, concat_axis=0, tiled=True)  69.2 us
    reshape x2, local copies, waits for them, and re-layouts, per_device(): w = gate_up_weight.reshape(YL * ZN * CORES, YH, share, wide)  21.8 us
    all_to_all x2, starting transfers between devices, exchange(): return lax.all_to_all(x, axes, split_axis=0, concat_axis=0, tiled=True)  17.2 us
    pallas_call x1, Pallas kernels, frozen_matmul(): pl.pallas_call(frozen_kernel, out_shape=jax.ShapeDtypeStruct(shape, f32),...  15.1 us
    all_to_all x1, blocking collectives, exchange(): return lax.all_to_all(x, axes, split_axis=0, concat_axis=0, tiled=True)  13.7 us
    ppermute x4, starting transfers between devices, swap(): return lax.ppermute(x, 'core', [(0, 1), (1, 0)])  8.64 us
    pallas_call x1, Pallas kernels, shrink(): pl.pallas_call(shrink_kernel, out_shape=jax.ShapeDtypeStruct((chips, CORE...  6.53 us
    all_gather x1, waiting for transfers between devices, per_device(): gathered = lax.all_gather(start, ('yhi', 'ylo', 'z'))  4.7 us
  transfers between devices with their start and end apart: 7, of which 4 were waited for; matrix products, arithmetic and copies ran while one was open for 17% of the time, Pallas kernels for 8%

profile of v9, /device:TPU:1, one launch (start us, length us, event | category | flops | bytes accessed | tf_op | source)
XLA Modules:
  0.0 191.7 jit_solution(10362508918383696005)
XLA Ops:
  6.5 1.0 constant_dynamic-slice_fusion.1
  7.5 3.3 %collective-permute-start = (bf16[512,128]{1,0:T(8,128)(2,1)S(1)}, bf16[512,128]{1,0:T(8,128)(2,1)S(1)}, u32[]{:S(2)}, u32[]{:S(2)}) collective-permute-start(bf16[512,128]{1,0:T(8,128)(2,1)S(1)} %get-tuple-element.28), channel_id=1, source_target_pairs={{0,2},{2,0},{1,3},{3,1},{4,6},{6,4},{5,7},{7,5},{8,10},{10,8},{9,1... | collective-permute-start | bytes 393224 | tf_op jit(solution)/shard_map/ppermute | solution.py:185
  10.9 1.0 collective-permute-done
  11.9 0.8 maximum_select_fusion
  12.7 1.5 copy.23
  14.2 0.2 copy.30
  14.4 0.7 copy.24
  15.1 0.7 copy.25
  15.8 1.9 pad_maximum_fusion
  17.7 10.3 %all-to-all-start = ((bf16[64,192,128]{2,1,0:T(8,128)(2,1)}), bf16[64,192,128]{2,1,0:T(8,128)(2,1)S(1)}, u32[]{:S(2)}, u32[]{:S(2)}) async-start(bf16[64,192,128]{2,1,0:T(8,128)(2,1)} %pad_maximum_fusion), calls=%async_computation | async-start | bytes 6291456 | tf_op jit(solution)/shard_map/all_to_all | solution.py:181
  28.0 14.1 %reshape.77 = bf16[32,2,128,512]{3,2,1,0:T(8,128)(2,1)} reshape(bf16[8192,2,256]{2,1,0:T(2,128)(2,1)} %param.8) | data formatting | bytes 16777216 | tf_op jit(solution)/shard_map/reshape | solution.py:226
  42.1 7.7 %copy.26 = bf16[32,2,128,512]{3,2,0,1:T(8,128)(2,1)} copy(bf16[32,2,128,512]{3,2,1,0:T(8,128)(2,1)} %reshape.77) | data formatting | bytes 16777216 | tf_op jit(solution)/shard_map/reshape | solution.py:226
  49.8 69.2 %all-to-all-done = bf16[64,192,128]{2,1,0:T(8,128)(2,1)S(1)} async-done(((bf16[64,192,128]{2,1,0:T(8,128)(2,1)}), bf16[64,192,128]{2,1,0:T(8,128)(2,1)S(1)}, u32[]{:S(2)}, u32[]{:S(2)}) %all-to-all-start) | async-done | bytes 3145760 | tf_op jit(solution)/shard_map/all_to_all | solution.py:181
  119.0 3.2 %collective-permute-start.2 = (bf16[8192,512]{1,0:T(8,128)(2,1)}, bf16[8192,512]{1,0:T(8,128)(2,1)}, u32[]{:S(2)}, u32[]{:S(2)}) collective-permute-start(bf16[8192,512]{1,0:T(8,128)(2,1)} %bitcast.35), channel_id=1, source_target_pairs={{0,2},{2,0},{1,3},{3,1},{4,6},{6,4},{5,7},{7,5},{8,10},{10,8},{9,1... | collective-permute-start | bytes 25165832 | tf_op jit(solution)/shard_map/ppermute | solution.py:185
  122.3 0.7 gather_fusion
  123.0 1.5 gather_fusion.1
  124.5 13.7 %all_to_all.15 = bf16[12,192,128]{2,1,0:T(8,128)(2,1)S(1)} all-to-all(bf16[12,192,128]{2,1,0:T(8,128)(2,1)} %gather_fusion.1), channel_id=1, replica_groups=mesh['grp'=4,'ylo'=2,'z'=8,'core'=2,'yhi'=2] {'grp'}, dimensions={0} | all-to-all | bytes 1179648 | tf_op jit(solution)/shard_map/all_to_all | solution.py:181
  138.2 1.4 collective-permute-start.1
  139.6 0.2 reduce-window.8
  139.8 0.6 dynamic_slice.9.tile_seg
  140.4 0.8 slice.24.own
  141.7 0.8 slice.25.other
  142.7 1.1 pad_maximum_fusion.1.columns
  143.8 4.7 %all-gather.3.cloned.1.call-done = bf16[16384,256]{1,0:T(8,128)(2,1)} async-done(((bf16[512,256]{1,0:T(8,128)(2,1)}), bf16[16384,256]{1,0:T(8,128)(2,1)}) %all-gather.3.cloned.1.call-update) | async-done | bytes 8388624 | tf_op jit(solution)/shard_map/all_gather | solution.py:216
  148.5 6.5 %shrink.1 = bf16[32,2,4,512]{3,2,1,0:T(4,128)(2,1)} custom-call(s32[4]{0:T(128)} %dynamic_slice.9.tile_seg, bf16[32,512,256]{2,1,0:T(8,128)(2,1)} %bitcast.33, bf16[64,8192]{1,0:T(8,128)(2,1)} %pad_maximum_fusion.1.columns), custom_call_target="tpu_custom_call" | custom-call | tf_op jit(solution)/shard_map/shrink/pallas_call | solution.py:60
  155.1 7.0 %all-to-all-start.2 = ((bf16[32,2,4,512]{3,2,1,0:T(4,128)(2,1)}), bf16[32,2,4,512]{3,2,1,0:T(4,128)(2,1)S(1)}, u32[]{:S(2)}, u32[]{:S(2)}) async-start(bf16[32,2,4,512]{3,2,1,0:T(4,128)(2,1)} %shrink.1), calls=%async_computation.2 | async-start | bytes 524288 | tf_op jit(solution)/shard_map/all_to_all | solution.py:181
  162.0 15.1 %frozen.1 = f32[2,512,512]{2,1,0:T(8,128)} custom-call(bf16[32,512,256]{2,1,0:T(8,128)(2,1)} %bitcast.34, bf16[8192,512]{1,0:T(8,128)(2,1)} %bitcast.36, bf16[8192,512]{1,0:T(8,128)(2,1)} %collective-permute-done.2.other), custom_call_target="tpu_custom_call" | custom-call | tf_op jit(solution)/shard_map/frozen/pallas_call | solution.py:101
  177.2 0.8 reshape.87.shrunk
  178.0 4.0 %adapt.1 = (bf16[1024,256]{1,0:T(8,128)(2,1)}, bf16[512,256]{1,0:T(8,128)(2,1)}) custom-call(s32[4]{0:T(128)} %dynamic_slice.9.tile_seg, s32[1]{0:T(128)} %bitcast.2.place, f32[2,512,512]{2,1,0:T(8,128)} %frozen.1, bf16[256,512]{1,0:T(8,128)(2,1)} %reshape.87.shrunk, bf16[4,3,128,128]{3,2,1,0:T(8,128)(2,1)} %slice.24.own, bf16[4,3,128,128]{3,2,1,0:T(8,128)(2,1)} %slice.25.other), custom_call_target="tpu_custom_call" | custom-call | tf_op jit(solution)/shard_map/adapt/pallas_call | solution.py:153
  182.0 0.7 collective-permute-start.3
  182.7 1.4 collective-permute-done.3
  184.1 0.7 constant_dynamic-update-slice_fusion
  (24 shorter events, 0.9 us)
Async XLA Ops:
  6.5 115.8 %copy-start = (s32[64]{0:T(128)S(1)}, s32[64]{0:T(128)}, u32[]{:S(2)}) copy-start(s32[64]{0:T(128)} %param.13) | copy-start | bytes 772
  6.5 142.0 %all-gather.3.cloned.1.call-start = ((), (), s32[]{:S(2)}) async-start(), calls=%async_computation.3 | async-start | bytes 8650752 | tf_op jit(solution)/shard_map/all_gather | solution.py:216
  7.5 4.3 %collective-permute-start = (bf16[512,128]{1,0:T(8,128)(2,1)S(1)}, bf16[512,128]{1,0:T(8,128)(2,1)S(1)}, u32[]{:S(2)}, u32[]{:S(2)}) collective-permute-start(bf16[512,128]{1,0:T(8,128)(2,1)S(1)} %get-tuple-element.28), channel_id=1, source_target_pairs={{0,2},{2,0},{1,3},{3,1},{4,6},{6,4},{5,7},{7,5},{8,10},{10,8},{9,1... | collective-permute-start | bytes 393224 | tf_op jit(solution)/shard_map/ppermute | solution.py:185
  14.2 1.6 copy-start.1
  17.7 101.3 %all-to-all-start = ((bf16[64,192,128]{2,1,0:T(8,128)(2,1)}), bf16[64,192,128]{2,1,0:T(8,128)(2,1)S(1)}, u32[]{:S(2)}, u32[]{:S(2)}) async-start(bf16[64,192,128]{2,1,0:T(8,128)(2,1)} %pad_maximum_fusion), calls=%async_computation | async-start | bytes 6291456 | tf_op jit(solution)/shard_map/all_to_all | solution.py:181
  42.1 80.1 %copy-start.2 = (s32[4,3]{1,0:T(4,128)S(1)}, s32[4,3]{1,0:T(4,128)}, u32[]{:S(2)}) copy-start(s32[4,3]{1,0:T(4,128)} %param.11) | copy-start | bytes 148
  42.1 97.5 %copy-start.3 = (s32[1,3]{1,0:T(1,128)S(1)}, s32[1,3]{1,0:T(1,128)}, u32[]{:S(2)}) copy-start(s32[1,3]{1,0:T(1,128)} %param.12) | copy-start | bytes 40
  119.0 24.8 %collective-permute-start.2 = (bf16[8192,512]{1,0:T(8,128)(2,1)}, bf16[8192,512]{1,0:T(8,128)(2,1)}, u32[]{:S(2)}, u32[]{:S(2)}) collective-permute-start(bf16[8192,512]{1,0:T(8,128)(2,1)} %bitcast.35), channel_id=1, source_target_pairs={{0,2},{2,0},{1,3},{3,1},{4,6},{6,4},{5,7},{7,5},{8,10},{10,8},{9,1... | collective-permute-start | bytes 25165832 | tf_op jit(solution)/shard_map/ppermute | solution.py:185
  138.2 3.0 %collective-permute-start.1 = (bf16[4,3,192,128]{3,2,1,0:T(8,128)(2,1)S(1)}, bf16[4,3,192,128]{3,2,1,0:T(8,128)(2,1)S(1)}, u32[]{:S(2)}, u32[]{:S(2)}) collective-permute-start(bf16[4,3,192,128]{3,2,1,0:T(8,128)(2,1)S(1)} %bitcast.40), channel_id=1, source_target_pairs={{0,2},{2,0},{1,3},{3,1},{4,6},{6,4},{5,7},{7,5},{8,10},{10,8},{9,1... | collective-permute-start | bytes 1769480 | tf_op jit(solution)/shard_map/ppermute | solution.py:185
  155.1 22.0 %all-to-all-start.2 = ((bf16[32,2,4,512]{3,2,1,0:T(4,128)(2,1)}), bf16[32,2,4,512]{3,2,1,0:T(4,128)(2,1)S(1)}, u32[]{:S(2)}, u32[]{:S(2)}) async-start(bf16[32,2,4,512]{3,2,1,0:T(4,128)(2,1)} %shrink.1), calls=%async_computation.2 | async-start | bytes 524288 | tf_op jit(solution)/shard_map/all_to_all | solution.py:181
  182.0 2.1 %collective-permute-start.3 = (bf16[512,256]{1,0:T(8,128)(2,1)}, bf16[512,256]{1,0:T(8,128)(2,1)S(1)}, u32[]{:S(2)}, u32[]{:S(2)}) collective-permute-start(bf16[512,256]{1,0:T(8,128)(2,1)} %get-tuple-element.24), channel_id=1, source_target_pairs={{0,2},{2,0},{1,3},{3,1},{4,6},{6,4},{5,7},{7,5},{8,10},{10,8},{9,1... | collective-permute-start | bytes 786440 | tf_op jit(solution)/shard_map/ppermute | solution.py:185
Sparse Core Ops, SparseCore 0:
  12.8 135.6 all-gather.2

commit v10 on v9

--- a/solution.py
+++ b/solution.py
@@ -18,7 +18,8 @@
 adapter_scale = 0.5
 
 SLOT = 8
-STEPS = 4
+TURNS = 8
+DEEP = 4
 HALVES = 2
 
 
@@ -77,37 +78,55 @@
     )(tile_seg, tokens, columns)
 
 
-def frozen_kernel(tokens, own, other, out):
-    step = pl.program_id(0)
-    block = jnp.concatenate([tokens[i] for i in range(tokens.shape[0])], axis=1)
-    for which, weight in enumerate((own, other)):
-        part = jnp.dot(block, weight[...], preferred_element_type=f32)
-
-        @pl.when(step == 0)
-        def _():
-            out[which] = part
-
-        @pl.when(step > 0)
-        def _():
-            out[which] += part
+def frozen_kernel(tokens, own, other, out, block, weights, sems):
+    turns = tokens.shape[0] // block.shape[1]
+    deep, chips, count, both = block.shape
+    part = chips * both
+
+    def copies(k):
+        slot = k % deep
+        pairs = [(tokens.at[pl.ds(k * chips, chips)], block.at[slot])]
+        for which, weight in enumerate((own, other)):
+            pairs.append((weight.at[pl.ds(k * part, part)], weights.at[slot, which]))
+        return [
+            pltpu.make_async_copy(a, b, sems.at[slot, j]) for j, (a, b) in enumerate(pairs)
+        ]
+
+    for k in range(deep):
+        for copy in copies(k):
+            copy.start()
+    for k in range(turns):
+        for copy in copies(k):
+            copy.wait()
+        slot = k % deep
+        wide = jnp.concatenate([block[slot, i] for i in range(chips)], axis=1)
+        for which in range(CORES):
+            more = jnp.dot(wide, weights[slot, which], preferred_element_type=f32)
+            if k == 0:
+                out[which] = more
+            else:
+                out[which] += more
+        if k + deep < turns:
+            for copy in copies(k + deep):
+                copy.start()
 
 
 def frozen_matmul(tokens, own, other):
     chips, count, both = tokens.shape
     width, wide = own.shape
-    part = width // STEPS
+    at_once = chips // TURNS
     shape = (CORES, count, wide)
-    weight = pl.BlockSpec((part, wide), lambda k: (k, 0))
     return pl.pallas_call(
         frozen_kernel,
         out_shape=jax.ShapeDtypeStruct(shape, f32),
-        grid=(STEPS,),
-        in_specs=[
-            pl.BlockSpec((chips // STEPS, count, both), lambda k: (k, 0, 0)),
-            weight,
-            weight,
+        grid=(1,),
+        in_specs=[pl.BlockSpec(memory_space=pl.ANY)] * 3,
+        out_specs=pl.BlockSpec(shape, lambda k: (0, 0, 0)),
+        scratch_shapes=[
+            pltpu.VMEM((DEEP, at_once, count, both), bf16),
+            pltpu.VMEM((DEEP, CORES, at_once * both, wide), bf16),
+            pltpu.SemaphoreType.DMA((DEEP, 1 + CORES)),
         ],
-        out_specs=pl.BlockSpec(shape, lambda k: (0, 0, 0)),
         compiler_params=pltpu.CompilerParams(
             dimension_semantics=("arbitrary",), vmem_limit_bytes=56 << 20
         ),

time: 192 us -> 190 us (0.990)
  Pallas kernels: 25.6 us -> 23.1 us
    pallas_call x1, Pallas kernels: 15.1 us -> 12.5 us  [frozen_matmul(): pl.pallas_call(frozen_kernel, out_shape=jax.ShapeDtypeStruct(shape, f32),...]
  transfers between devices with their start and end apart: 7 -> 7, of which waited for: 4 -> 4; matrix products, arithmetic and copies ran while one was open for 17% -> 18% of each run, Pallas kernels for 8% -> 7%
where the time goes in v10:
time: 190 us
  waiting for transfers between devices  76.3 us (40%)
  local copies, waits for them, and re-layouts  32.5 us (17%)
  starting transfers between devices  26.3 us (14%)
  Pallas kernels  23.1 us (12%)
  blocking collectives  13.7 us (7%)
  between operations  13.5 us (7%)
  other arithmetic  4.16 us (2%)
    all_to_all x2, waiting for transfers between devices, exchange(): return lax.all_to_all(x, axes, split_axis=0, concat_axis=0, tiled=True)  69.2 us
    reshape x2, local copies, waits for them, and re-layouts, per_device(): w = gate_up_weight.reshape(YL * ZN * CORES, YH, share, wide)  21.8 us
    all_to_all x2, starting transfers between devices, exchange(): return lax.all_to_all(x, axes, split_axis=0, concat_axis=0, tiled=True)  17.4 us
    all_to_all x1, blocking collectives, exchange(): return lax.all_to_all(x, axes, split_axis=0, concat_axis=0, tiled=True)  13.7 us
    pallas_call x1, Pallas kernels, frozen_matmul(): pl.pallas_call(frozen_kernel, out_shape=jax.ShapeDtypeStruct(shape, f32),...  12.5 us
    ppermute x4, starting transfers between devices, swap(): return lax.ppermute(x, 'core', [(0, 1), (1, 0)])  8.89 us
    pallas_call x1, Pallas kernels, shrink(): pl.pallas_call(shrink_kernel, out_shape=jax.ShapeDtypeStruct((chips, CORE...  6.54 us
    all_gather x1, waiting for transfers between devices, per_device(): gathered = lax.all_gather(start, ('yhi', 'ylo', 'z'))  4.7 us
  transfers between devices with their start and end apart: 7, of which 4 were waited for; matrix products, arithmetic and copies ran while one was open for 18% of the time, Pallas kernels for 7%

profile of v10, /device:TPU:1, one launch (start us, length us, event | category | flops | bytes accessed | tf_op | source)
XLA Modules:
  0.0 189.6 jit_solution(7715381538952993127)
XLA Ops:
  6.5 1.0 constant_dynamic-slice_fusion.1
  7.5 3.3 %collective-permute-start = (bf16[512,128]{1,0:T(8,128)(2,1)S(1)}, bf16[512,128]{1,0:T(8,128)(2,1)S(1)}, u32[]{:S(2)}, u32[]{:S(2)}) collective-permute-start(bf16[512,128]{1,0:T(8,128)(2,1)S(1)} %get-tuple-element.28), channel_id=1, source_target_pairs={{0,2},{2,0},{1,3},{3,1},{4,6},{6,4},{5,7},{7,5},{8,10},{10,8},{9,1... | collective-permute-start | bytes 393224 | tf_op jit(solution)/shard_map/ppermute | solution.py:204
  10.9 1.0 collective-permute-done
  11.9 0.8 maximum_select_fusion
  12.7 1.5 copy.23
  14.2 0.2 copy.30
  14.4 0.7 copy.24
  15.1 0.7 copy.25
  15.8 1.9 %pad_maximum_fusion = bf16[64,192,128]{2,1,0:T(8,128)(2,1)} fusion(bf16[64,64,128]{2,1,0:T(8,128)(2,1)S(1)} %copy.25, bf16[64,128,128]{2,1,0:T(8,128)(2,1)S(1)} %bitcast.43), kind=kLoop, calls=%fused_computation.2 | loop fusion | flops 6291456 | bytes 6291456 | tf_op jit(solution)/shard_map/concatenate | solution.py:242
  17.7 10.3 %all-to-all-start = ((bf16[64,192,128]{2,1,0:T(8,128)(2,1)}), bf16[64,192,128]{2,1,0:T(8,128)(2,1)S(1)}, u32[]{:S(2)}, u32[]{:S(2)}) async-start(bf16[64,192,128]{2,1,0:T(8,128)(2,1)} %pad_maximum_fusion), calls=%async_computation | async-start | bytes 6291456 | tf_op jit(solution)/shard_map/all_to_all | solution.py:200
  28.0 14.1 %reshape.77 = bf16[32,2,128,512]{3,2,1,0:T(8,128)(2,1)} reshape(bf16[8192,2,256]{2,1,0:T(2,128)(2,1)} %param.8) | data formatting | bytes 16777216 | tf_op jit(solution)/shard_map/reshape | solution.py:245
  42.1 7.7 %copy.26 = bf16[32,2,128,512]{3,2,0,1:T(8,128)(2,1)} copy(bf16[32,2,128,512]{3,2,1,0:T(8,128)(2,1)} %reshape.77) | data formatting | bytes 16777216 | tf_op jit(solution)/shard_map/reshape | solution.py:245
  49.8 69.2 %all-to-all-done = bf16[64,192,128]{2,1,0:T(8,128)(2,1)S(1)} async-done(((bf16[64,192,128]{2,1,0:T(8,128)(2,1)}), bf16[64,192,128]{2,1,0:T(8,128)(2,1)S(1)}, u32[]{:S(2)}, u32[]{:S(2)}) %all-to-all-start) | async-done | bytes 3145760 | tf_op jit(solution)/shard_map/all_to_all | solution.py:200
  119.0 3.2 %collective-permute-start.2 = (bf16[8192,512]{1,0:T(8,128)(2,1)}, bf16[8192,512]{1,0:T(8,128)(2,1)}, u32[]{:S(2)}, u32[]{:S(2)}) collective-permute-start(bf16[8192,512]{1,0:T(8,128)(2,1)} %bitcast.35), channel_id=1, source_target_pairs={{0,2},{2,0},{1,3},{3,1},{4,6},{6,4},{5,7},{7,5},{8,10},{10,8},{9,1... | collective-permute-start | bytes 25165832 | tf_op jit(solution)/shard_map/ppermute | solution.py:204
  122.3 0.7 gather_fusion
  123.0 1.5 gather_fusion.1
  124.5 13.7 %all_to_all.15 = bf16[12,192,128]{2,1,0:T(8,128)(2,1)S(1)} all-to-all(bf16[12,192,128]{2,1,0:T(8,128)(2,1)} %gather_fusion.1), channel_id=1, replica_groups=mesh['grp'=4,'ylo'=2,'z'=8,'core'=2,'yhi'=2] {'grp'}, dimensions={0} | all-to-all | bytes 1179648 | tf_op jit(solution)/shard_map/all_to_all | solution.py:200
  138.2 1.4 collective-permute-start.1
  139.6 0.2 reduce-window.8
  139.8 0.6 dynamic_slice.9.tile_seg
  140.4 0.8 slice.24.own
  141.7 0.8 slice.25.other
  142.7 1.1 pad_maximum_fusion.1.columns
  143.8 4.7 %all-gather.3.cloned.1.call-done = bf16[16384,256]{1,0:T(8,128)(2,1)} async-done(((bf16[512,256]{1,0:T(8,128)(2,1)}), bf16[16384,256]{1,0:T(8,128)(2,1)}) %all-gather.3.cloned.1.call-update) | async-done | bytes 8388624 | tf_op jit(solution)/shard_map/all_gather | solution.py:235
  148.5 6.5 %shrink.1 = bf16[32,2,4,512]{3,2,1,0:T(4,128)(2,1)} custom-call(s32[4]{0:T(128)} %dynamic_slice.9.tile_seg, bf16[32,512,256]{2,1,0:T(8,128)(2,1)} %bitcast.33, bf16[64,8192]{1,0:T(8,128)(2,1)} %pad_maximum_fusion.1.columns), custom_call_target="tpu_custom_call" | custom-call | tf_op jit(solution)/shard_map/shrink/pallas_call | solution.py:61
  155.1 7.1 %all-to-all-start.2 = ((bf16[32,2,4,512]{3,2,1,0:T(4,128)(2,1)}), bf16[32,2,4,512]{3,2,1,0:T(4,128)(2,1)S(1)}, u32[]{:S(2)}, u32[]{:S(2)}) async-start(bf16[32,2,4,512]{3,2,1,0:T(4,128)(2,1)} %shrink.1), calls=%async_computation.2 | async-start | bytes 524288 | tf_op jit(solution)/shard_map/all_to_all | solution.py:200
  162.2 12.5 %frozen.1 = f32[2,512,512]{2,1,0:T(8,128)} custom-call(bf16[32,512,256]{2,1,0:T(8,128)(2,1)} %bitcast.34, bf16[8192,512]{1,0:T(8,128)(2,1)} %bitcast.36, bf16[8192,512]{1,0:T(8,128)(2,1)} %collective-permute-done.2.other), custom_call_target="tpu_custom_call" | custom-call | tf_op jit(solution)/shard_map/frozen/pallas_call | solution.py:119
  174.9 0.8 reshape.87.shrunk
  175.6 4.0 %adapt.1 = (bf16[1024,256]{1,0:T(8,128)(2,1)}, bf16[512,256]{1,0:T(8,128)(2,1)}) custom-call(s32[4]{0:T(128)} %dynamic_slice.9.tile_seg, s32[1]{0:T(128)} %bitcast.2.place, f32[2,512,512]{2,1,0:T(8,128)} %frozen.1, bf16[256,512]{1,0:T(8,128)(2,1)} %reshape.87.shrunk, bf16[4,3,128,128]{3,2,1,0:T(8,128)(2,1)} %slice.24.own, bf16[4,3,128,128]{3,2,1,0:T(8,128)(2,1)} %slice.25.other), custom_call_target="tpu_custom_call" | custom-call | tf_op jit(solution)/shard_map/adapt/pallas_call | solution.py:172
  179.6 1.0 collective-permute-start.3
  180.6 1.4 collective-permute-done.3
  182.0 0.7 constant_dynamic-update-slice_fusion
  (24 shorter events, 0.9 us)
Async XLA Ops:
  6.5 115.8 %copy-start = (s32[64]{0:T(128)S(1)}, s32[64]{0:T(128)}, u32[]{:S(2)}) copy-start(s32[64]{0:T(128)} %param.13) | copy-start | bytes 772
  6.5 142.0 %all-gather.3.cloned.1.call-start = ((), (), s32[]{:S(2)}) async-start(), calls=%async_computation.3 | async-start | bytes 8650752 | tf_op jit(solution)/shard_map/all_gather | solution.py:235
  7.5 4.3 %collective-permute-start = (bf16[512,128]{1,0:T(8,128)(2,1)S(1)}, bf16[512,128]{1,0:T(8,128)(2,1)S(1)}, u32[]{:S(2)}, u32[]{:S(2)}) collective-permute-start(bf16[512,128]{1,0:T(8,128)(2,1)S(1)} %get-tuple-element.28), channel_id=1, source_target_pairs={{0,2},{2,0},{1,3},{3,1},{4,6},{6,4},{5,7},{7,5},{8,10},{10,8},{9,1... | collective-permute-start | bytes 393224 | tf_op jit(solution)/shard_map/ppermute | solution.py:204
  14.2 1.6 copy-start.1
  17.7 101.3 %all-to-all-start = ((bf16[64,192,128]{2,1,0:T(8,128)(2,1)}), bf16[64,192,128]{2,1,0:T(8,128)(2,1)S(1)}, u32[]{:S(2)}, u32[]{:S(2)}) async-start(bf16[64,192,128]{2,1,0:T(8,128)(2,1)} %pad_maximum_fusion), calls=%async_computation | async-start | bytes 6291456 | tf_op jit(solution)/shard_map/all_to_all | solution.py:200
  42.1 80.1 %copy-start.2 = (s32[4,3]{1,0:T(4,128)S(1)}, s32[4,3]{1,0:T(4,128)}, u32[]{:S(2)}) copy-start(s32[4,3]{1,0:T(4,128)} %param.11) | copy-start | bytes 148
  42.1 97.5 %copy-start.3 = (s32[1,3]{1,0:T(1,128)S(1)}, s32[1,3]{1,0:T(1,128)}, u32[]{:S(2)}) copy-start(s32[1,3]{1,0:T(1,128)} %param.12) | copy-start | bytes 40
  119.0 24.8 %collective-permute-start.2 = (bf16[8192,512]{1,0:T(8,128)(2,1)}, bf16[8192,512]{1,0:T(8,128)(2,1)}, u32[]{:S(2)}, u32[]{:S(2)}) collective-permute-start(bf16[8192,512]{1,0:T(8,128)(2,1)} %bitcast.35), channel_id=1, source_target_pairs={{0,2},{2,0},{1,3},{3,1},{4,6},{6,4},{5,7},{7,5},{8,10},{10,8},{9,1... | collective-permute-start | bytes 25165832 | tf_op jit(solution)/shard_map/ppermute | solution.py:204
  138.2 3.0 %collective-permute-start.1 = (bf16[4,3,192,128]{3,2,1,0:T(8,128)(2,1)S(1)}, bf16[4,3,192,128]{3,2,1,0:T(8,128)(2,1)S(1)}, u32[]{:S(2)}, u32[]{:S(2)}) collective-permute-start(bf16[4,3,192,128]{3,2,1,0:T(8,128)(2,1)S(1)} %bitcast.40), channel_id=1, source_target_pairs={{0,2},{2,0},{1,3},{3,1},{4,6},{6,4},{5,7},{7,5},{8,10},{10,8},{9,1... | collective-permute-start | bytes 1769480 | tf_op jit(solution)/shard_map/ppermute | solution.py:204
  155.1 19.7 %all-to-all-start.2 = ((bf16[32,2,4,512]{3,2,1,0:T(4,128)(2,1)}), bf16[32,2,4,512]{3,2,1,0:T(4,128)(2,1)S(1)}, u32[]{:S(2)}, u32[]{:S(2)}) async-start(bf16[32,2,4,512]{3,2,1,0:T(4,128)(2,1)} %shrink.1), calls=%async_computation.2 | async-start | bytes 524288 | tf_op jit(solution)/shard_map/all_to_all | solution.py:200
  179.6 2.4 %collective-permute-start.3 = (bf16[512,256]{1,0:T(8,128)(2,1)}, bf16[512,256]{1,0:T(8,128)(2,1)S(1)}, u32[]{:S(2)}, u32[]{:S(2)}) collective-permute-start(bf16[512,256]{1,0:T(8,128)(2,1)} %get-tuple-element.24), channel_id=1, source_target_pairs={{0,2},{2,0},{1,3},{3,1},{4,6},{6,4},{5,7},{7,5},{8,10},{10,8},{9,1... | collective-permute-start | bytes 786440 | tf_op jit(solution)/shard_map/ppermute | solution.py:204
Sparse Core Ops, SparseCore 0:
  12.8 135.6 all-gather.2
